TPU v7x, 512 devices: a whole 4x4x16 slice. The times are simulated.
512 devices in a mesh: grp: 16 (over z), sub: 32 (over x, y, core).
Axes of the slice: x: 4, y: 4, z: 16, core: 2. Of those that a mesh axis runs over, the one named last changes fastest.
Arguments:
- top_basis: bfloat16 [16, 512, 256], P('grp', 'sub'), may hold values from -0.375 to 0.375
- top_coeffs: bfloat16 [16, 256, 128], P('grp'), may hold values from -6 to 6
- top_coupling: float32 [16, 512, 512], P('grp')
- block_coupling: float32 [16, 32, 128, 512], P('grp', 'sub'), may hold values from -0.09375 to 0.09375
- block_basis: bfloat16 [16, 32, 128, 128], P('grp', 'sub'), may hold values from -0.5 to 0.5
- block_coeffs: bfloat16 [16, 32, 128, 128], P('grp', 'sub'), may hold values from -6 to 6
- sub_basis: bfloat16 [16, 32, 1536, 256], P('grp', 'sub'), may hold values from -0.375 to 0.375
- sub_coeffs: bfloat16 [16, 32, 256, 128], P('grp', 'sub'), may hold values from -6 to 6
- basis_widths: int32 [16, 32], P('grp', 'sub'), may hold values from 32 to 256
- constraint_modes: bfloat16 [16, 32, 1536, 512], P('grp', 'sub'), may hold values from -0.25 to 0.25
- adjacency: int32 [16, 32, 4], P('grp', 'sub'), may hold values from 0 to 4, as said below
Outputs:
- top_values: float32 [16, 512, 128], P('grp')
- block_values: bfloat16 [16, 32, 128, 128], P('grp', 'sub')
- interior: bfloat16 [16, 32, 1536, 128], P('grp', 'sub')
Inputs may be any that keep to these rules, and one draw needn't show every extreme that they name: `adjacency`: the 4 entries of one substructure are different.
All inputs are finite; a program needn't handle non-finite values.
Results may differ from a plain program's by a relative error of at most 0.0044.
Values may be sent and summed in bfloat16 or wider, within the bound.
No kernel may reach another device: no remote copies, remote signals or barrier semaphores. Data moves between devices by JAX's collectives and lax.ppermute only.
A program may use at most 64 MiB of HBM per device.

v0:
```python
import jax
import jax.numpy as jnp
from jax import lax
from jax.sharding import PartitionSpec as P


def from_behind(shard, axis, by):
    peers = lax.axis_size(axis)
    return lax.ppermute(shard, axis, [(i, (i + by) % peers) for i in range(peers)])


def from_behind_2(value, axis, steps):
    count = lax.axis_size(axis)
    first, last = (max(0, -steps), min(count, count - steps))
    return lax.ppermute(value, axis, [(source, source + steps) for source in range(first, last)])


def neighbour_block(block, offset):
    return from_behind(block, "sub", -offset)


def run_chain(top_own, chain_matrix):
    highest = lax.Precision.HIGHEST

    def relay(turn_index, current):
        earlier = from_behind_2(current, "grp", 1)
        return top_own + jnp.dot(chain_matrix, earlier, precision=highest)

    return lax.fori_loop(0, lax.axis_size("grp"), relay, jnp.zeros_like(top_own))


def body(
    top_basis,
    top_coeffs,
    top_coupling,
    block_coupling,
    block_basis,
    block_coeffs,
    sub_basis,
    sub_coeffs,
    basis_widths,
    constraint_modes,
    adjacency,
):
    highest = lax.Precision.HIGHEST
    rows_own = jnp.dot(top_basis[0], top_coeffs[0], preferred_element_type=jnp.float32)
    chain_matrix = top_coupling[0]
    top_own = lax.all_gather(rows_own, "sub", axis=0, tiled=True)
    top_field = run_chain(top_own, chain_matrix)
    own_block = jnp.dot(block_basis[0, 0], block_coeffs[0, 0], preferred_element_type=jnp.float32)
    from_top = jnp.dot(block_coupling[0, 0], top_field, precision=highest)
    block = (own_block + from_top).astype(jnp.bfloat16)
    records = [block, block, block, block, block]
    for offset in (-2, -1, 1, 2):
        records[offset + 2] = neighbour_block(block, offset)
    candidates = jnp.stack(records)
    slots = adjacency[0, 0]
    chosen = jnp.take(candidates, slots, axis=0)
    linked = chosen.reshape(slots.shape[0] * block.shape[0], block.shape[1])
    bound_part = jnp.dot(constraint_modes[0, 0], linked, preferred_element_type=jnp.float32)
    kept_width = basis_widths[0, 0]
    coeffs = sub_coeffs[0, 0]
    basis = sub_basis[0, 0]
    width_total = coeffs.shape[0]
    live_mask = lax.broadcasted_iota(jnp.int32, (width_total, 1), 0) < kept_width
    live_coeffs = jnp.where(live_mask, coeffs, jnp.zeros_like(coeffs))
    fixed_part = jnp.dot(basis, live_coeffs, preferred_element_type=jnp.float32)
    interior = (fixed_part + bound_part).astype(jnp.bfloat16)
    return (top_field[None], block[None, None], interior[None, None])


def solution(mesh):
    placed = (
        P("grp", "sub", None),
        P("grp", None, None),
        P("grp", None, None),
        P("grp", "sub", None, None),
        P("grp", "sub", None, None),
        P("grp", "sub", None, None),
        P("grp", "sub", None, None),
        P("grp", "sub", None, None),
        P("grp", "sub"),
        P("grp", "sub", None, None),
        P("grp", "sub", None),
    )
    return jax.shard_map(
        body,
        mesh=mesh,
        in_specs=placed,
        out_specs=(P("grp", None, None), P("grp", "sub", None, None), P("grp", "sub", None, None)),
        check_vma=False,
    )
```

profile of v0, /device:TPU:384, one launch (start us, length us, event | category | flops | bytes accessed | tf_op | source)
XLA Modules:
  0.0 249.1 jit_solution(1026725116123611253)
XLA Ops:
  1.8 25.2 %all_gather.3 = f32[512,128]{1,0:T(8,128)S(1)} all-gather(f32[16,128]{1,0:T(8,128)S(1)} %fusion.8), channel_id=1, replica_groups=mesh['grp'=16,'sub'=32] {'sub'}, dimensions={0}, use_global_device_ids=true | all-gather | bytes 270336 | tf_op jit(solution)/shard_map/all_gather | solution.py:48
  26.9 199.4 %while.11 = (s32[]{:T(128)}, f32[512,128]{1,0:T(8,128)S(1)}, f32[512,512]{1,0:T(8,128)}, f32[512,128]{1,0:T(8,128)S(1)}, s32[]{:T(128)}, /*index=5*/s32[]{:T(128)}) while((s32[]{:T(128)}, f32[512,128]{1,0:T(8,128)S(1)}, f32[512,512]{1,0:T(8,128)}, f32[512,128]{1,0:T(8,128)S(1)}, s32[]{:T(128)}, /*index=5*/s32[]{:T(128)}) %tuple.30), condition=%wide.region_1.0_spmd.clone, body=%wide.region_0.0_spmd.clone.sunk | while | flops 402784256 | bytes 3407991 | solution.py:29
  27.0 3.1 %collective-permute-start = (f32[512,128]{1,0:T(8,128)S(1)}, f32[512,128]{1,0:T(8,128)S(1)}, u32[]{:S(2)}, u32[]{:S(2)}) collective-permute-start(f32[512,128]{1,0:T(8,128)S(1)} %broadcast_select_fusion.3), channel_id=1, source_target_pairs={{0,32},{32,64},{64,96},{96,128},{128,160},{160,192},{192,224},{224... | collective-permute-start | bytes 786440 | tf_op jit(solution)/shard_map/while/body/eval_jaxpr/ppermute | solution.py:15
  30.0 8.8 %collective-permute-done = f32[512,128]{1,0:T(8,128)S(1)} collective-permute-done((f32[512,128]{1,0:T(8,128)S(1)}, f32[512,128]{1,0:T(8,128)S(1)}, u32[]{:S(2)}, u32[]{:S(2)}) %collective-permute-start) | collective-permute-done | bytes 262176 | tf_op jit(solution)/shard_map/while/body/eval_jaxpr/ppermute | solution.py:15
  38.8 2.2 convolution_add_fusion.4
  41.0 1.9 collective-permute-start
  43.0 8.9 %collective-permute-done = f32[512,128]{1,0:T(8,128)S(1)} collective-permute-done((f32[512,128]{1,0:T(8,128)S(1)}, f32[512,128]{1,0:T(8,128)S(1)}, u32[]{:S(2)}, u32[]{:S(2)}) %collective-permute-start) | collective-permute-done | bytes 262176 | tf_op jit(solution)/shard_map/while/body/eval_jaxpr/ppermute | solution.py:15
  51.9 2.2 convolution_add_fusion.4
  54.1 1.9 collective-permute-start
  56.1 8.0 %collective-permute-done = f32[512,128]{1,0:T(8,128)S(1)} collective-permute-done((f32[512,128]{1,0:T(8,128)S(1)}, f32[512,128]{1,0:T(8,128)S(1)}, u32[]{:S(2)}, u32[]{:S(2)}) %collective-permute-start) | collective-permute-done | bytes 262176 | tf_op jit(solution)/shard_map/while/body/eval_jaxpr/ppermute | solution.py:15
  64.1 2.2 convolution_add_fusion.4
  66.4 1.9 collective-permute-start
  68.3 7.5 %collective-permute-done = f32[512,128]{1,0:T(8,128)S(1)} collective-permute-done((f32[512,128]{1,0:T(8,128)S(1)}, f32[512,128]{1,0:T(8,128)S(1)}, u32[]{:S(2)}, u32[]{:S(2)}) %collective-permute-start) | collective-permute-done | bytes 262176 | tf_op jit(solution)/shard_map/while/body/eval_jaxpr/ppermute | solution.py:15
  75.9 2.2 convolution_add_fusion.4
  78.1 1.9 collective-permute-start
  80.0 7.5 %collective-permute-done = f32[512,128]{1,0:T(8,128)S(1)} collective-permute-done((f32[512,128]{1,0:T(8,128)S(1)}, f32[512,128]{1,0:T(8,128)S(1)}, u32[]{:S(2)}, u32[]{:S(2)}) %collective-permute-start) | collective-permute-done | bytes 262176 | tf_op jit(solution)/shard_map/while/body/eval_jaxpr/ppermute | solution.py:15
  87.6 2.2 convolution_add_fusion.4
  89.9 1.9 collective-permute-start
  91.8 7.5 %collective-permute-done = f32[512,128]{1,0:T(8,128)S(1)} collective-permute-done((f32[512,128]{1,0:T(8,128)S(1)}, f32[512,128]{1,0:T(8,128)S(1)}, u32[]{:S(2)}, u32[]{:S(2)}) %collective-permute-start) | collective-permute-done | bytes 262176 | tf_op jit(solution)/shard_map/while/body/eval_jaxpr/ppermute | solution.py:15
  99.3 2.2 convolution_add_fusion.4
  101.6 1.9 collective-permute-start
  103.5 7.5 %collective-permute-done = f32[512,128]{1,0:T(8,128)S(1)} collective-permute-done((f32[512,128]{1,0:T(8,128)S(1)}, f32[512,128]{1,0:T(8,128)S(1)}, u32[]{:S(2)}, u32[]{:S(2)}) %collective-permute-start) | collective-permute-done | bytes 262176 | tf_op jit(solution)/shard_map/while/body/eval_jaxpr/ppermute | solution.py:15
  111.1 2.2 convolution_add_fusion.4
  113.3 1.9 collective-permute-start
  115.3 7.6 %collective-permute-done = f32[512,128]{1,0:T(8,128)S(1)} collective-permute-done((f32[512,128]{1,0:T(8,128)S(1)}, f32[512,128]{1,0:T(8,128)S(1)}, u32[]{:S(2)}, u32[]{:S(2)}) %collective-permute-start) | collective-permute-done | bytes 262176 | tf_op jit(solution)/shard_map/while/body/eval_jaxpr/ppermute | solution.py:15
  122.8 2.2 convolution_add_fusion.4
  125.1 1.9 collective-permute-start
  127.0 8.7 %collective-permute-done = f32[512,128]{1,0:T(8,128)S(1)} collective-permute-done((f32[512,128]{1,0:T(8,128)S(1)}, f32[512,128]{1,0:T(8,128)S(1)}, u32[]{:S(2)}, u32[]{:S(2)}) %collective-permute-start) | collective-permute-done | bytes 262176 | tf_op jit(solution)/shard_map/while/body/eval_jaxpr/ppermute | solution.py:15
  135.7 2.2 convolution_add_fusion.4
  139.9 9.9 %collective-permute-done = f32[512,128]{1,0:T(8,128)S(1)} collective-permute-done((f32[512,128]{1,0:T(8,128)S(1)}, f32[512,128]{1,0:T(8,128)S(1)}, u32[]{:S(2)}, u32[]{:S(2)}) %collective-permute-start) | collective-permute-done | bytes 262176 | tf_op jit(solution)/shard_map/while/body/eval_jaxpr/ppermute | solution.py:15
  149.7 2.2 convolution_add_fusion.4
  153.9 9.7 %collective-permute-done = f32[512,128]{1,0:T(8,128)S(1)} collective-permute-done((f32[512,128]{1,0:T(8,128)S(1)}, f32[512,128]{1,0:T(8,128)S(1)}, u32[]{:S(2)}, u32[]{:S(2)}) %collective-permute-start) | collective-permute-done | bytes 262176 | tf_op jit(solution)/shard_map/while/body/eval_jaxpr/ppermute | solution.py:15
  163.6 2.2 convolution_add_fusion.4
  167.8 8.9 %collective-permute-done = f32[512,128]{1,0:T(8,128)S(1)} collective-permute-done((f32[512,128]{1,0:T(8,128)S(1)}, f32[512,128]{1,0:T(8,128)S(1)}, u32[]{:S(2)}, u32[]{:S(2)}) %collective-permute-start) | collective-permute-done | bytes 262176 | tf_op jit(solution)/shard_map/while/body/eval_jaxpr/ppermute | solution.py:15
  176.7 2.2 convolution_add_fusion.4
  180.9 8.0 %collective-permute-done = f32[512,128]{1,0:T(8,128)S(1)} collective-permute-done((f32[512,128]{1,0:T(8,128)S(1)}, f32[512,128]{1,0:T(8,128)S(1)}, u32[]{:S(2)}, u32[]{:S(2)}) %collective-permute-start) | collective-permute-done | bytes 262176 | tf_op jit(solution)/shard_map/while/body/eval_jaxpr/ppermute | solution.py:15
  188.9 2.2 convolution_add_fusion.4
  191.1 1.9 collective-permute-start
  193.1 7.5 %collective-permute-done = f32[512,128]{1,0:T(8,128)S(1)} collective-permute-done((f32[512,128]{1,0:T(8,128)S(1)}, f32[512,128]{1,0:T(8,128)S(1)}, u32[]{:S(2)}, u32[]{:S(2)}) %collective-permute-start) | collective-permute-done | bytes 262176 | tf_op jit(solution)/shard_map/while/body/eval_jaxpr/ppermute | solution.py:15
  200.6 2.2 convolution_add_fusion.4
  204.8 7.5 %collective-permute-done = f32[512,128]{1,0:T(8,128)S(1)} collective-permute-done((f32[512,128]{1,0:T(8,128)S(1)}, f32[512,128]{1,0:T(8,128)S(1)}, u32[]{:S(2)}, u32[]{:S(2)}) %collective-permute-start) | collective-permute-done | bytes 262176 | tf_op jit(solution)/shard_map/while/body/eval_jaxpr/ppermute | solution.py:15
  212.4 2.2 convolution_add_fusion.4
  216.5 7.5 %collective-permute-done = f32[512,128]{1,0:T(8,128)S(1)} collective-permute-done((f32[512,128]{1,0:T(8,128)S(1)}, f32[512,128]{1,0:T(8,128)S(1)}, u32[]{:S(2)}, u32[]{:S(2)}) %collective-permute-start) | collective-permute-done | bytes 262176 | tf_op jit(solution)/shard_map/while/body/eval_jaxpr/ppermute | solution.py:15
  224.1 2.2 convolution_add_fusion.4
  228.7 4.6 %collective-permute-start.4 = (bf16[128,128]{1,0:T(8,128)(2,1)S(1)}, bf16[128,128]{1,0:T(8,128)(2,1)S(1)}, u32[]{:S(2)}, u32[]{:S(2)}) collective-permute-start(bf16[128,128]{1,0:T(8,128)(2,1)S(1)} %fusion.3), channel_id=1, source_target_pairs={{0,30},{1,31},{2,0},{3,1},{4,2},{5,3},{6,4},{7,5},{8,6},{9,7},{10,... | collective-permute-start | bytes 98312 | tf_op jit(solution)/shard_map/ppermute | solution.py:9
  235.2 2.4 collective-permute-start.2
  237.7 1.9 collective-permute-start.1
  240.8 6.0 %collective-permute-done.1 = bf16[128,128]{1,0:T(8,128)(2,1)S(1)} collective-permute-done((bf16[128,128]{1,0:T(8,128)(2,1)S(1)}, bf16[128,128]{1,0:T(8,128)(2,1)S(1)}, u32[]{:S(2)}, u32[]{:S(2)}) %collective-permute-start.1) | collective-permute-done | bytes 32800 | tf_op jit(solution)/shard_map/ppermute | solution.py:9
  (58 shorter events, 20.0 us)
Async XLA Ops:
  0.6 246.9 %copy-start = (bf16[1,1,1536,512]{3,2,1,0:T(8,128)(2,1)S(1)}, bf16[1,1,1536,512]{3,2,1,0:T(8,128)(2,1)}, u32[]{:S(2)}) copy-start(bf16[1,1,1536,512]{3,2,1,0:T(8,128)(2,1)} %param.22) | copy-start | bytes 4718596
  26.9 200.9 %copy-start.5 = (bf16[1,1,128,128]{3,2,1,0:T(8,128)(2,1)S(1)}, bf16[1,1,128,128]{3,2,1,0:T(8,128)(2,1)}, u32[]{:S(2)}) copy-start(bf16[1,1,128,128]{3,2,1,0:T(8,128)(2,1)} %param.18) | copy-start | bytes 98308
  26.9 212.7 %copy-start.6 = (s32[1,1,4]{2,1,0:T(1,128)S(1)}, s32[1,1,4]{2,1,0:T(1,128)}, u32[]{:S(2)}) copy-start(s32[1,1,4]{2,1,0:T(1,128)} %param.23) | copy-start | bytes 52
  26.9 213.4 %copy-start.2 = (bf16[1,1,1536,256]{3,2,1,0:T(8,128)(2,1)S(1)}, bf16[1,1,1536,256]{3,2,1,0:T(8,128)(2,1)}, u32[]{:S(2)}) copy-start(bf16[1,1,1536,256]{3,2,1,0:T(8,128)(2,1)} %param.19) | copy-start | bytes 2359300
  26.9 213.4 %copy-start.4 = (bf16[1,1,256,128]{3,2,1,0:T(8,128)(2,1)S(1)}, bf16[1,1,256,128]{3,2,1,0:T(8,128)(2,1)}, u32[]{:S(2)}) copy-start(bf16[1,1,256,128]{3,2,1,0:T(8,128)(2,1)} %param.20) | copy-start | bytes 196612
  27.0 11.8 %collective-permute-start = (f32[512,128]{1,0:T(8,128)S(1)}, f32[512,128]{1,0:T(8,128)S(1)}, u32[]{:S(2)}, u32[]{:S(2)}) collective-permute-start(f32[512,128]{1,0:T(8,128)S(1)} %broadcast_select_fusion.3), channel_id=1, source_target_pairs={{0,32},{32,64},{64,96},{96,128},{128,160},{160,192},{192,224},{224... | collective-permute-start | bytes 786440 | tf_op jit(solution)/shard_map/while/body/eval_jaxpr/ppermute | solution.py:15
  41.0 10.8 %collective-permute-start = (f32[512,128]{1,0:T(8,128)S(1)}, f32[512,128]{1,0:T(8,128)S(1)}, u32[]{:S(2)}, u32[]{:S(2)}) collective-permute-start(f32[512,128]{1,0:T(8,128)S(1)} %broadcast_select_fusion.3), channel_id=1, source_target_pairs={{0,32},{32,64},{64,96},{96,128},{128,160},{160,192},{192,224},{224... | collective-permute-start | bytes 786440 | tf_op jit(solution)/shard_map/while/body/eval_jaxpr/ppermute | solution.py:15
  54.1 10.0 %collective-permute-start = (f32[512,128]{1,0:T(8,128)S(1)}, f32[512,128]{1,0:T(8,128)S(1)}, u32[]{:S(2)}, u32[]{:S(2)}) collective-permute-start(f32[512,128]{1,0:T(8,128)S(1)} %broadcast_select_fusion.3), channel_id=1, source_target_pairs={{0,32},{32,64},{64,96},{96,128},{128,160},{160,192},{192,224},{224... | collective-permute-start | bytes 786440 | tf_op jit(solution)/shard_map/while/body/eval_jaxpr/ppermute | solution.py:15
  66.4 9.5 %collective-permute-start = (f32[512,128]{1,0:T(8,128)S(1)}, f32[512,128]{1,0:T(8,128)S(1)}, u32[]{:S(2)}, u32[]{:S(2)}) collective-permute-start(f32[512,128]{1,0:T(8,128)S(1)} %broadcast_select_fusion.3), channel_id=1, source_target_pairs={{0,32},{32,64},{64,96},{96,128},{128,160},{160,192},{192,224},{224... | collective-permute-start | bytes 786440 | tf_op jit(solution)/shard_map/while/body/eval_jaxpr/ppermute | solution.py:15
  78.1 9.5 %collective-permute-start = (f32[512,128]{1,0:T(8,128)S(1)}, f32[512,128]{1,0:T(8,128)S(1)}, u32[]{:S(2)}, u32[]{:S(2)}) collective-permute-start(f32[512,128]{1,0:T(8,128)S(1)} %broadcast_select_fusion.3), channel_id=1, source_target_pairs={{0,32},{32,64},{64,96},{96,128},{128,160},{160,192},{192,224},{224... | collective-permute-start | bytes 786440 | tf_op jit(solution)/shard_map/while/body/eval_jaxpr/ppermute | solution.py:15
  89.9 9.5 %collective-permute-start = (f32[512,128]{1,0:T(8,128)S(1)}, f32[512,128]{1,0:T(8,128)S(1)}, u32[]{:S(2)}, u32[]{:S(2)}) collective-permute-start(f32[512,128]{1,0:T(8,128)S(1)} %broadcast_select_fusion.3), channel_id=1, source_target_pairs={{0,32},{32,64},{64,96},{96,128},{128,160},{160,192},{192,224},{224... | collective-permute-start | bytes 786440 | tf_op jit(solution)/shard_map/while/body/eval_jaxpr/ppermute | solution.py:15
  101.6 9.5 %collective-permute-start = (f32[512,128]{1,0:T(8,128)S(1)}, f32[512,128]{1,0:T(8,128)S(1)}, u32[]{:S(2)}, u32[]{:S(2)}) collective-permute-start(f32[512,128]{1,0:T(8,128)S(1)} %broadcast_select_fusion.3), channel_id=1, source_target_pairs={{0,32},{32,64},{64,96},{96,128},{128,160},{160,192},{192,224},{224... | collective-permute-start | bytes 786440 | tf_op jit(solution)/shard_map/while/body/eval_jaxpr/ppermute | solution.py:15
  113.3 9.5 %collective-permute-start = (f32[512,128]{1,0:T(8,128)S(1)}, f32[512,128]{1,0:T(8,128)S(1)}, u32[]{:S(2)}, u32[]{:S(2)}) collective-permute-start(f32[512,128]{1,0:T(8,128)S(1)} %broadcast_select_fusion.3), channel_id=1, source_target_pairs={{0,32},{32,64},{64,96},{96,128},{128,160},{160,192},{192,224},{224... | collective-permute-start | bytes 786440 | tf_op jit(solution)/shard_map/while/body/eval_jaxpr/ppermute | solution.py:15
  125.1 10.6 %collective-permute-start = (f32[512,128]{1,0:T(8,128)S(1)}, f32[512,128]{1,0:T(8,128)S(1)}, u32[]{:S(2)}, u32[]{:S(2)}) collective-permute-start(f32[512,128]{1,0:T(8,128)S(1)} %broadcast_select_fusion.3), channel_id=1, source_target_pairs={{0,32},{32,64},{64,96},{96,128},{128,160},{160,192},{192,224},{224... | collective-permute-start | bytes 786440 | tf_op jit(solution)/shard_map/while/body/eval_jaxpr/ppermute | solution.py:15
  138.0 11.8 %collective-permute-start = (f32[512,128]{1,0:T(8,128)S(1)}, f32[512,128]{1,0:T(8,128)S(1)}, u32[]{:S(2)}, u32[]{:S(2)}) collective-permute-start(f32[512,128]{1,0:T(8,128)S(1)} %broadcast_select_fusion.3), channel_id=1, source_target_pairs={{0,32},{32,64},{64,96},{96,128},{128,160},{160,192},{192,224},{224... | collective-permute-start | bytes 786440 | tf_op jit(solution)/shard_map/while/body/eval_jaxpr/ppermute | solution.py:15
  152.0 11.6 %collective-permute-start = (f32[512,128]{1,0:T(8,128)S(1)}, f32[512,128]{1,0:T(8,128)S(1)}, u32[]{:S(2)}, u32[]{:S(2)}) collective-permute-start(f32[512,128]{1,0:T(8,128)S(1)} %broadcast_select_fusion.3), channel_id=1, source_target_pairs={{0,32},{32,64},{64,96},{96,128},{128,160},{160,192},{192,224},{224... | collective-permute-start | bytes 786440 | tf_op jit(solution)/shard_map/while/body/eval_jaxpr/ppermute | solution.py:15
  165.9 10.8 %collective-permute-start = (f32[512,128]{1,0:T(8,128)S(1)}, f32[512,128]{1,0:T(8,128)S(1)}, u32[]{:S(2)}, u32[]{:S(2)}) collective-permute-start(f32[512,128]{1,0:T(8,128)S(1)} %broadcast_select_fusion.3), channel_id=1, source_target_pairs={{0,32},{32,64},{64,96},{96,128},{128,160},{160,192},{192,224},{224... | collective-permute-start | bytes 786440 | tf_op jit(solution)/shard_map/while/body/eval_jaxpr/ppermute | solution.py:15
  179.0 9.9 %collective-permute-start = (f32[512,128]{1,0:T(8,128)S(1)}, f32[512,128]{1,0:T(8,128)S(1)}, u32[]{:S(2)}, u32[]{:S(2)}) collective-permute-start(f32[512,128]{1,0:T(8,128)S(1)} %broadcast_select_fusion.3), channel_id=1, source_target_pairs={{0,32},{32,64},{64,96},{96,128},{128,160},{160,192},{192,224},{224... | collective-permute-start | bytes 786440 | tf_op jit(solution)/shard_map/while/body/eval_jaxpr/ppermute | solution.py:15
  191.1 9.5 %collective-permute-start = (f32[512,128]{1,0:T(8,128)S(1)}, f32[512,128]{1,0:T(8,128)S(1)}, u32[]{:S(2)}, u32[]{:S(2)}) collective-permute-start(f32[512,128]{1,0:T(8,128)S(1)} %broadcast_select_fusion.3), channel_id=1, source_target_pairs={{0,32},{32,64},{64,96},{96,128},{128,160},{160,192},{192,224},{224... | collective-permute-start | bytes 786440 | tf_op jit(solution)/shard_map/while/body/eval_jaxpr/ppermute | solution.py:15
  202.9 9.5 %collective-permute-start = (f32[512,128]{1,0:T(8,128)S(1)}, f32[512,128]{1,0:T(8,128)S(1)}, u32[]{:S(2)}, u32[]{:S(2)}) collective-permute-start(f32[512,128]{1,0:T(8,128)S(1)} %broadcast_select_fusion.3), channel_id=1, source_target_pairs={{0,32},{32,64},{64,96},{96,128},{128,160},{160,192},{192,224},{224... | collective-permute-start | bytes 786440 | tf_op jit(solution)/shard_map/while/body/eval_jaxpr/ppermute | solution.py:15
  214.6 9.5 %collective-permute-start = (f32[512,128]{1,0:T(8,128)S(1)}, f32[512,128]{1,0:T(8,128)S(1)}, u32[]{:S(2)}, u32[]{:S(2)}) collective-permute-start(f32[512,128]{1,0:T(8,128)S(1)} %broadcast_select_fusion.3), channel_id=1, source_target_pairs={{0,32},{32,64},{64,96},{96,128},{128,160},{160,192},{192,224},{224... | collective-permute-start | bytes 786440 | tf_op jit(solution)/shard_map/while/body/eval_jaxpr/ppermute | solution.py:15
  226.3 21.2 %copy-start.1 = (f32[512,128]{1,0:T(8,128)}, f32[512,128]{1,0:T(8,128)S(1)}, u32[]{:S(2)}) copy-start(f32[512,128]{1,0:T(8,128)S(1)} %get-tuple-element.25) | copy-start | bytes 786436
  228.7 19.5 %copy-start.3 = (bf16[128,128]{1,0:T(8,128)(2,1)}, bf16[128,128]{1,0:T(8,128)(2,1)S(1)}, u32[]{:S(2)}) copy-start(bf16[128,128]{1,0:T(8,128)(2,1)S(1)} %fusion.3) | copy-start | bytes 98308
  228.7 18.1 %collective-permute-start.4 = (bf16[128,128]{1,0:T(8,128)(2,1)S(1)}, bf16[128,128]{1,0:T(8,128)(2,1)S(1)}, u32[]{:S(2)}, u32[]{:S(2)}) collective-permute-start(bf16[128,128]{1,0:T(8,128)(2,1)S(1)} %fusion.3), channel_id=1, source_target_pairs={{0,30},{1,31},{2,0},{3,1},{4,2},{5,3},{6,4},{7,5},{8,6},{9,7},{10,... | collective-permute-start | bytes 98312 | tf_op jit(solution)/shard_map/ppermute | solution.py:9
  233.3 13.5 %collective-permute-start.3 = (bf16[128,128]{1,0:T(8,128)(2,1)S(1)}, bf16[128,128]{1,0:T(8,128)(2,1)S(1)}, u32[]{:S(2)}, u32[]{:S(2)}) collective-permute-start(bf16[128,128]{1,0:T(8,128)(2,1)S(1)} %fusion.3), channel_id=1, source_target_pairs={{0,31},{1,0},{2,1},{3,2},{4,3},{5,4},{6,5},{7,6},{8,7},{9,8},{10,9... | collective-permute-start | bytes 98312 | tf_op jit(solution)/shard_map/ppermute | solution.py:9
  235.2 11.5 %collective-permute-start.2 = (bf16[128,128]{1,0:T(8,128)(2,1)S(1)}, bf16[128,128]{1,0:T(8,128)(2,1)S(1)}, u32[]{:S(2)}, u32[]{:S(2)}) collective-permute-start(bf16[128,128]{1,0:T(8,128)(2,1)S(1)} %fusion.3), channel_id=1, source_target_pairs={{0,1},{1,2},{2,3},{3,4},{4,5},{5,6},{6,7},{7,8},{8,9},{9,10},{10,1... | collective-permute-start | bytes 98312 | tf_op jit(solution)/shard_map/ppermute | solution.py:9
  237.7 9.1 %collective-permute-start.1 = (bf16[128,128]{1,0:T(8,128)(2,1)S(1)}, bf16[128,128]{1,0:T(8,128)(2,1)S(1)}, u32[]{:S(2)}, u32[]{:S(2)}) collective-permute-start(bf16[128,128]{1,0:T(8,128)(2,1)S(1)} %fusion.3), channel_id=1, source_target_pairs={{0,2},{1,3},{2,4},{3,5},{4,6},{5,7},{6,8},{7,9},{8,10},{9,11},{10,... | collective-permute-start | bytes 98312 | tf_op jit(solution)/shard_map/ppermute | solution.py:9
where the time goes:
time: 251 us; the launch traced here: 249 us
  waiting for transfers between devices  137 us (55%)
  starting transfers between devices  42.7 us (17%)
  matrix products  39.9 us (16%)
  blocking collectives  25.2 us (10%)
    ppermute x16, waiting for transfers between devices, from_behind_2(): lax.ppermute(value, axis, [(source, source + steps) for source in range(f...  131 us
    dot_general x16, matrix products, relay(): return top_own + jnp.dot(chain_matrix, earlier, precision=highest)  35.4 us
    ppermute x16, starting transfers between devices, from_behind_2(): lax.ppermute(value, axis, [(source, source + steps) for source in range(f...  31.9 us
    all_gather x1, blocking collectives, body(): top_own = lax.all_gather(rows_own, 'sub', axis=0, tiled=True)  25.2 us
    ppermute x4, starting transfers between devices, from_behind(): lax.ppermute(shard, axis, [(i, (i + by) % peers) for i in range(peers)])  10.8 us
    ppermute x4, waiting for transfers between devices, from_behind(): lax.ppermute(shard, axis, [(i, (i + by) % peers) for i in range(peers)])  6 us
  transfers between devices with their start and end apart: 20, of which 17 were waited for; matrix products, arithmetic and copies ran while one was open for 0% of the time, Pallas kernels for 0%

commit v1 on v0

v1 whole, which is shorter than its diff:
```python
import jax
import jax.numpy as jnp
from jax import lax
from jax.sharding import PartitionSpec as P

BF16 = jnp.bfloat16
F32 = jnp.float32
WINDOW = 3


def split(value):
    high = lax.reduce_precision(value, 8, 7)
    return high.astype(BF16), (value - high).astype(BF16)


def spread(piece):
    peers = lax.axis_size("sub")
    copies = jnp.broadcast_to(piece[None], (peers,) + piece.shape)
    return lax.all_to_all(copies, "sub", 0, 0)


def along_chain(value, by, groups):
    peers = lax.axis_size("sub")
    pairs = [((g - by) * peers + s, g * peers + s) for g in groups if g >= by for s in range(1, peers, 2)]
    return lax.ppermute(value, ("grp", "sub"), pairs)


def along_loop(value, by):
    peers = lax.axis_size("sub")
    return lax.ppermute(value, "sub", [(i, (i + by) % peers) for i in range(peers)])


def times(left, right):
    dims = (((1,), (1,)), ((), ()))
    high, low = left
    return lax.dot_general(right, high, dims, preferred_element_type=F32) + lax.dot_general(
        right, low, dims, preferred_element_type=F32
    )


def rows_times(value, left):
    dims = (((1,), (1,)), ((), ()))
    return lax.dot_general(value, left, dims, precision=lax.Precision.HIGH, preferred_element_type=F32)


def body(
    top_basis,
    top_coeffs,
    top_coupling,
    block_coupling,
    block_basis,
    block_coeffs,
    sub_basis,
    sub_coeffs,
    basis_widths,
    constraint_modes,
    adjacency,
):
    chain = lax.axis_size("grp")
    place = lax.axis_index("sub")
    coupling = top_coupling[0]
    high, low = split(coupling)

    back_1 = along_chain(high, 1, range(2, chain))
    back_2 = along_chain(high, 2, range(3, chain))
    basis = spread(top_basis[0]).reshape(-1, top_basis.shape[-1])

    columns = top_coeffs.shape[-1] * 2 // lax.axis_size("sub")
    coeffs = lax.dynamic_slice_in_dim(top_coeffs[0].T, (place // 2) * columns, columns, 0)
    own = lax.dot_general(coeffs, basis, (((1,), (1,)), ((), ())), preferred_element_type=F32)

    two = jnp.dot(high, back_1, preferred_element_type=F32) + jnp.dot(low, back_1, preferred_element_type=F32)
    two_high, two_low = split(two)
    three = jnp.dot(two_high, back_2, preferred_element_type=F32) + jnp.dot(two_low, back_2, preferred_element_type=F32)

    own_1 = along_chain(own, 1, range(1, chain))
    own_2 = along_chain(own, 2, range(2, chain))
    field = own + rows_times(own_1, coupling) + rows_times(own_2, two)
    for first in range(WINDOW, chain, WINDOW):
        earlier = along_chain(field, WINDOW, range(first, min(first + WINDOW, chain)))
        field = field + rows_times(earlier, three)

    pieces = spread(field.astype(BF16))
    whole = pieces.reshape(-1, 2, columns, pieces.shape[-1])[:, 1].reshape(-1, pieces.shape[-1])
    top_field = whole.astype(F32).T

    own_block = jnp.dot(block_basis[0, 0], block_coeffs[0, 0], preferred_element_type=F32)
    nt = (((1,), (1,)), ((), ()))
    from_top = lax.dot_general(block_coupling[0, 0].astype(BF16), whole, nt, preferred_element_type=F32)
    block = (own_block + from_top).astype(BF16)
    records = [along_loop(block, -offset) if offset else block for offset in (-2, -1, 0, 1, 2)]
    candidates = jnp.stack(records)
    slots = adjacency[0, 0]
    chosen = jnp.take(candidates, slots, axis=0)
    linked = chosen.reshape(slots.shape[0] * block.shape[0], block.shape[1])
    bound_part = jnp.dot(constraint_modes[0, 0], linked, preferred_element_type=F32)
    coeffs = sub_coeffs[0, 0]
    live_mask = lax.broadcasted_iota(jnp.int32, (coeffs.shape[0], 1), 0) < basis_widths[0, 0]
    live_coeffs = jnp.where(live_mask, coeffs, jnp.zeros_like(coeffs))
    fixed_part = jnp.dot(sub_basis[0, 0], live_coeffs, preferred_element_type=F32)
    interior = (fixed_part + bound_part).astype(BF16)
    return (top_field[None], block[None, None], interior[None, None])


def solution(mesh):
    placed = (
        P("grp", "sub", None),
        P("grp", None, None),
        P("grp", None, None),
        P("grp", "sub", None, None),
        P("grp", "sub", None, None),
        P("grp", "sub", None, None),
        P("grp", "sub", None, None),
        P("grp", "sub", None, None),
        P("grp", "sub"),
        P("grp", "sub", None, None),
        P("grp", "sub", None),
    )
    return jax.shard_map(
        body,
        mesh=mesh,
        in_specs=placed,
        out_specs=(P("grp", None, None), P("grp", "sub", None, None), P("grp", "sub", None, None)),
        check_vma=False,
    )
```

time: 251 us -> 98.7 us (0.39)
  the two profiles are of different devices: /device:TPU:384 before, /device:TPU:480 now
where the time goes in v1:
time: 98.7 us; the launch traced here: 98 us
  starting transfers between devices  64.8 us (66%)
  waiting for transfers between devices  14.3 us (14%)
  matrix products  10.3 us (10%)
  local copies, waits for them, and re-layouts  4.74 us (5%)
  other arithmetic  2.22 us (2%)
  between operations  1.72 us (2%)
    all_to_all x2, starting transfers between devices, spread(): return lax.all_to_all(copies, 'sub', 0, 0)  43.1 us
    ppermute x4, starting transfers between devices, along_loop(): lax.ppermute(value, 'sub', [(i, (i + by) % peers) for i in range(peers)])  14.7 us
    all_to_all x2, waiting for transfers between devices, spread(): return lax.all_to_all(copies, 'sub', 0, 0)  13.1 us
    ppermute x9, starting transfers between devices, along_chain(): return lax.ppermute(value, ('grp', 'sub'), pairs)  6.93 us
    dot_general x7, matrix products, rows_times(): lax.dot_general(value, left, dims, precision=lax.Precision.HIGH, preferre...  3.61 us
    broadcast_in_dim x2, local copies, waits for them, and re-layouts, spread(): copies = jnp.broadcast_to(piece[None], (peers,) + piece.shape)  2.31 us
    convert_element_type x1, other arithmetic, split(): return (high.astype(BF16), (value - high).astype(BF16))  2.1 us
  transfers between devices with their start and end apart: 15, of which 3 were waited for; matrix products, arithmetic and copies ran while one was open for 9% of the time, Pallas kernels for 0%

profile of v1, /device:TPU:480, one launch (start us, length us, event | category | flops | bytes accessed | tf_op | source)
XLA Modules:
  0.0 98.0 jit_solution(550960114264948436)
XLA Ops:
  0.6 0.0 copy-start
  0.6 0.0 copy-start.1
  0.7 1.6 %broadcast_in_dim.47 = bf16[32,16,256]{2,1,0:T(8,128)(2,1)} broadcast(bf16[16,256]{1,0:T(8,128)(2,1)} %bitcast.94), dimensions={1,2} | broadcast | bytes 270336 | tf_op jit(solution)/shard_map/broadcast_in_dim | solution.py:18
  2.3 7.3 %all-to-all-start = ((bf16[32,16,256]{2,1,0:T(8,128)(2,1)}), bf16[32,16,256]{2,1,0:T(8,128)(2,1)S(1)}, u32[]{:S(2)}, u32[]{:S(2)}) async-start(bf16[32,16,256]{2,1,0:T(8,128)(2,1)} %broadcast_in_dim.47), calls=%async_computation | async-start | bytes 524288 | tf_op jit(solution)/shard_map/all_to_all | solution.py:19
  9.6 2.1 %reduce-precision_convert_fusion.1 = bf16[512,512]{1,0:T(8,128)(2,1)} fusion(f32[1,512,512]{2,1,0:T(8,128)} %param.13), kind=kLoop, calls=%fused_computation.8 | loop fusion | flops 524288 | bytes 1572864 | tf_op jit(solution)/shard_map/convert_element_type | solution.py:13
  11.7 1.5 %collective-permute-start.2 = (bf16[512,512]{1,0:T(8,128)(2,1)}, bf16[512,512]{1,0:T(8,128)(2,1)}, u32[]{:S(2)}, u32[]{:S(2)}) collective-permute-start(bf16[512,512]{1,0:T(8,128)(2,1)} %reduce-precision_convert_fusion.1), channel_id=1, source_target_pairs={{33,65},{35,67},{37,69},{39,71},{41,73},{43,75},{45,77},{47,79},{4... | collective-permute-start | bytes 1572872 | tf_op jit(solution)/shard_map/ppermute | solution.py:25
  13.1 0.7 collective-permute-start.4
  13.8 4.7 %all-to-all-done = bf16[32,16,256]{2,1,0:T(8,128)(2,1)S(1)} async-done(((bf16[32,16,256]{2,1,0:T(8,128)(2,1)}), bf16[32,16,256]{2,1,0:T(8,128)(2,1)S(1)}, u32[]{:S(2)}, u32[]{:S(2)}) %all-to-all-start) | async-done | bytes 262176 | tf_op jit(solution)/shard_map/all_to_all | solution.py:19
  18.5 0.2 fusion.18
  18.7 0.7 collective-permute-start
  19.4 0.1 fusion.23
  19.6 0.7 collective-permute-start.1
  20.2 0.0 collective-permute-done
  20.3 0.5 convolution_add_fusion.9
  20.8 1.5 %fusion.13 = f32[512,512]{1,0:T(8,128)S(1)} fusion(bf16[512,512]{1,0:T(8,128)(2,1)} %collective-permute-done.2, f32[1,512,512]{2,1,0:T(8,128)S(1)} %copy-done.1), kind=kOutput, calls=%fused_computation.28 | convolution fusion | flops 269221888 | bytes 2621440 | tf_op jit(solution)/shard_map/dot_general | solution.py:72
  22.3 1.6 %convolution_add_fusion.2 = f32[512,512]{1,0:T(8,128)S(1)} fusion(f32[512,512]{1,0:T(8,128)S(1)} %fusion.13, bf16[512,512]{1,0:T(8,128)(2,1)} %reduce-precision_convert_fusion.1, bf16[512,512]{1,0:T(8,128)(2,1)} %collective-permute-done.2), kind=kOutput, calls=%fused_computation.10 | convolution fusion | flops 268697600 | bytes 3145728 | tf_op jit(solution)/shard_map/dot_general | solution.py:72
  23.9 0.0 collective-permute-done.1
  23.9 0.5 convolution_add_fusion.8
  24.4 0.7 collective-permute-start.3
  25.1 0.4 fusion.11
  25.6 0.0 copy-start.8
  25.6 0.4 convolution_add_fusion.1
  26.0 0.5 convolution_add_fusion.7
  26.6 0.7 collective-permute-start.5
  27.3 0.5 convolution_add_fusion.6
  27.8 0.7 collective-permute-start.6
  28.5 0.5 convolution_add_fusion.5
  29.0 0.0 copy-start.4
  29.0 0.8 collective-permute-start.7
  30.5 0.5 convolution_add_fusion.4
  31.0 0.7 collective-permute-start.8
  31.7 0.5 fusion.5
  32.2 0.7 broadcast_in_dim.48
  33.0 35.8 %all-to-all-start.1 = ((bf16[32,8,512]{2,1,0:T(8,128)(2,1)}), bf16[32,8,512]{2,1,0:T(8,128)(2,1)S(1)}, u32[]{:S(2)}, u32[]{:S(2)}) async-start(bf16[32,8,512]{2,1,0:T(8,128)(2,1)} %broadcast_in_dim.48), calls=%async_computation.1 | async-start | bytes 524288 | tf_op jit(solution)/shard_map/all_to_all | solution.py:19
  68.8 0.5 fusion.9
  69.3 8.4 %all-to-all-done.1 = bf16[32,8,512]{2,1,0:T(8,128)(2,1)S(1)} async-done(((bf16[32,8,512]{2,1,0:T(8,128)(2,1)}), bf16[32,8,512]{2,1,0:T(8,128)(2,1)S(1)}, u32[]{:S(2)}, u32[]{:S(2)}) %all-to-all-start.1) | async-done | bytes 262176 | tf_op jit(solution)/shard_map/all_to_all | solution.py:19
  77.7 1.1 %fusion.4 = bf16[128,128]{1,0:T(8,128)(2,1)S(1)} fusion(f32[128,128]{1,0:T(8,128)S(1)} %fusion.23, f32[1,1,128,512]{3,2,1,0:T(8,128)} %param.14, bf16[16,2,8,512]{3,2,1,0:T(8,128)(2,1)S(1)} %bitcast.90), kind=kOutput, calls=%fused_computation.13 | convolution fusion | flops 16875520 | bytes 491520 | tf_op jit(solution)/shard_map/dot_general | solution.py:89
  78.9 0.0 copy-start.3
  78.9 2.2 %collective-permute-start.9 = (bf16[128,128]{1,0:T(8,128)(2,1)S(1)}, bf16[128,128]{1,0:T(8,128)(2,1)S(1)}, u32[]{:S(2)}, u32[]{:S(2)}) collective-permute-start(bf16[128,128]{1,0:T(8,128)(2,1)S(1)} %fusion.4), channel_id=1, source_target_pairs={{0,2},{1,3},{2,4},{3,5},{4,6},{5,7},{6,8},{7,9},{8,10},{9,11},{10,... | collective-permute-start | bytes 98312 | tf_op jit(solution)/shard_map/ppermute | solution.py:30
  81.0 2.2 %collective-permute-start.10 = (bf16[128,128]{1,0:T(8,128)(2,1)S(1)}, bf16[128,128]{1,0:T(8,128)(2,1)S(1)}, u32[]{:S(2)}, u32[]{:S(2)}) collective-permute-start(bf16[128,128]{1,0:T(8,128)(2,1)S(1)} %fusion.4), channel_id=1, source_target_pairs={{0,1},{1,2},{2,3},{3,4},{4,5},{5,6},{6,7},{7,8},{8,9},{9,10},{10,1... | collective-permute-start | bytes 98312 | tf_op jit(solution)/shard_map/ppermute | solution.py:30
  83.2 6.7 %collective-permute-start.11 = (bf16[128,128]{1,0:T(8,128)(2,1)S(1)}, bf16[128,128]{1,0:T(8,128)(2,1)S(1)}, u32[]{:S(2)}, u32[]{:S(2)}) collective-permute-start(bf16[128,128]{1,0:T(8,128)(2,1)S(1)} %fusion.4), channel_id=1, source_target_pairs={{0,31},{1,0},{2,1},{3,2},{4,3},{5,4},{6,5},{7,6},{8,7},{9,8},{10,9... | collective-permute-start | bytes 98312 | tf_op jit(solution)/shard_map/ppermute | solution.py:30
  89.9 3.7 %collective-permute-start.12 = (bf16[128,128]{1,0:T(8,128)(2,1)S(1)}, bf16[128,128]{1,0:T(8,128)(2,1)S(1)}, u32[]{:S(2)}, u32[]{:S(2)}) collective-permute-start(bf16[128,128]{1,0:T(8,128)(2,1)S(1)} %fusion.4), channel_id=1, source_target_pairs={{0,30},{1,31},{2,0},{3,1},{4,2},{5,3},{6,4},{7,5},{8,6},{9,7},{10,... | collective-permute-start | bytes 98312 | tf_op jit(solution)/shard_map/ppermute | solution.py:30
  93.7 0.8 copy.17
  94.6 1.2 %collective-permute-done.12 = bf16[128,128]{1,0:T(8,128)(2,1)S(1)} collective-permute-done((bf16[128,128]{1,0:T(8,128)(2,1)S(1)}, bf16[128,128]{1,0:T(8,128)(2,1)S(1)}, u32[]{:S(2)}, u32[]{:S(2)}) %collective-permute-start.12) | collective-permute-done | bytes 32800 | tf_op jit(solution)/shard_map/ppermute | solution.py:30
  95.7 0.6 gather_fusion
  96.3 0.1 broadcast_select_fusion
  96.4 0.7 fusion.1
  97.1 0.9 copy.18
  (33 shorter events, 0.1 us)
Async XLA Ops:
  0.6 95.8 %copy-start = (bf16[1,1,1536,512]{3,2,1,0:T(8,128)(2,1)S(1)}, bf16[1,1,1536,512]{3,2,1,0:T(8,128)(2,1)}, u32[]{:S(2)}) copy-start(bf16[1,1,1536,512]{3,2,1,0:T(8,128)(2,1)} %param.20) | copy-start | bytes 4718596
  0.6 19.6 %copy-start.1 = (f32[1,512,512]{2,1,0:T(8,128)S(1)}, f32[1,512,512]{2,1,0:T(8,128)}, u32[]{:S(2)}) copy-start(f32[1,512,512]{2,1,0:T(8,128)} %param.13) | copy-start | bytes 3145732
  0.7 17.8 %copy-start.5 = (bf16[1,256,128]{2,1,0:T(8,128)(2,1)S(1)}, bf16[1,256,128]{2,1,0:T(8,128)(2,1)}, u32[]{:S(2)}) copy-start(bf16[1,256,128]{2,1,0:T(8,128)(2,1)} %param.12) | copy-start | bytes 196612
  0.7 18.8 %copy-start.7 = (bf16[1,1,128,128]{3,2,1,0:T(8,128)(2,1)S(1)}, bf16[1,1,128,128]{3,2,1,0:T(8,128)(2,1)}, u32[]{:S(2)}) copy-start(bf16[1,1,128,128]{3,2,1,0:T(8,128)(2,1)} %param.15) | copy-start | bytes 98308
  0.7 18.8 %copy-start.6 = (bf16[1,1,128,128]{3,2,1,0:T(8,128)(2,1)S(1)}, bf16[1,1,128,128]{3,2,1,0:T(8,128)(2,1)}, u32[]{:S(2)}) copy-start(bf16[1,1,128,128]{3,2,1,0:T(8,128)(2,1)} %param.16) | copy-start | bytes 98308
  2.3 16.2 %all-to-all-start = ((bf16[32,16,256]{2,1,0:T(8,128)(2,1)}), bf16[32,16,256]{2,1,0:T(8,128)(2,1)S(1)}, u32[]{:S(2)}, u32[]{:S(2)}) async-start(bf16[32,16,256]{2,1,0:T(8,128)(2,1)} %broadcast_in_dim.47), calls=%async_computation | async-start | bytes 524288 | tf_op jit(solution)/shard_map/all_to_all | solution.py:19
  11.7 9.1 %collective-permute-start.2 = (bf16[512,512]{1,0:T(8,128)(2,1)}, bf16[512,512]{1,0:T(8,128)(2,1)}, u32[]{:S(2)}, u32[]{:S(2)}) collective-permute-start(bf16[512,512]{1,0:T(8,128)(2,1)} %reduce-precision_convert_fusion.1), channel_id=1, source_target_pairs={{33,65},{35,67},{37,69},{39,71},{41,73},{43,75},{45,77},{47,79},{4... | collective-permute-start | bytes 1572872 | tf_op jit(solution)/shard_map/ppermute | solution.py:25
  13.1 12.0 %collective-permute-start.4 = (bf16[512,512]{1,0:T(8,128)(2,1)}, bf16[512,512]{1,0:T(8,128)(2,1)S(1)}, u32[]{:S(2)}, u32[]{:S(2)}) collective-permute-start(bf16[512,512]{1,0:T(8,128)(2,1)} %reduce-precision_convert_fusion.1), channel_id=1, source_target_pairs={{33,97},{35,99},{37,101},{39,103},{41,105},{43,107},{45,109},{47,1... | collective-permute-start | bytes 1572872 | tf_op jit(solution)/shard_map/ppermute | solution.py:25
  18.7 1.5 %collective-permute-start = (f32[8,512]{1,0:T(8,128)S(1)}, f32[8,512]{1,0:T(8,128)S(1)}, u32[]{:S(2)}, u32[]{:S(2)}) collective-permute-start(f32[8,512]{1,0:T(8,128)S(1)} %fusion.18), channel_id=1, source_target_pairs={{1,33},{3,35},{5,37},{7,39},{9,41},{11,43},{13,45},{15,47},{17,49}... | collective-permute-start | bytes 49160 | tf_op jit(solution)/shard_map/ppermute | solution.py:25
  19.6 4.4 %collective-permute-start.1 = (f32[8,512]{1,0:T(8,128)S(1)}, f32[8,512]{1,0:T(8,128)S(1)}, u32[]{:S(2)}, u32[]{:S(2)}) collective-permute-start(f32[8,512]{1,0:T(8,128)S(1)} %fusion.18), channel_id=1, source_target_pairs={{1,65},{3,67},{5,69},{7,71},{9,73},{11,75},{13,77},{15,79},{17,81}... | collective-permute-start | bytes 49160 | tf_op jit(solution)/shard_map/ppermute | solution.py:25
  24.4 1.6 %collective-permute-start.3 = (f32[8,512]{1,0:T(8,128)S(1)}, f32[8,512]{1,0:T(8,128)S(1)}, u32[]{:S(2)}, u32[]{:S(2)}) collective-permute-start(f32[8,512]{1,0:T(8,128)S(1)} %convolution_add_fusion.8), channel_id=1, source_target_pairs={{1,97},{3,99},{5,101},{7,103},{9,105},{11,107},{13,109},{15,111},{... | collective-permute-start | bytes 49160 | tf_op jit(solution)/shard_map/ppermute | solution.py:25
  25.6 1.7 %copy-start.8 = (s32[1,1,4]{2,1,0:T(1,128)S(1)}, s32[1,1,4]{2,1,0:T(1,128)}, u32[]{:S(2)}) copy-start(s32[1,1,4]{2,1,0:T(1,128)} %param.21) | copy-start | bytes 52
  26.6 0.7 collective-permute-start.5
  27.8 0.7 collective-permute-start.6
  29.0 39.8 %copy-start.2 = (bf16[1,1,1536,256]{3,2,1,0:T(8,128)(2,1)S(1)}, bf16[1,1,1536,256]{3,2,1,0:T(8,128)(2,1)}, u32[]{:S(2)}) copy-start(bf16[1,1,1536,256]{3,2,1,0:T(8,128)(2,1)} %param.17) | copy-start | bytes 2359300
  29.0 39.8 %copy-start.4 = (bf16[1,1,256,128]{3,2,1,0:T(8,128)(2,1)S(1)}, bf16[1,1,256,128]{3,2,1,0:T(8,128)(2,1)}, u32[]{:S(2)}) copy-start(bf16[1,1,256,128]{3,2,1,0:T(8,128)(2,1)} %param.18) | copy-start | bytes 196612
  29.0 1.5 %collective-permute-start.7 = (f32[8,512]{1,0:T(8,128)S(1)}, f32[8,512]{1,0:T(8,128)S(1)}, u32[]{:S(2)}, u32[]{:S(2)}) collective-permute-start(f32[8,512]{1,0:T(8,128)S(1)} %convolution_add_fusion.5), channel_id=1, source_target_pairs={{289,385},{291,387},{293,389},{295,391},{297,393},{299,395},{301,3... | collective-permute-start | bytes 49160 | tf_op jit(solution)/shard_map/ppermute | solution.py:25
  31.0 0.7 collective-permute-start.8
  33.0 44.7 %all-to-all-start.1 = ((bf16[32,8,512]{2,1,0:T(8,128)(2,1)}), bf16[32,8,512]{2,1,0:T(8,128)(2,1)S(1)}, u32[]{:S(2)}, u32[]{:S(2)}) async-start(bf16[32,8,512]{2,1,0:T(8,128)(2,1)} %broadcast_in_dim.48), calls=%async_computation.1 | async-start | bytes 524288 | tf_op jit(solution)/shard_map/all_to_all | solution.py:19
  78.9 18.2 %copy-start.3 = (bf16[128,128]{1,0:T(8,128)(2,1)}, bf16[128,128]{1,0:T(8,128)(2,1)S(1)}, u32[]{:S(2)}) copy-start(bf16[128,128]{1,0:T(8,128)(2,1)S(1)} %fusion.4) | copy-start | bytes 98308
  78.9 15.6 %collective-permute-start.9 = (bf16[128,128]{1,0:T(8,128)(2,1)S(1)}, bf16[128,128]{1,0:T(8,128)(2,1)S(1)}, u32[]{:S(2)}, u32[]{:S(2)}) collective-permute-start(bf16[128,128]{1,0:T(8,128)(2,1)S(1)} %fusion.4), channel_id=1, source_target_pairs={{0,2},{1,3},{2,4},{3,5},{4,6},{5,7},{6,8},{7,9},{8,10},{9,11},{10,... | collective-permute-start | bytes 98312 | tf_op jit(solution)/shard_map/ppermute | solution.py:30
  81.0 13.5 %collective-permute-start.10 = (bf16[128,128]{1,0:T(8,128)(2,1)S(1)}, bf16[128,128]{1,0:T(8,128)(2,1)S(1)}, u32[]{:S(2)}, u32[]{:S(2)}) collective-permute-start(bf16[128,128]{1,0:T(8,128)(2,1)S(1)} %fusion.4), channel_id=1, source_target_pairs={{0,1},{1,2},{2,3},{3,4},{4,5},{5,6},{6,7},{7,8},{8,9},{9,10},{10,1... | collective-permute-start | bytes 98312 | tf_op jit(solution)/shard_map/ppermute | solution.py:30
  83.2 11.3 %collective-permute-start.11 = (bf16[128,128]{1,0:T(8,128)(2,1)S(1)}, bf16[128,128]{1,0:T(8,128)(2,1)S(1)}, u32[]{:S(2)}, u32[]{:S(2)}) collective-permute-start(bf16[128,128]{1,0:T(8,128)(2,1)S(1)} %fusion.4), channel_id=1, source_target_pairs={{0,31},{1,0},{2,1},{3,2},{4,3},{5,4},{6,5},{7,6},{8,7},{9,8},{10,9... | collective-permute-start | bytes 98312 | tf_op jit(solution)/shard_map/ppermute | solution.py:30
  89.9 5.8 %collective-permute-start.12 = (bf16[128,128]{1,0:T(8,128)(2,1)S(1)}, bf16[128,128]{1,0:T(8,128)(2,1)S(1)}, u32[]{:S(2)}, u32[]{:S(2)}) collective-permute-start(bf16[128,128]{1,0:T(8,128)(2,1)S(1)} %fusion.4), channel_id=1, source_target_pairs={{0,30},{1,31},{2,0},{3,1},{4,2},{5,3},{6,4},{7,5},{8,6},{9,7},{10,... | collective-permute-start | bytes 98312 | tf_op jit(solution)/shard_map/ppermute | solution.py:30

commit v2 on v1

v2 whole, which is shorter than its diff:
```python
import jax
import jax.numpy as jnp
from jax import lax
from jax.experimental import pallas as pl
from jax.experimental.pallas import tpu as pltpu
from jax.sharding import PartitionSpec as P


BF16 = jnp.bfloat16
F32 = jnp.float32
HALF = 8
PARTS = 2


def split(value):
    high = lax.reduce_precision(value, 8, 7)
    return high.astype(BF16), (value - high).astype(BF16)


def spread(piece, parts=1):
    peers = lax.axis_size("sub") // parts
    copies = jnp.broadcast_to(piece[None], (peers,) + piece.shape)
    groups = [list(range(part * peers, (part + 1) * peers)) for part in range(parts)]
    return lax.all_to_all(copies, "sub", 0, 0, axis_index_groups=groups if parts > 1 else None)


def along_chain(value, by, groups):
    peers = lax.axis_size("sub")
    pairs = [((g - by) * peers + s, g * peers + s) for g in groups if g >= by for s in range(1, peers, 2)]
    return lax.ppermute(value, ("grp", "sub"), pairs)


def swap_cores(value):
    peers = lax.axis_size("sub")
    return lax.ppermute(value, "sub", [(i, i ^ 1) for i in range(peers)])


def even_along_loop(value, by):
    peers = lax.axis_size("sub")
    return lax.ppermute(value, "sub", [(i, (i + by) % peers) for i in range(0, peers, 2)])


def even_to_odd(value):
    peers = lax.axis_size("sub")
    return lax.ppermute(value, "sub", [(i, i + 1) for i in range(0, peers, 2)])


def rows_times(value, left):
    dims = (((1,), (1,)), ((), ()))
    return lax.dot_general(value, left, dims, precision=lax.Precision.HIGH, preferred_element_type=F32)


ROWS = 256


def prepare_kernel(picks, mine, partner, before, after, returned, modes, basis, coeffs, weight, fixed, linked):
    size = mine.shape[0]
    length = weight.shape[1]
    parity = picks[5]
    for slot in range(4):
        pick = picks[slot]
        rows = pl.ds(slot * size, size)

        @pl.when(pick < 2)
        def _():
            linked[rows, :] = before[pick] + returned[pick]

        @pl.when(pick == parity + 2)
        def _():
            linked[rows, :] = mine[...]

        @pl.when(pick == 3 - parity)
        def _():
            linked[rows, :] = partner[...]

        @pl.when(pick > 3)
        def _():
            linked[rows, :] = after[pick - 4] + returned[pick - 2]

    live = lax.broadcasted_iota(jnp.int32, coeffs.shape, 0) < picks[4]
    kept = jnp.where(live, coeffs[...], jnp.zeros(coeffs.shape, coeffs.dtype))

    @pl.loop(0, modes.shape[0] // ROWS)
    def _(step):
        rows = pl.ds(pl.multiple_of(step * ROWS, ROWS), ROWS)
        both = jnp.dot(modes[rows, :], linked[...], preferred_element_type=F32)
        weight[rows, :] = both[:, :length].astype(BF16)
        fixed[rows, :] = both[:, length:] + jnp.dot(basis[rows, :], kept, preferred_element_type=F32)


def prepare(picks, mine, partner, before, after, returned, modes, basis, coeffs):
    vmem = pl.BlockSpec(memory_space=pltpu.VMEM)
    points, depth = modes.shape
    columns = coeffs.shape[1]
    length = mine.shape[1] - columns
    return pl.pallas_call(
        prepare_kernel,
        out_shape=(jax.ShapeDtypeStruct((points, length), BF16), jax.ShapeDtypeStruct((points, columns), F32)),
        in_specs=[pl.BlockSpec(memory_space=pltpu.SMEM)] + [vmem] * 8,
        out_specs=(vmem, vmem),
        scratch_shapes=[pltpu.VMEM((depth, mine.shape[1]), BF16)],
        compiler_params=pltpu.CompilerParams(vmem_limit_bytes=24 << 20),
        cost_estimate=pl.CostEstimate(flops=1_200_000_000, bytes_accessed=7_000_000, transcendentals=0),
    )(picks, mine, partner, before, after, returned, modes, basis, coeffs)


def close_kernel(pieces, coupling, own, weight, fixed, top, block, interior):
    chips, _, columns, length = pieces.shape
    field = pieces[:, 1].reshape(chips * columns, length).astype(F32).T
    top[...] = field
    rounded = field.astype(BF16)
    block[...] = (own[...] + jnp.dot(coupling[...], rounded, preferred_element_type=F32)).astype(BF16)

    @pl.loop(0, weight.shape[0] // ROWS)
    def _(step):
        rows = pl.ds(pl.multiple_of(step * ROWS, ROWS), ROWS)
        part = jnp.dot(weight[rows, :], rounded, preferred_element_type=F32)
        interior[rows, :] = (fixed[rows, :] + part).astype(BF16)


def close(pieces, coupling, own_block, weight, fixed):
    members, columns, length = pieces.shape
    vmem = pl.BlockSpec(memory_space=pltpu.VMEM)
    return pl.pallas_call(
        close_kernel,
        out_shape=(
            jax.ShapeDtypeStruct((length, members // 2 * columns), F32),
            jax.ShapeDtypeStruct(own_block.shape, BF16),
            jax.ShapeDtypeStruct(fixed.shape, BF16),
        ),
        in_specs=[vmem] * 5,
        out_specs=(vmem, vmem, vmem),
        compiler_params=pltpu.CompilerParams(vmem_limit_bytes=24 << 20),
        cost_estimate=pl.CostEstimate(flops=230_000_000, bytes_accessed=4_000_000, transcendentals=0),
    )(pieces.reshape(members // 2, 2, columns, length), coupling, own_block, weight, fixed)


def body(
    top_basis,
    top_coeffs,
    top_coupling,
    block_coupling,
    block_basis,
    block_coeffs,
    sub_basis,
    sub_coeffs,
    basis_widths,
    constraint_modes,
    adjacency,
):
    chain = lax.axis_size("grp")
    place = lax.axis_index("sub")
    coupling = top_coupling[0]
    high, low = split(coupling)

    basis = spread(top_basis[0]).reshape(-1, top_basis.shape[-1])
    back_1 = along_chain(high, 1, range(2, chain))

    chips = lax.axis_size("sub") // (2 * PARTS)
    columns = top_coeffs.shape[-1] // chips
    coeffs = lax.dynamic_slice_in_dim(top_coeffs[0].T, (place // 2 % chips) * columns, columns, 0)
    own = lax.dot_general(coeffs, basis, (((1,), (1,)), ((), ())), preferred_element_type=F32)

    own_1 = along_chain(own, 1, range(1, chain))
    two = jnp.dot(high, back_1, preferred_element_type=F32) + jnp.dot(low, back_1, preferred_element_type=F32)
    two_high, two_low = split(two)
    field = own + rows_times(own_1, coupling)

    back_2 = along_chain(two_high, 2, range(HALF, chain))
    late_2 = along_chain(field, 2, range(HALF, chain))
    for first in range(2, HALF, 2):
        earlier = along_chain(field, 2, range(first, first + 2))
        field = field + rows_times(earlier, two)
    field = field + rows_times(late_2, two)
    four = jnp.dot(two_high, back_2, preferred_element_type=F32) + jnp.dot(two_low, back_2, preferred_element_type=F32)
    for first in range(HALF, chain, 4):
        earlier = along_chain(field, 4, range(first, first + 4))
        field = field + rows_times(earlier, four)

    pieces = spread(field.astype(BF16), PARTS)

    own_block = jnp.dot(block_basis[0, 0], block_coeffs[0, 0], preferred_element_type=F32)
    block_high = block_coupling[0, 0].astype(BF16)
    mine = jnp.concatenate([block_high, own_block.astype(BF16)], axis=1)
    partner = swap_cores(mine)
    pair = jnp.stack([mine, partner])
    before = even_along_loop(pair, 2)
    after = even_along_loop(pair, -2)
    both = jnp.concatenate([before, after])
    returned = even_to_odd(both)
    parity = place % 2
    picks = jnp.concatenate([adjacency[0, 0] + parity, basis_widths[0], parity[None]]).astype(jnp.int32)
    weight, fixed = prepare(
        picks,
        mine,
        partner,
        before,
        after,
        returned,
        constraint_modes[0, 0],
        sub_basis[0, 0],
        sub_coeffs[0, 0],
    )
    top_field, block, interior = close(pieces, block_high, own_block, weight, fixed)
    return (top_field[None], block[None, None], interior[None, None])


def solution(mesh):
    placed = (
        P("grp", "sub", None),
        P("grp", None, None),
        P("grp", None, None),
        P("grp", "sub", None, None),
        P("grp", "sub", None, None),
        P("grp", "sub", None, None),
        P("grp", "sub", None, None),
        P("grp", "sub", None, None),
        P("grp", "sub"),
        P("grp", "sub", None, None),
        P("grp", "sub", None),
    )

    return jax.shard_map(
        body,
        mesh=mesh,
        in_specs=placed,
        out_specs=(P("grp", None, None), P("grp", "sub", None, None), P("grp", "sub", None, None)),
        check_vma=False,
    )
```

time: 98.7 us -> 81.6 us (0.83)
  the two profiles are of different devices: /device:TPU:480 before, /device:TPU:423 now
where the time goes in v2:
time: 81.6 us; the launch traced here: 80.8 us
  starting transfers between devices  32.3 us (40%)
  waiting for transfers between devices  21.5 us (26%)
  local copies, waits for them, and re-layouts  9.43 us (12%)
  matrix products  7.85 us (10%)
  Pallas kernels  5.56 us (7%)
  other arithmetic  2.49 us (3%)
  between operations  1.73 us (2%)
    ppermute x9, waiting for transfers between devices, along_chain(): return lax.ppermute(value, ('grp', 'sub'), pairs)  20.6 us
    ppermute x9, starting transfers between devices, along_chain(): return lax.ppermute(value, ('grp', 'sub'), pairs)  14.4 us
    all_to_all x2, starting transfers between devices, spread(): lax.all_to_all(copies, 'sub', 0, 0, axis_index_groups=groups if parts > 1...  13.3 us
    unnamed x34, local copies, waits for them, and re-layouts  7.22 us
    dot_general x7, matrix products, rows_times(): lax.dot_general(value, left, dims, precision=lax.Precision.HIGH, preferre...  3.64 us
    pallas_call x1, Pallas kernels, prepare(): pl.pallas_call(prepare_kernel, out_shape=(jax.ShapeDtypeStruct((points, l...  3.24 us
    pallas_call x1, Pallas kernels, close(): pl.pallas_call(close_kernel, out_shape=(jax.ShapeDtypeStruct((length, mem...  2.32 us
    broadcast_in_dim x2, local copies, waits for them, and re-layouts, spread(): copies = jnp.broadcast_to(piece[None], (peers,) + piece.shape)  2.21 us
  transfers between devices with their start and end apart: 15, of which 4 were waited for; matrix products, arithmetic and copies ran while one was open for 14% of the time, Pallas kernels for 4%

profile of v2, /device:TPU:423, one launch (start us, length us, event | category | flops | bytes accessed | tf_op | source)
XLA Modules:
  0.0 80.8 jit_solution(6577752018251960479)
XLA Ops:
  0.7 1.5 %broadcast_in_dim.26 = bf16[32,16,256]{2,1,0:T(8,128)(2,1)} broadcast(bf16[16,256]{1,0:T(8,128)(2,1)} %bitcast.64), dimensions={1,2} | broadcast | bytes 270336 | tf_op jit(solution)/shard_map/broadcast_in_dim | solution.py:22
  2.1 7.9 %all-to-all-start = ((bf16[32,16,256]{2,1,0:T(8,128)(2,1)}), bf16[32,16,256]{2,1,0:T(8,128)(2,1)S(1)}, u32[]{:S(2)}, u32[]{:S(2)}) async-start(bf16[32,16,256]{2,1,0:T(8,128)(2,1)} %broadcast_in_dim.26), calls=%async_computation | async-start | bytes 524288 | tf_op jit(solution)/shard_map/all_to_all | solution.py:24
  10.0 1.4 %reduce-precision_convert_fusion.1 = bf16[512,512]{1,0:T(8,128)(2,1)S(1)} fusion(f32[1,512,512]{2,1,0:T(8,128)} %param.13), kind=kLoop, calls=%fused_computation.3 | loop fusion | flops 524288 | bytes 1572864 | tf_op jit(solution)/shard_map/convert_element_type | solution.py:17
  11.4 2.6 %collective-permute-start.2 = (bf16[512,512]{1,0:T(8,128)(2,1)S(1)}, bf16[512,512]{1,0:T(8,128)(2,1)}, u32[]{:S(2)}, u32[]{:S(2)}) collective-permute-start(bf16[512,512]{1,0:T(8,128)(2,1)S(1)} %reduce-precision_convert_fusion.1), channel_id=1, source_target_pairs={{33,65},{35,67},{37,69},{39,71},{41,73},{43,75},{45,77},{47,79},{4... | collective-permute-start | bytes 1572872 | tf_op jit(solution)/shard_map/ppermute | solution.py:30
  14.2 0.1 fusion.17
  14.3 1.9 %collective-permute-start.9 = (bf16[128,640]{1,0:T(8,128)(2,1)S(1)}, bf16[128,640]{1,0:T(8,128)(2,1)S(1)}, u32[]{:S(2)}, u32[]{:S(2)}) collective-permute-start(bf16[128,640]{1,0:T(8,128)(2,1)S(1)} %get-tuple-element.14.mine), channel_id=1, source_target_pairs={{0,1},{1,0},{2,3},{3,2},{4,5},{5,4},{6,7},{7,6},{8,9},{9,8},{10,11... | collective-permute-start | bytes 491528 | tf_op jit(solution)/shard_map/ppermute | solution.py:35
  16.3 0.9 %all-to-all-done = bf16[32,16,256]{2,1,0:T(8,128)(2,1)S(1)} async-done(((bf16[32,16,256]{2,1,0:T(8,128)(2,1)}), bf16[32,16,256]{2,1,0:T(8,128)(2,1)S(1)}, u32[]{:S(2)}, u32[]{:S(2)}) %all-to-all-start) | async-done | bytes 262176 | tf_op jit(solution)/shard_map/all_to_all | solution.py:24
  17.2 0.2 fusion.9
  17.4 2.7 %collective-permute-start = (f32[16,512]{1,0:T(8,128)S(1)}, f32[16,512]{1,0:T(8,128)S(1)}, u32[]{:S(2)}, u32[]{:S(2)}) collective-permute-start(f32[16,512]{1,0:T(8,128)S(1)} %fusion.9), channel_id=1, source_target_pairs={{1,33},{3,35},{5,37},{7,39},{9,41},{11,43},{13,45},{15,47},{17,49}... | collective-permute-start | bytes 98312 | tf_op jit(solution)/shard_map/ppermute | solution.py:30
  20.1 0.7 collective-permute-start.10
  20.8 0.7 collective-permute-start.11
  21.5 0.6 collective-permute-done
  22.1 0.5 convolution_add_fusion.7
  22.6 0.0 copy-done.11
  22.6 3.1 %collective-permute-start.5 = (f32[16,512]{1,0:T(8,128)S(1)}, f32[16,512]{1,0:T(8,128)S(1)}, u32[]{:S(2)}, u32[]{:S(2)}) collective-permute-start(f32[16,512]{1,0:T(8,128)S(1)} %convolution_add_fusion.7), channel_id=1, source_target_pairs={{193,257},{195,259},{197,261},{199,263},{201,265},{203,267},{205,2... | collective-permute-start | bytes 98312 | tf_op jit(solution)/shard_map/ppermute | solution.py:30
  25.7 0.8 collective-permute-start.1
  26.6 1.5 %fusion.7 = f32[512,512]{1,0:T(8,128)S(1)} fusion(bf16[512,512]{1,0:T(8,128)(2,1)} %collective-permute-done.2, f32[1,512,512]{2,1,0:T(8,128)S(1)} %copy-done.10), kind=kOutput, calls=%fused_computation.19 | convolution fusion | flops 269221888 | bytes 2621440 | tf_op jit(solution)/shard_map/dot_general | solution.py:165
  28.1 1.5 %reduce-precision_convert_fusion = (bf16[512,512]{1,0:T(8,128)(2,1)S(1)}, f32[512,512]{1,0:T(8,128)S(1)}) fusion(f32[512,512]{1,0:T(8,128)S(1)} %fusion.7, bf16[512,512]{1,0:T(8,128)(2,1)S(1)} %copy-done.12, bf16[512,512]{1,0:T(8,128)(2,1)} %collective-permute-done.2), kind=kOutput, calls=%fused_computation.1 | convolution fusion | flops 269221888 | bytes 3670016 | tf_op jit(solution)/shard_map/dot_general | solution.py:165
  29.6 0.5 convolution_add_fusion.6
  30.1 0.7 collective-permute-start.3
  30.8 0.9 %pad_maximum_fusion = bf16[4,128,640]{2,1,0:T(8,128)(2,1)} fusion(bf16[2,128,640]{2,1,0:T(8,128)(2,1)S(1)} %collective-permute-done.11.after, bf16[2,128,640]{2,1,0:T(8,128)(2,1)S(1)} %collective-permute-done.10.before), kind=kLoop, calls=%fused_computation.17 | loop fusion | flops 327680 | bytes 1310720 | tf_op jit(solution)/shard_map/concatenate | solution.py:189
  31.7 1.3 %collective-permute-start.12 = (bf16[4,128,640]{2,1,0:T(8,128)(2,1)}, bf16[4,128,640]{2,1,0:T(8,128)(2,1)S(1)}, u32[]{:S(2)}, u32[]{:S(2)}) collective-permute-start(bf16[4,128,640]{2,1,0:T(8,128)(2,1)} %pad_maximum_fusion), channel_id=1, source_target_pairs={{0,1},{2,3},{4,5},{6,7},{8,9},{10,11},{12,13},{14,15},{16,17},{18,... | collective-permute-start | bytes 1966088 | tf_op jit(solution)/shard_map/ppermute | solution.py:45
  33.0 1.9 %collective-permute-start.7 = (bf16[512,512]{1,0:T(8,128)(2,1)S(1)}, bf16[512,512]{1,0:T(8,128)(2,1)S(1)}, u32[]{:S(2)}, u32[]{:S(2)}) collective-permute-start(bf16[512,512]{1,0:T(8,128)(2,1)S(1)} %get-tuple-element.15), channel_id=1, source_target_pairs={{193,257},{195,259},{197,261},{199,263},{201,265},{203,267},{205,2... | collective-permute-start | bytes 1572872 | tf_op jit(solution)/shard_map/ppermute | solution.py:30
  34.9 0.5 convolution_add_fusion.5
  35.5 0.7 collective-permute-start.4
  36.1 0.5 fusion.18
  36.7 0.0 collective-permute-done.4
  36.7 0.5 fusion
  37.2 0.7 collective-permute-start.6
  37.9 12.8 %collective-permute-done.7 = bf16[512,512]{1,0:T(8,128)(2,1)S(1)} collective-permute-done((bf16[512,512]{1,0:T(8,128)(2,1)S(1)}, bf16[512,512]{1,0:T(8,128)(2,1)S(1)}, u32[]{:S(2)}, u32[]{:S(2)}) %collective-permute-start.7) | collective-permute-done | bytes 524320 | tf_op jit(solution)/shard_map/ppermute | solution.py:30
  50.7 0.4 fusion.5
  51.1 0.4 convolution_add_fusion
  51.6 0.5 convolution_add_fusion.3
  52.1 1.3 %collective-permute-start.8 = (f32[16,512]{1,0:T(8,128)S(1)}, f32[16,512]{1,0:T(8,128)S(1)}, u32[]{:S(2)}, u32[]{:S(2)}) collective-permute-start(f32[16,512]{1,0:T(8,128)S(1)} %convolution_add_fusion.3), channel_id=1, source_target_pairs={{257,385},{259,387},{261,389},{263,391},{265,393},{267,395},{269,3... | collective-permute-start | bytes 98312 | tf_op jit(solution)/shard_map/ppermute | solution.py:30
  53.4 7.3 %collective-permute-done.8 = f32[16,512]{1,0:T(8,128)S(1)} collective-permute-done((f32[16,512]{1,0:T(8,128)S(1)}, f32[16,512]{1,0:T(8,128)S(1)}, u32[]{:S(2)}, u32[]{:S(2)}) %collective-permute-start.8) | collective-permute-done | bytes 32800 | tf_op jit(solution)/shard_map/ppermute | solution.py:30
  60.7 0.5 fusion.1
  61.2 0.7 broadcast_in_dim.27
  61.9 5.4 %all-to-all-start.1 = ((bf16[16,16,512]{2,1,0:T(8,128)(2,1)}), bf16[16,16,512]{2,1,0:T(8,128)(2,1)S(1)}, u32[]{:S(2)}, u32[]{:S(2)}) async-start(bf16[16,16,512]{2,1,0:T(8,128)(2,1)} %broadcast_in_dim.27), calls=%async_computation.1 | async-start | bytes 524288 | tf_op jit(solution)/shard_map/all_to_all | solution.py:24
  68.0 0.1 pad_add_fusion.picks
  68.1 0.9 %copy-done.7 = bf16[4,128,640]{2,1,0:T(8,128)(2,1)} copy-done((bf16[4,128,640]{2,1,0:T(8,128)(2,1)}, bf16[4,128,640]{2,1,0:T(8,128)(2,1)S(1)}, u32[]{:S(2)}) %copy-start.7) | copy-done | bytes 655384
  68.9 0.9 %copy-done.2 = bf16[128,640]{1,0:T(8,128)(2,1)S(1)} copy-done((bf16[128,640]{1,0:T(8,128)(2,1)S(1)}, bf16[128,640]{1,0:T(8,128)(2,1)}, u32[]{:S(2)}) %copy-start.2) | copy-done | bytes 163864
  69.9 0.9 %copy-done.4 = bf16[128,640]{1,0:T(8,128)(2,1)S(1)} copy-done((bf16[128,640]{1,0:T(8,128)(2,1)S(1)}, bf16[128,640]{1,0:T(8,128)(2,1)}, u32[]{:S(2)}) %copy-start.4) | copy-done | bytes 163864
  70.8 1.4 %copy-done.5 = bf16[1,1,1536,512]{3,2,1,0:T(8,128)(2,1)S(1)} copy-done((bf16[1,1,1536,512]{3,2,1,0:T(8,128)(2,1)S(1)}, bf16[1,1,1536,512]{3,2,1,0:T(8,128)(2,1)}, u32[]{:S(2)}) %copy-start.5) | copy-done | bytes 1572888
  72.2 1.1 %copy-done.6 = bf16[1,1,1536,256]{3,2,1,0:T(8,128)(2,1)S(1)} copy-done((bf16[1,1,1536,256]{3,2,1,0:T(8,128)(2,1)S(1)}, bf16[1,1,1536,256]{3,2,1,0:T(8,128)(2,1)}, u32[]{:S(2)}) %copy-start.6) | copy-done | bytes 786456
  73.3 1.1 %copy-done.8 = bf16[4,128,640]{2,1,0:T(8,128)(2,1)S(1)} copy-done((bf16[4,128,640]{2,1,0:T(8,128)(2,1)S(1)}, bf16[4,128,640]{2,1,0:T(8,128)(2,1)}, u32[]{:S(2)}) %copy-start.8) | copy-done | bytes 655384
  74.4 0.8 %copy-done.9 = bf16[1,1,256,128]{3,2,1,0:T(8,128)(2,1)S(1)} copy-done((bf16[1,1,256,128]{3,2,1,0:T(8,128)(2,1)S(1)}, bf16[1,1,256,128]{3,2,1,0:T(8,128)(2,1)}, u32[]{:S(2)}) %copy-start.9) | copy-done | bytes 65560
  75.2 3.2 %shard_map.130 = (bf16[1536,512]{1,0:T(8,128)(2,1)S(1)}, f32[1536,128]{1,0:T(8,128)S(1)}) custom-call(s32[6]{0:T(128)S(1)} %pad_add_fusion.picks, bf16[128,640]{1,0:T(8,128)(2,1)S(1)} %copy-done.4, bf16[128,640]{1,0:T(8,128)(2,1)S(1)} %copy-done.2, bf16[2,128,640]{2,1,0:T(8,128)(2,1)S(1)} %collective-permute-done.10.before, ...), custom_call_target="tpu_custom_call" | custom-call | flops 1200000000 | bytes 7000000 | tf_op jit(solution)/shard_map/pallas_call | solution.py:96
  78.5 2.3 %shard_map.131 = (f32[512,128]{1,0:T(8,128)}, bf16[128,128]{1,0:T(8,128)(2,1)}, bf16[1536,128]{1,0:T(8,128)(2,1)}) custom-call(bf16[8,2,16,512]{3,2,1,0:T(8,128)(2,1)S(1)} %bitcast.58, bf16[128,512]{1,0:T(8,128)(2,1)S(1)} %convert_bitcast_fusion.coupling, f32[128,128]{1,0:T(8,128)S(1)} %get-tuple-element.18.own, ...), custom_call_target="tpu_custom_call" | custom-call | flops 230000000 | bytes 4000000 | tf_op jit(solution)/shard_map/pallas_call | solution.py:124
  (40 shorter events, 0.2 us)
Async XLA Ops:
  0.6 16.5 %copy-start = (bf16[1,256,128]{2,1,0:T(8,128)(2,1)S(1)}, bf16[1,256,128]{2,1,0:T(8,128)(2,1)}, u32[]{:S(2)}) copy-start(bf16[1,256,128]{2,1,0:T(8,128)(2,1)} %param.12) | copy-start | bytes 196612
  0.6 13.5 %copy-start.13 = (f32[1,1,128,512]{3,2,1,0:T(8,128)S(1)}, f32[1,1,128,512]{3,2,1,0:T(8,128)}, u32[]{:S(2)}) copy-start(f32[1,1,128,512]{3,2,1,0:T(8,128)} %param.14) | copy-start | bytes 786436
  0.7 13.5 %copy-start.14 = (bf16[1,1,128,128]{3,2,1,0:T(8,128)(2,1)S(1)}, bf16[1,1,128,128]{3,2,1,0:T(8,128)(2,1)}, u32[]{:S(2)}) copy-start(bf16[1,1,128,128]{3,2,1,0:T(8,128)(2,1)} %param.16) | copy-start | bytes 98308
  0.7 13.5 %copy-start.15 = (bf16[1,1,128,128]{3,2,1,0:T(8,128)(2,1)S(1)}, bf16[1,1,128,128]{3,2,1,0:T(8,128)(2,1)}, u32[]{:S(2)}) copy-start(bf16[1,1,128,128]{3,2,1,0:T(8,128)(2,1)} %param.15) | copy-start | bytes 98308
  2.1 15.0 %all-to-all-start = ((bf16[32,16,256]{2,1,0:T(8,128)(2,1)}), bf16[32,16,256]{2,1,0:T(8,128)(2,1)S(1)}, u32[]{:S(2)}, u32[]{:S(2)}) async-start(bf16[32,16,256]{2,1,0:T(8,128)(2,1)} %broadcast_in_dim.26), calls=%async_computation | async-start | bytes 524288 | tf_op jit(solution)/shard_map/all_to_all | solution.py:24
  10.0 12.0 %copy-start.10 = (f32[1,512,512]{2,1,0:T(8,128)S(1)}, f32[1,512,512]{2,1,0:T(8,128)}, u32[]{:S(2)}) copy-start(f32[1,512,512]{2,1,0:T(8,128)} %param.13) | copy-start | bytes 3145732
  11.4 11.2 %copy-start.11 = (bf16[512,512]{1,0:T(8,128)(2,1)}, bf16[512,512]{1,0:T(8,128)(2,1)S(1)}, u32[]{:S(2)}) copy-start(bf16[512,512]{1,0:T(8,128)(2,1)S(1)} %reduce-precision_convert_fusion.1) | copy-start | bytes 1572868
  11.4 15.1 %collective-permute-start.2 = (bf16[512,512]{1,0:T(8,128)(2,1)S(1)}, bf16[512,512]{1,0:T(8,128)(2,1)}, u32[]{:S(2)}, u32[]{:S(2)}) collective-permute-start(bf16[512,512]{1,0:T(8,128)(2,1)S(1)} %reduce-precision_convert_fusion.1), channel_id=1, source_target_pairs={{33,65},{35,67},{37,69},{39,71},{41,73},{43,75},{45,77},{47,79},{4... | collective-permute-start | bytes 1572872 | tf_op jit(solution)/shard_map/ppermute | solution.py:30
  14.3 13.7 %copy-start.3 = (bf16[128,640]{1,0:T(8,128)(2,1)}, bf16[128,640]{1,0:T(8,128)(2,1)S(1)}, u32[]{:S(2)}) copy-start(bf16[128,640]{1,0:T(8,128)(2,1)S(1)} %get-tuple-element.14.mine) | copy-start | bytes 491524
  14.3 5.7 %collective-permute-start.9 = (bf16[128,640]{1,0:T(8,128)(2,1)S(1)}, bf16[128,640]{1,0:T(8,128)(2,1)S(1)}, u32[]{:S(2)}, u32[]{:S(2)}) collective-permute-start(bf16[128,640]{1,0:T(8,128)(2,1)S(1)} %get-tuple-element.14.mine), channel_id=1, source_target_pairs={{0,1},{1,0},{2,3},{3,2},{4,5},{5,4},{6,7},{7,6},{8,9},{9,8},{10,11... | collective-permute-start | bytes 491528 | tf_op jit(solution)/shard_map/ppermute | solution.py:35
  17.4 4.7 %collective-permute-start = (f32[16,512]{1,0:T(8,128)S(1)}, f32[16,512]{1,0:T(8,128)S(1)}, u32[]{:S(2)}, u32[]{:S(2)}) collective-permute-start(f32[16,512]{1,0:T(8,128)S(1)} %fusion.9), channel_id=1, source_target_pairs={{1,33},{3,35},{5,37},{7,39},{9,41},{11,43},{13,45},{15,47},{17,49}... | collective-permute-start | bytes 98312 | tf_op jit(solution)/shard_map/ppermute | solution.py:30
  20.1 8.0 %copy-start.1 = (bf16[128,640]{1,0:T(8,128)(2,1)}, bf16[128,640]{1,0:T(8,128)(2,1)S(1)}, u32[]{:S(2)}) copy-start(bf16[128,640]{1,0:T(8,128)(2,1)S(1)} %collective-permute-done.9.partner) | copy-start | bytes 491524
  20.1 10.6 %collective-permute-start.10 = (bf16[2,128,640]{2,1,0:T(8,128)(2,1)S(1)}, bf16[2,128,640]{2,1,0:T(8,128)(2,1)S(1)}, u32[]{:S(2)}, u32[]{:S(2)}) collective-permute-start(bf16[2,128,640]{2,1,0:T(8,128)(2,1)S(1)} %pad_maximum_fusion.1), channel_id=1, source_target_pairs={{0,2},{2,4},{4,6},{6,8},{8,10},{10,12},{12,14},{14,16},{16,18},{18... | collective-permute-start | bytes 983048 | tf_op jit(solution)/shard_map/ppermute | solution.py:40
  20.8 9.9 %collective-permute-start.11 = (bf16[2,128,640]{2,1,0:T(8,128)(2,1)S(1)}, bf16[2,128,640]{2,1,0:T(8,128)(2,1)S(1)}, u32[]{:S(2)}, u32[]{:S(2)}) collective-permute-start(bf16[2,128,640]{2,1,0:T(8,128)(2,1)S(1)} %pad_maximum_fusion.1), channel_id=1, source_target_pairs={{0,30},{2,0},{4,2},{6,4},{8,6},{10,8},{12,10},{14,12},{16,14},{18,... | collective-permute-start | bytes 983048 | tf_op jit(solution)/shard_map/ppermute | solution.py:40
  22.6 13.5 %collective-permute-start.5 = (f32[16,512]{1,0:T(8,128)S(1)}, f32[16,512]{1,0:T(8,128)S(1)}, u32[]{:S(2)}, u32[]{:S(2)}) collective-permute-start(f32[16,512]{1,0:T(8,128)S(1)} %convolution_add_fusion.7), channel_id=1, source_target_pairs={{193,257},{195,259},{197,261},{199,263},{201,265},{203,267},{205,2... | collective-permute-start | bytes 98312 | tf_op jit(solution)/shard_map/ppermute | solution.py:30
  25.7 2.3 %copy-start.12 = (bf16[512,512]{1,0:T(8,128)(2,1)S(1)}, bf16[512,512]{1,0:T(8,128)(2,1)}, u32[]{:S(2)}) copy-start(bf16[512,512]{1,0:T(8,128)(2,1)} %copy-done.11) | copy-start | bytes 1572868
  25.7 3.8 %collective-permute-start.1 = (f32[16,512]{1,0:T(8,128)S(1)}, f32[16,512]{1,0:T(8,128)S(1)}, u32[]{:S(2)}, u32[]{:S(2)}) collective-permute-start(f32[16,512]{1,0:T(8,128)S(1)} %convolution_add_fusion.7), channel_id=1, source_target_pairs={{1,65},{3,67},{5,69},{7,71},{9,73},{11,75},{13,77},{15,79},{17,81}... | collective-permute-start | bytes 98312 | tf_op jit(solution)/shard_map/ppermute | solution.py:30
  30.1 4.8 %collective-permute-start.3 = (f32[16,512]{1,0:T(8,128)S(1)}, f32[16,512]{1,0:T(8,128)S(1)}, u32[]{:S(2)}, u32[]{:S(2)}) collective-permute-start(f32[16,512]{1,0:T(8,128)S(1)} %convolution_add_fusion.6), channel_id=1, source_target_pairs={{65,129},{67,131},{69,133},{71,135},{73,137},{75,139},{77,141},{79... | collective-permute-start | bytes 98312 | tf_op jit(solution)/shard_map/ppermute | solution.py:30
  31.7 36.4 %collective-permute-start.12 = (bf16[4,128,640]{2,1,0:T(8,128)(2,1)}, bf16[4,128,640]{2,1,0:T(8,128)(2,1)S(1)}, u32[]{:S(2)}, u32[]{:S(2)}) collective-permute-start(bf16[4,128,640]{2,1,0:T(8,128)(2,1)} %pad_maximum_fusion), channel_id=1, source_target_pairs={{0,1},{2,3},{4,5},{6,7},{8,9},{10,11},{12,13},{14,15},{16,17},{18,... | collective-permute-start | bytes 1966088 | tf_op jit(solution)/shard_map/ppermute | solution.py:45
  33.0 17.7 %collective-permute-start.7 = (bf16[512,512]{1,0:T(8,128)(2,1)S(1)}, bf16[512,512]{1,0:T(8,128)(2,1)S(1)}, u32[]{:S(2)}, u32[]{:S(2)}) collective-permute-start(bf16[512,512]{1,0:T(8,128)(2,1)S(1)} %get-tuple-element.15), channel_id=1, source_target_pairs={{193,257},{195,259},{197,261},{199,263},{201,265},{203,267},{205,2... | collective-permute-start | bytes 1572872 | tf_op jit(solution)/shard_map/ppermute | solution.py:30
  35.5 1.2 %collective-permute-start.4 = (f32[16,512]{1,0:T(8,128)S(1)}, f32[16,512]{1,0:T(8,128)S(1)}, u32[]{:S(2)}, u32[]{:S(2)}) collective-permute-start(f32[16,512]{1,0:T(8,128)S(1)} %convolution_add_fusion.5), channel_id=1, source_target_pairs={{129,193},{131,195},{133,197},{135,199},{137,201},{139,203},{141,2... | collective-permute-start | bytes 98312 | tf_op jit(solution)/shard_map/ppermute | solution.py:30
  37.2 14.3 %collective-permute-start.6 = (f32[16,512]{1,0:T(8,128)S(1)}, f32[16,512]{1,0:T(8,128)S(1)}, u32[]{:S(2)}, u32[]{:S(2)}) collective-permute-start(f32[16,512]{1,0:T(8,128)S(1)} %fusion), channel_id=1, source_target_pairs={{129,257},{131,259},{133,261},{135,263},{137,265},{139,267},{141,2... | collective-permute-start | bytes 98312 | tf_op jit(solution)/shard_map/ppermute | solution.py:30
  51.5 15.8 %copy-start.16 = (s32[1,1,4]{2,1,0:T(1,128)S(1)}, s32[1,1,4]{2,1,0:T(1,128)}, u32[]{:S(2)}) copy-start(s32[1,1,4]{2,1,0:T(1,128)} %param.21) | copy-start | bytes 52
  52.1 8.6 %collective-permute-start.8 = (f32[16,512]{1,0:T(8,128)S(1)}, f32[16,512]{1,0:T(8,128)S(1)}, u32[]{:S(2)}, u32[]{:S(2)}) collective-permute-start(f32[16,512]{1,0:T(8,128)S(1)} %convolution_add_fusion.3), channel_id=1, source_target_pairs={{257,385},{259,387},{261,389},{263,391},{265,393},{267,395},{269,3... | collective-permute-start | bytes 98312 | tf_op jit(solution)/shard_map/ppermute | solution.py:30
  61.9 16.6 %all-to-all-start.1 = ((bf16[16,16,512]{2,1,0:T(8,128)(2,1)}), bf16[16,16,512]{2,1,0:T(8,128)(2,1)S(1)}, u32[]{:S(2)}, u32[]{:S(2)}) async-start(bf16[16,16,512]{2,1,0:T(8,128)(2,1)} %broadcast_in_dim.27), calls=%async_computation.1 | async-start | bytes 524288 | tf_op jit(solution)/shard_map/all_to_all | solution.py:24
  68.1 0.9 %copy-start.7 = (bf16[4,128,640]{2,1,0:T(8,128)(2,1)}, bf16[4,128,640]{2,1,0:T(8,128)(2,1)S(1)}, u32[]{:S(2)}) copy-start(bf16[4,128,640]{2,1,0:T(8,128)(2,1)S(1)} %collective-permute-done.12.returned) | copy-start | bytes 1966084
  68.9 0.9 %copy-start.2 = (bf16[128,640]{1,0:T(8,128)(2,1)S(1)}, bf16[128,640]{1,0:T(8,128)(2,1)}, u32[]{:S(2)}) copy-start(bf16[128,640]{1,0:T(8,128)(2,1)} %copy-done.1) | copy-start | bytes 491524
  69.9 0.9 %copy-start.4 = (bf16[128,640]{1,0:T(8,128)(2,1)S(1)}, bf16[128,640]{1,0:T(8,128)(2,1)}, u32[]{:S(2)}) copy-start(bf16[128,640]{1,0:T(8,128)(2,1)} %copy-done.3) | copy-start | bytes 491524
  70.8 1.4 %copy-start.5 = (bf16[1,1,1536,512]{3,2,1,0:T(8,128)(2,1)S(1)}, bf16[1,1,1536,512]{3,2,1,0:T(8,128)(2,1)}, u32[]{:S(2)}) copy-start(bf16[1,1,1536,512]{3,2,1,0:T(8,128)(2,1)} %param.20) | copy-start | bytes 4718596
  72.2 1.1 %copy-start.6 = (bf16[1,1,1536,256]{3,2,1,0:T(8,128)(2,1)S(1)}, bf16[1,1,1536,256]{3,2,1,0:T(8,128)(2,1)}, u32[]{:S(2)}) copy-start(bf16[1,1,1536,256]{3,2,1,0:T(8,128)(2,1)} %param.17) | copy-start | bytes 2359300
  73.3 1.1 %copy-start.8 = (bf16[4,128,640]{2,1,0:T(8,128)(2,1)S(1)}, bf16[4,128,640]{2,1,0:T(8,128)(2,1)}, u32[]{:S(2)}) copy-start(bf16[4,128,640]{2,1,0:T(8,128)(2,1)} %copy-done.7) | copy-start | bytes 1966084
  74.4 0.8 %copy-start.9 = (bf16[1,1,256,128]{3,2,1,0:T(8,128)(2,1)S(1)}, bf16[1,1,256,128]{3,2,1,0:T(8,128)(2,1)}, u32[]{:S(2)}) copy-start(bf16[1,1,256,128]{3,2,1,0:T(8,128)(2,1)} %param.18) | copy-start | bytes 196612

commit v3 on v2

--- a/solution.py
+++ b/solution.py
@@ -1,3 +1,5 @@
+import functools
+
 import jax
 import jax.numpy as jnp
 from jax import lax
@@ -8,13 +10,10 @@
 
 BF16 = jnp.bfloat16
 F32 = jnp.float32
-HALF = 8
+ROWS = 256
+LATE = 10
+LAST = 12
 PARTS = 2
-
-
-def split(value):
-    high = lax.reduce_precision(value, 8, 7)
-    return high.astype(BF16), (value - high).astype(BF16)
 
 
 def spread(piece, parts=1):
@@ -45,12 +44,46 @@
     return lax.ppermute(value, "sub", [(i, i + 1) for i in range(0, peers, 2)])
 
 
+def advance_kernel(first, last, left, right, product, *rounded):
+    steps = left.shape[0] // ROWS
+    if first:
+        group = lax.axis_index("grp")
+        used = (group >= first) & (group < last)
+
+        @pl.when(jnp.logical_not(used))
+        def _():
+            product[...] = jnp.zeros(product.shape, F32)
+
+        steps = jnp.where(used, steps, 0)
+
+    @pl.loop(0, steps)
+    def _(step):
+        rows = pl.ds(pl.multiple_of(step * ROWS, ROWS), ROWS)
+        whole = left[rows, :]
+        high = whole.astype(BF16)
+        low = (whole - high.astype(F32)).astype(BF16)
+        result = jnp.dot(high, right[...], preferred_element_type=F32)
+        result = result + jnp.dot(low, right[...], preferred_element_type=F32)
+        product[rows, :] = result
+        for out in rounded:
+            out[rows, :] = result.astype(BF16)
+
+
+def advance(left, right, copies, first, last):
+    vmem = pl.BlockSpec(memory_space=pltpu.VMEM)
+    return pl.pallas_call(
+        functools.partial(advance_kernel, first, last),
+        out_shape=[jax.ShapeDtypeStruct(left.shape, F32)] + [jax.ShapeDtypeStruct(left.shape, BF16)] * copies,
+        in_specs=[vmem] * 2,
+        out_specs=[vmem] * (1 + copies),
+        compiler_params=pltpu.CompilerParams(vmem_limit_bytes=8 << 20),
+        cost_estimate=pl.CostEstimate(flops=540_000_000, bytes_accessed=3_000_000, transcendentals=0),
+    )(left, right)
+
+
 def rows_times(value, left):
     dims = (((1,), (1,)), ((), ()))
     return lax.dot_general(value, left, dims, precision=lax.Precision.HIGH, preferred_element_type=F32)
-
-
-ROWS = 256
 
 
 def prepare_kernel(picks, mine, partner, before, after, returned, modes, basis, coeffs, weight, fixed, linked):
@@ -151,7 +184,7 @@
     chain = lax.axis_size("grp")
     place = lax.axis_index("sub")
     coupling = top_coupling[0]
-    high, low = split(coupling)
+    high = coupling.astype(BF16)
 
     basis = spread(top_basis[0]).reshape(-1, top_basis.shape[-1])
     back_1 = along_chain(high, 1, range(2, chain))
@@ -162,20 +195,25 @@
     own = lax.dot_general(coeffs, basis, (((1,), (1,)), ((), ())), preferred_element_type=F32)
 
     own_1 = along_chain(own, 1, range(1, chain))
-    two = jnp.dot(high, back_1, preferred_element_type=F32) + jnp.dot(low, back_1, preferred_element_type=F32)
-    two_high, two_low = split(two)
+    two, two_a, two_b = advance(coupling, back_1, 2, 0, chain)
     field = own + rows_times(own_1, coupling)
 
-    back_2 = along_chain(two_high, 2, range(HALF, chain))
-    late_2 = along_chain(field, 2, range(HALF, chain))
-    for first in range(2, HALF, 2):
+    back_2a = along_chain(two_a, 2, range(LATE, LAST))
+    back_2b = along_chain(two_b, 2, range(LAST, chain))
+    late_2a = along_chain(field, 2, range(LATE, LAST))
+    late_2b = along_chain(field, 2, range(LAST, chain))
+    for first in range(2, LATE - 2, 2):
         earlier = along_chain(field, 2, range(first, first + 2))
         field = field + rows_times(earlier, two)
-    field = field + rows_times(late_2, two)
-    four = jnp.dot(two_high, back_2, preferred_element_type=F32) + jnp.dot(two_low, back_2, preferred_element_type=F32)
-    for first in range(HALF, chain, 4):
-        earlier = along_chain(field, 4, range(first, first + 4))
-        field = field + rows_times(earlier, four)
+    earlier_4 = along_chain(field, 4, range(LATE, LAST))
+    earlier = along_chain(field, 2, range(LATE - 2, LATE))
+    late_a = lax.optimization_barrier(rows_times(late_2a, two))
+    (four_a,) = advance(two, back_2a, 0, LATE, LAST)
+    field = field + late_a + rows_times(earlier, two) + rows_times(earlier_4, four_a)
+    earlier = along_chain(field, 4, range(LAST, chain))
+    late_b = lax.optimization_barrier(rows_times(late_2b, two))
+    (four_b,) = advance(two, back_2b, 0, LAST, chain)
+    field = field + late_b + rows_times(earlier, four_b)
 
     pieces = spread(field.astype(BF16), PARTS)
 

time: 81.6 us -> 76.6 us (0.939)
  the two profiles are of different devices: /device:TPU:423 before, /device:TPU:483 now
where the time goes in v3:
time: 76.6 us; the launch traced here: 75.9 us
  starting transfers between devices  29.2 us (38%)
  waiting for transfers between devices  20.6 us (27%)
  local copies, waits for them, and re-layouts  9.41 us (12%)
  Pallas kernels  7.46 us (10%)
  matrix products  5.08 us (7%)
  other arithmetic  2.42 us (3%)
  between operations  1.75 us (2%)
    ppermute x12, waiting for transfers between devices, along_chain(): return lax.ppermute(value, ('grp', 'sub'), pairs)  18.4 us
    all_to_all x2, starting transfers between devices, spread(): lax.all_to_all(copies, 'sub', 0, 0, axis_index_groups=groups if parts > 1...  13.4 us
    ppermute x12, starting transfers between devices, along_chain(): return lax.ppermute(value, ('grp', 'sub'), pairs)  11.1 us
    unnamed x30, local copies, waits for them, and re-layouts  7.2 us
    dot_general x9, matrix products, rows_times(): lax.dot_general(value, left, dims, precision=lax.Precision.HIGH, preferre...  4.7 us
    pallas_call x1, Pallas kernels, prepare(): pl.pallas_call(prepare_kernel, out_shape=(jax.ShapeDtypeStruct((points, l...  3.26 us
    pallas_call x1, Pallas kernels, close(): pl.pallas_call(close_kernel, out_shape=(jax.ShapeDtypeStruct((length, mem...  2.32 us
    broadcast_in_dim x2, local copies, waits for them, and re-layouts, spread(): copies = jnp.broadcast_to(piece[None], (peers,) + piece.shape)  2.21 us
  transfers between devices with their start and end apart: 18, of which 4 were waited for; matrix products, arithmetic and copies ran while one was open for 11% of the time, Pallas kernels for 7%

profile of v3, /device:TPU:483, one launch (start us, length us, event | category | flops | bytes accessed | tf_op | source)
XLA Modules:
  0.0 75.9 jit_solution(8487061500872900296)
XLA Ops:
  0.7 1.5 %broadcast_in_dim.26 = bf16[32,16,256]{2,1,0:T(8,128)(2,1)} broadcast(bf16[16,256]{1,0:T(8,128)(2,1)} %bitcast.61), dimensions={1,2} | broadcast | bytes 270336 | tf_op jit(solution)/shard_map/broadcast_in_dim | solution.py:21
  2.1 7.9 %all-to-all-start = ((bf16[32,16,256]{2,1,0:T(8,128)(2,1)}), bf16[32,16,256]{2,1,0:T(8,128)(2,1)S(1)}, u32[]{:S(2)}, u32[]{:S(2)}) async-start(bf16[32,16,256]{2,1,0:T(8,128)(2,1)} %broadcast_in_dim.26), calls=%async_computation | async-start | bytes 524288 | tf_op jit(solution)/shard_map/all_to_all | solution.py:23
  10.1 2.2 %bitcast_convert_fusion = bf16[512,512]{1,0:T(8,128)(2,1)} fusion(f32[1,512,512]{2,1,0:T(8,128)} %param.13), kind=kLoop, calls=%fused_computation.19 | loop fusion | flops 262144 | bytes 1572864 | tf_op jit(solution)/shard_map/convert_element_type | solution.py:187
  12.2 1.3 %collective-permute-start.2 = (bf16[512,512]{1,0:T(8,128)(2,1)}, bf16[512,512]{1,0:T(8,128)(2,1)S(1)}, u32[]{:S(2)}, u32[]{:S(2)}) collective-permute-start(bf16[512,512]{1,0:T(8,128)(2,1)} %bitcast_convert_fusion), channel_id=1, source_target_pairs={{33,65},{35,67},{37,69},{39,71},{41,73},{43,75},{45,77},{47,79},{4... | collective-permute-start | bytes 1572872 | tf_op jit(solution)/shard_map/ppermute | solution.py:29
  13.6 0.1 fusion.9
  13.8 1.9 %collective-permute-start.12 = (bf16[128,640]{1,0:T(8,128)(2,1)S(1)}, bf16[128,640]{1,0:T(8,128)(2,1)S(1)}, u32[]{:S(2)}, u32[]{:S(2)}) collective-permute-start(bf16[128,640]{1,0:T(8,128)(2,1)S(1)} %get-tuple-element.20.mine), channel_id=1, source_target_pairs={{0,1},{1,0},{2,3},{3,2},{4,5},{5,4},{6,7},{7,6},{8,9},{9,8},{10,11... | collective-permute-start | bytes 491528 | tf_op jit(solution)/shard_map/ppermute | solution.py:34
  15.7 2.2 %all-to-all-done = bf16[32,16,256]{2,1,0:T(8,128)(2,1)S(1)} async-done(((bf16[32,16,256]{2,1,0:T(8,128)(2,1)}), bf16[32,16,256]{2,1,0:T(8,128)(2,1)S(1)}, u32[]{:S(2)}, u32[]{:S(2)}) %all-to-all-start) | async-done | bytes 262176 | tf_op jit(solution)/shard_map/all_to_all | solution.py:23
  17.9 0.2 fusion
  18.2 1.3 %collective-permute-start = (f32[16,512]{1,0:T(8,128)S(1)}, f32[16,512]{1,0:T(8,128)S(1)}, u32[]{:S(2)}, u32[]{:S(2)}) collective-permute-start(f32[16,512]{1,0:T(8,128)S(1)} %fusion), channel_id=1, source_target_pairs={{1,33},{3,35},{5,37},{7,39},{9,41},{11,43},{13,45},{15,47},{17,49}... | collective-permute-start | bytes 98312 | tf_op jit(solution)/shard_map/ppermute | solution.py:29
  19.5 0.7 collective-permute-start.13
  20.2 0.7 collective-permute-start.14
  20.9 1.9 %collective-permute-done = f32[16,512]{1,0:T(8,128)S(1)} collective-permute-done((f32[16,512]{1,0:T(8,128)S(1)}, f32[16,512]{1,0:T(8,128)S(1)}, u32[]{:S(2)}, u32[]{:S(2)}) %collective-permute-start) | collective-permute-done | bytes 32800 | tf_op jit(solution)/shard_map/ppermute | solution.py:29
  22.8 0.5 convolution_add_fusion.3
  23.3 0.7 collective-permute-start.1
  24.0 0.7 collective-permute-start.5
  24.7 1.3 %collective-permute-start.9 = (f32[16,512]{1,0:T(8,128)S(1)}, f32[16,512]{1,0:T(8,128)S(1)}, u32[]{:S(2)}, u32[]{:S(2)}) collective-permute-start(f32[16,512]{1,0:T(8,128)S(1)} %convolution_add_fusion.3), channel_id=1, source_target_pairs={{321,385},{323,387},{325,389},{327,391},{329,393},{331,395},{333,3... | collective-permute-start | bytes 98312 | tf_op jit(solution)/shard_map/ppermute | solution.py:29
  26.0 0.9 %shard_map.130 = (f32[512,512]{1,0:T(8,128)S(1)}, bf16[512,512]{1,0:T(8,128)(2,1)S(1)}, bf16[512,512]{1,0:T(8,128)(2,1)S(1)}) custom-call(f32[512,512]{1,0:T(8,128)S(1)} %bitcast.54, bf16[512,512]{1,0:T(8,128)(2,1)S(1)} %collective-permute-done.2.right), custom_call_target="tpu_custom_call" | custom-call | flops 540000000 | bytes 3000000 | tf_op jit(solution)/shard_map/pallas_call | solution.py:74
  26.9 0.5 convolution_add_fusion.2
  27.5 0.7 collective-permute-start.3
  28.2 1.3 %collective-permute-start.15 = (bf16[4,128,640]{2,1,0:T(8,128)(2,1)S(1)}, bf16[4,128,640]{2,1,0:T(8,128)(2,1)S(1)}, u32[]{:S(2)}, u32[]{:S(2)}) collective-permute-start(bf16[4,128,640]{2,1,0:T(8,128)(2,1)S(1)} %pad_maximum_fusion), channel_id=1, source_target_pairs={{0,1},{2,3},{4,5},{6,7},{8,9},{10,11},{12,13},{14,15},{16,17},{18,... | collective-permute-start | bytes 1966088 | tf_op jit(solution)/shard_map/ppermute | solution.py:44
  29.5 0.7 collective-permute-start.8
  30.2 0.5 convolution_add_fusion.1
  30.8 0.7 collective-permute-start.4
  31.5 0.5 fusion.10
  32.0 0.5 convolution_add_fusion
  32.5 0.7 collective-permute-start.6
  33.2 0.5 fusion.12
  33.7 1.3 %collective-permute-start.11 = (bf16[512,512]{1,0:T(8,128)(2,1)S(1)}, bf16[512,512]{1,0:T(8,128)(2,1)S(1)}, u32[]{:S(2)}, u32[]{:S(2)}) collective-permute-start(bf16[512,512]{1,0:T(8,128)(2,1)S(1)} %get-tuple-element.13), channel_id=1, source_target_pairs={{321,385},{323,387},{325,389},{327,391},{329,393},{331,395},{333,3... | collective-permute-start | bytes 1572872 | tf_op jit(solution)/shard_map/ppermute | solution.py:29
  35.0 0.7 collective-permute-start.7
  35.7 0.5 fusion.11
  36.2 0.1 shard_map.131
  36.3 0.5 add_add_fusion
  36.9 1.3 %collective-permute-start.10 = (f32[16,512]{1,0:T(8,128)S(1)}, f32[16,512]{1,0:T(8,128)S(1)}, u32[]{:S(2)}, u32[]{:S(2)}) collective-permute-start(f32[16,512]{1,0:T(8,128)S(1)} %add_add_fusion), channel_id=1, source_target_pairs={{257,385},{259,387},{261,389},{263,391},{265,393},{267,395},{269,3... | collective-permute-start | bytes 98312 | tf_op jit(solution)/shard_map/ppermute | solution.py:29
  38.2 12.6 %collective-permute-done.11.right = bf16[512,512]{1,0:T(8,128)(2,1)S(1)} collective-permute-done((bf16[512,512]{1,0:T(8,128)(2,1)S(1)}, bf16[512,512]{1,0:T(8,128)(2,1)S(1)}, u32[]{:S(2)}, u32[]{:S(2)}) %collective-permute-start.11) | collective-permute-done | bytes 524320 | tf_op jit(solution)/shard_map/ppermute | solution.py:29
  50.8 0.9 %shard_map.132 = f32[512,512]{1,0:T(8,128)S(1)} custom-call(f32[512,512]{1,0:T(8,128)S(1)} %get-tuple-element.11.left, bf16[512,512]{1,0:T(8,128)(2,1)S(1)} %collective-permute-done.11.right), custom_call_target="tpu_custom_call" | custom-call | flops 540000000 | bytes 3000000 | tf_op jit(solution)/shard_map/pallas_call | solution.py:74
  51.7 3.9 %collective-permute-done.10 = f32[16,512]{1,0:T(8,128)S(1)} collective-permute-done((f32[16,512]{1,0:T(8,128)S(1)}, f32[16,512]{1,0:T(8,128)S(1)}, u32[]{:S(2)}, u32[]{:S(2)}) %collective-permute-start.10) | collective-permute-done | bytes 32800 | tf_op jit(solution)/shard_map/ppermute | solution.py:29
  55.6 0.5 add_convert_fusion
  56.1 0.7 broadcast_in_dim.27
  56.9 5.5 %all-to-all-start.1 = ((bf16[16,16,512]{2,1,0:T(8,128)(2,1)}), bf16[16,16,512]{2,1,0:T(8,128)(2,1)S(1)}, u32[]{:S(2)}, u32[]{:S(2)}) async-start(bf16[16,16,512]{2,1,0:T(8,128)(2,1)} %broadcast_in_dim.27), calls=%async_computation.1 | async-start | bytes 524288 | tf_op jit(solution)/shard_map/all_to_all | solution.py:23
  63.1 0.9 %copy-done.8 = bf16[4,128,640]{2,1,0:T(8,128)(2,1)} copy-done((bf16[4,128,640]{2,1,0:T(8,128)(2,1)}, bf16[4,128,640]{2,1,0:T(8,128)(2,1)S(1)}, u32[]{:S(2)}) %copy-start.8) | copy-done | bytes 655384
  64.0 0.9 %copy-done.3 = bf16[128,640]{1,0:T(8,128)(2,1)S(1)} copy-done((bf16[128,640]{1,0:T(8,128)(2,1)S(1)}, bf16[128,640]{1,0:T(8,128)(2,1)}, u32[]{:S(2)}) %copy-start.3) | copy-done | bytes 163864
  64.9 0.9 %copy-done.5 = bf16[128,640]{1,0:T(8,128)(2,1)S(1)} copy-done((bf16[128,640]{1,0:T(8,128)(2,1)S(1)}, bf16[128,640]{1,0:T(8,128)(2,1)}, u32[]{:S(2)}) %copy-start.5) | copy-done | bytes 163864
  65.8 1.4 %copy-done.6 = bf16[1,1,1536,512]{3,2,1,0:T(8,128)(2,1)S(1)} copy-done((bf16[1,1,1536,512]{3,2,1,0:T(8,128)(2,1)S(1)}, bf16[1,1,1536,512]{3,2,1,0:T(8,128)(2,1)}, u32[]{:S(2)}) %copy-start.6) | copy-done | bytes 1572888
  67.2 1.1 %copy-done.7 = bf16[1,1,1536,256]{3,2,1,0:T(8,128)(2,1)S(1)} copy-done((bf16[1,1,1536,256]{3,2,1,0:T(8,128)(2,1)S(1)}, bf16[1,1,1536,256]{3,2,1,0:T(8,128)(2,1)}, u32[]{:S(2)}) %copy-start.7) | copy-done | bytes 786456
  68.4 1.1 %copy-done.9 = bf16[4,128,640]{2,1,0:T(8,128)(2,1)S(1)} copy-done((bf16[4,128,640]{2,1,0:T(8,128)(2,1)S(1)}, bf16[4,128,640]{2,1,0:T(8,128)(2,1)}, u32[]{:S(2)}) %copy-start.9) | copy-done | bytes 655384
  69.5 0.8 %copy-done.10 = bf16[1,1,256,128]{3,2,1,0:T(8,128)(2,1)S(1)} copy-done((bf16[1,1,256,128]{3,2,1,0:T(8,128)(2,1)S(1)}, bf16[1,1,256,128]{3,2,1,0:T(8,128)(2,1)}, u32[]{:S(2)}) %copy-start.10) | copy-done | bytes 65560
  70.3 3.3 %shard_map.133 = (bf16[1536,512]{1,0:T(8,128)(2,1)S(1)}, f32[1536,128]{1,0:T(8,128)S(1)}) custom-call(s32[6]{0:T(128)S(1)} %pad_add_fusion.picks, bf16[128,640]{1,0:T(8,128)(2,1)S(1)} %copy-done.5, bf16[128,640]{1,0:T(8,128)(2,1)S(1)} %copy-done.3, bf16[2,128,640]{2,1,0:T(8,128)(2,1)S(1)} %collective-permute-done.13.before, ...), custom_call_target="tpu_custom_call" | custom-call | flops 1200000000 | bytes 7000000 | tf_op jit(solution)/shard_map/pallas_call | solution.py:129
  73.6 2.3 %shard_map.134 = (f32[512,128]{1,0:T(8,128)}, bf16[128,128]{1,0:T(8,128)(2,1)}, bf16[1536,128]{1,0:T(8,128)(2,1)}) custom-call(bf16[8,2,16,512]{3,2,1,0:T(8,128)(2,1)S(1)} %bitcast.55, bf16[128,512]{1,0:T(8,128)(2,1)S(1)} %convert_bitcast_fusion.coupling, f32[128,128]{1,0:T(8,128)S(1)} %get-tuple-element.22.own, ...), custom_call_target="tpu_custom_call" | custom-call | flops 230000000 | bytes 4000000 | tf_op jit(solution)/shard_map/pallas_call | solution.py:157
  (43 shorter events, 0.4 us)
Async XLA Ops:
  0.6 17.3 %copy-start = (bf16[1,256,128]{2,1,0:T(8,128)(2,1)S(1)}, bf16[1,256,128]{2,1,0:T(8,128)(2,1)}, u32[]{:S(2)}) copy-start(bf16[1,256,128]{2,1,0:T(8,128)(2,1)} %param.12) | copy-start | bytes 196612
  0.6 12.9 %copy-start.11 = (f32[1,1,128,512]{3,2,1,0:T(8,128)S(1)}, f32[1,1,128,512]{3,2,1,0:T(8,128)}, u32[]{:S(2)}) copy-start(f32[1,1,128,512]{3,2,1,0:T(8,128)} %param.14) | copy-start | bytes 786436
  0.7 12.9 %copy-start.12 = (bf16[1,1,128,128]{3,2,1,0:T(8,128)(2,1)S(1)}, bf16[1,1,128,128]{3,2,1,0:T(8,128)(2,1)}, u32[]{:S(2)}) copy-start(bf16[1,1,128,128]{3,2,1,0:T(8,128)(2,1)} %param.16) | copy-start | bytes 98308
  0.7 12.9 %copy-start.13 = (bf16[1,1,128,128]{3,2,1,0:T(8,128)(2,1)S(1)}, bf16[1,1,128,128]{3,2,1,0:T(8,128)(2,1)}, u32[]{:S(2)}) copy-start(bf16[1,1,128,128]{3,2,1,0:T(8,128)(2,1)} %param.15) | copy-start | bytes 98308
  2.1 15.8 %all-to-all-start = ((bf16[32,16,256]{2,1,0:T(8,128)(2,1)}), bf16[32,16,256]{2,1,0:T(8,128)(2,1)S(1)}, u32[]{:S(2)}, u32[]{:S(2)}) async-start(bf16[32,16,256]{2,1,0:T(8,128)(2,1)} %broadcast_in_dim.26), calls=%async_computation | async-start | bytes 524288 | tf_op jit(solution)/shard_map/all_to_all | solution.py:23
  10.0 12.8 %copy-start.1 = (f32[1,512,512]{2,1,0:T(8,128)S(1)}, f32[1,512,512]{2,1,0:T(8,128)}, u32[]{:S(2)}) copy-start(f32[1,512,512]{2,1,0:T(8,128)} %param.13) | copy-start | bytes 3145732
  12.2 12.5 %collective-permute-start.2 = (bf16[512,512]{1,0:T(8,128)(2,1)}, bf16[512,512]{1,0:T(8,128)(2,1)S(1)}, u32[]{:S(2)}, u32[]{:S(2)}) collective-permute-start(bf16[512,512]{1,0:T(8,128)(2,1)} %bitcast_convert_fusion), channel_id=1, source_target_pairs={{33,65},{35,67},{37,69},{39,71},{41,73},{43,75},{45,77},{47,79},{4... | collective-permute-start | bytes 1572872 | tf_op jit(solution)/shard_map/ppermute | solution.py:29
  13.7 13.2 %copy-start.4 = (bf16[128,640]{1,0:T(8,128)(2,1)}, bf16[128,640]{1,0:T(8,128)(2,1)S(1)}, u32[]{:S(2)}) copy-start(bf16[128,640]{1,0:T(8,128)(2,1)S(1)} %get-tuple-element.20.mine) | copy-start | bytes 491524
  13.8 5.7 %collective-permute-start.12 = (bf16[128,640]{1,0:T(8,128)(2,1)S(1)}, bf16[128,640]{1,0:T(8,128)(2,1)S(1)}, u32[]{:S(2)}, u32[]{:S(2)}) collective-permute-start(bf16[128,640]{1,0:T(8,128)(2,1)S(1)} %get-tuple-element.20.mine), channel_id=1, source_target_pairs={{0,1},{1,0},{2,3},{3,2},{4,5},{5,4},{6,7},{7,6},{8,9},{9,8},{10,11... | collective-permute-start | bytes 491528 | tf_op jit(solution)/shard_map/ppermute | solution.py:34
  18.2 4.7 %collective-permute-start = (f32[16,512]{1,0:T(8,128)S(1)}, f32[16,512]{1,0:T(8,128)S(1)}, u32[]{:S(2)}, u32[]{:S(2)}) collective-permute-start(f32[16,512]{1,0:T(8,128)S(1)} %fusion), channel_id=1, source_target_pairs={{1,33},{3,35},{5,37},{7,39},{9,41},{11,43},{13,45},{15,47},{17,49}... | collective-permute-start | bytes 98312 | tf_op jit(solution)/shard_map/ppermute | solution.py:29
  19.5 7.5 %copy-start.2 = (bf16[128,640]{1,0:T(8,128)(2,1)}, bf16[128,640]{1,0:T(8,128)(2,1)S(1)}, u32[]{:S(2)}) copy-start(bf16[128,640]{1,0:T(8,128)(2,1)S(1)} %collective-permute-done.12.partner) | copy-start | bytes 491524
  19.5 8.6 %collective-permute-start.13 = (bf16[2,128,640]{2,1,0:T(8,128)(2,1)S(1)}, bf16[2,128,640]{2,1,0:T(8,128)(2,1)S(1)}, u32[]{:S(2)}, u32[]{:S(2)}) collective-permute-start(bf16[2,128,640]{2,1,0:T(8,128)(2,1)S(1)} %pad_maximum_fusion.1), channel_id=1, source_target_pairs={{0,2},{2,4},{4,6},{6,8},{8,10},{10,12},{12,14},{14,16},{16,18},{18... | collective-permute-start | bytes 983048 | tf_op jit(solution)/shard_map/ppermute | solution.py:39
  20.2 7.9 %collective-permute-start.14 = (bf16[2,128,640]{2,1,0:T(8,128)(2,1)S(1)}, bf16[2,128,640]{2,1,0:T(8,128)(2,1)S(1)}, u32[]{:S(2)}, u32[]{:S(2)}) collective-permute-start(bf16[2,128,640]{2,1,0:T(8,128)(2,1)S(1)} %pad_maximum_fusion.1), channel_id=1, source_target_pairs={{0,30},{2,0},{4,2},{6,4},{8,6},{10,8},{12,10},{14,12},{16,14},{18,... | collective-permute-start | bytes 983048 | tf_op jit(solution)/shard_map/ppermute | solution.py:39
  23.3 3.6 %collective-permute-start.1 = (f32[16,512]{1,0:T(8,128)S(1)}, f32[16,512]{1,0:T(8,128)S(1)}, u32[]{:S(2)}, u32[]{:S(2)}) collective-permute-start(f32[16,512]{1,0:T(8,128)S(1)} %convolution_add_fusion.3), channel_id=1, source_target_pairs={{1,65},{3,67},{5,69},{7,71},{9,73},{11,75},{13,77},{15,79},{17,81}... | collective-permute-start | bytes 98312 | tf_op jit(solution)/shard_map/ppermute | solution.py:29
  24.0 7.4 %collective-permute-start.5 = (f32[16,512]{1,0:T(8,128)S(1)}, f32[16,512]{1,0:T(8,128)S(1)}, u32[]{:S(2)}, u32[]{:S(2)}) collective-permute-start(f32[16,512]{1,0:T(8,128)S(1)} %convolution_add_fusion.3), channel_id=1, source_target_pairs={{257,321},{259,323},{261,325},{263,327},{265,329},{267,331},{269,3... | collective-permute-start | bytes 98312 | tf_op jit(solution)/shard_map/ppermute | solution.py:29
  24.7 8.5 %collective-permute-start.9 = (f32[16,512]{1,0:T(8,128)S(1)}, f32[16,512]{1,0:T(8,128)S(1)}, u32[]{:S(2)}, u32[]{:S(2)}) collective-permute-start(f32[16,512]{1,0:T(8,128)S(1)} %convolution_add_fusion.3), channel_id=1, source_target_pairs={{321,385},{323,387},{325,389},{327,391},{329,393},{331,395},{333,3... | collective-permute-start | bytes 98312 | tf_op jit(solution)/shard_map/ppermute | solution.py:29
  27.5 2.8 %collective-permute-start.3 = (f32[16,512]{1,0:T(8,128)S(1)}, f32[16,512]{1,0:T(8,128)S(1)}, u32[]{:S(2)}, u32[]{:S(2)}) collective-permute-start(f32[16,512]{1,0:T(8,128)S(1)} %convolution_add_fusion.2), channel_id=1, source_target_pairs={{65,129},{67,131},{69,133},{71,135},{73,137},{75,139},{77,141},{79... | collective-permute-start | bytes 98312 | tf_op jit(solution)/shard_map/ppermute | solution.py:29
  28.2 34.9 %collective-permute-start.15 = (bf16[4,128,640]{2,1,0:T(8,128)(2,1)S(1)}, bf16[4,128,640]{2,1,0:T(8,128)(2,1)S(1)}, u32[]{:S(2)}, u32[]{:S(2)}) collective-permute-start(bf16[4,128,640]{2,1,0:T(8,128)(2,1)S(1)} %pad_maximum_fusion), channel_id=1, source_target_pairs={{0,1},{2,3},{4,5},{6,7},{8,9},{10,11},{12,13},{14,15},{16,17},{18,... | collective-permute-start | bytes 1966088 | tf_op jit(solution)/shard_map/ppermute | solution.py:44
  29.5 6.7 %collective-permute-start.8 = (bf16[512,512]{1,0:T(8,128)(2,1)S(1)}, bf16[512,512]{1,0:T(8,128)(2,1)S(1)}, u32[]{:S(2)}, u32[]{:S(2)}) collective-permute-start(bf16[512,512]{1,0:T(8,128)(2,1)S(1)} %get-tuple-element.12), channel_id=1, source_target_pairs={{257,321},{259,323},{261,325},{263,327},{265,329},{267,331},{269,3... | collective-permute-start | bytes 1572872 | tf_op jit(solution)/shard_map/ppermute | solution.py:29
  30.8 1.2 %collective-permute-start.4 = (f32[16,512]{1,0:T(8,128)S(1)}, f32[16,512]{1,0:T(8,128)S(1)}, u32[]{:S(2)}, u32[]{:S(2)}) collective-permute-start(f32[16,512]{1,0:T(8,128)S(1)} %convolution_add_fusion.1), channel_id=1, source_target_pairs={{129,193},{131,195},{133,197},{135,199},{137,201},{139,203},{141,2... | collective-permute-start | bytes 98312 | tf_op jit(solution)/shard_map/ppermute | solution.py:29
  32.5 3.2 %collective-permute-start.6 = (f32[16,512]{1,0:T(8,128)S(1)}, f32[16,512]{1,0:T(8,128)S(1)}, u32[]{:S(2)}, u32[]{:S(2)}) collective-permute-start(f32[16,512]{1,0:T(8,128)S(1)} %convolution_add_fusion), channel_id=1, source_target_pairs={{193,257},{195,259},{197,261},{199,263},{201,265},{203,267},{205,2... | collective-permute-start | bytes 98312 | tf_op jit(solution)/shard_map/ppermute | solution.py:29
  33.7 17.1 %collective-permute-start.11 = (bf16[512,512]{1,0:T(8,128)(2,1)S(1)}, bf16[512,512]{1,0:T(8,128)(2,1)S(1)}, u32[]{:S(2)}, u32[]{:S(2)}) collective-permute-start(bf16[512,512]{1,0:T(8,128)(2,1)S(1)} %get-tuple-element.13), channel_id=1, source_target_pairs={{321,385},{323,387},{325,389},{327,391},{329,393},{331,395},{333,3... | collective-permute-start | bytes 1572872 | tf_op jit(solution)/shard_map/ppermute | solution.py:29
  35.0 1.3 %collective-permute-start.7 = (f32[16,512]{1,0:T(8,128)S(1)}, f32[16,512]{1,0:T(8,128)S(1)}, u32[]{:S(2)}, u32[]{:S(2)}) collective-permute-start(f32[16,512]{1,0:T(8,128)S(1)} %convolution_add_fusion), channel_id=1, source_target_pairs={{193,321},{195,323},{197,325},{199,327},{201,329},{203,331},{205,3... | collective-permute-start | bytes 98312 | tf_op jit(solution)/shard_map/ppermute | solution.py:29
  36.9 18.7 %collective-permute-start.10 = (f32[16,512]{1,0:T(8,128)S(1)}, f32[16,512]{1,0:T(8,128)S(1)}, u32[]{:S(2)}, u32[]{:S(2)}) collective-permute-start(f32[16,512]{1,0:T(8,128)S(1)} %add_add_fusion), channel_id=1, source_target_pairs={{257,385},{259,387},{261,389},{263,391},{265,393},{267,395},{269,3... | collective-permute-start | bytes 98312 | tf_op jit(solution)/shard_map/ppermute | solution.py:29
  51.7 10.7 %copy-start.14 = (s32[1,1,4]{2,1,0:T(1,128)S(1)}, s32[1,1,4]{2,1,0:T(1,128)}, u32[]{:S(2)}) copy-start(s32[1,1,4]{2,1,0:T(1,128)} %param.21) | copy-start | bytes 52
  56.9 16.7 %all-to-all-start.1 = ((bf16[16,16,512]{2,1,0:T(8,128)(2,1)}), bf16[16,16,512]{2,1,0:T(8,128)(2,1)S(1)}, u32[]{:S(2)}, u32[]{:S(2)}) async-start(bf16[16,16,512]{2,1,0:T(8,128)(2,1)} %broadcast_in_dim.27), calls=%async_computation.1 | async-start | bytes 524288 | tf_op jit(solution)/shard_map/all_to_all | solution.py:23
  63.1 0.9 %copy-start.8 = (bf16[4,128,640]{2,1,0:T(8,128)(2,1)}, bf16[4,128,640]{2,1,0:T(8,128)(2,1)S(1)}, u32[]{:S(2)}) copy-start(bf16[4,128,640]{2,1,0:T(8,128)(2,1)S(1)} %collective-permute-done.15.returned) | copy-start | bytes 1966084
  64.0 0.9 %copy-start.3 = (bf16[128,640]{1,0:T(8,128)(2,1)S(1)}, bf16[128,640]{1,0:T(8,128)(2,1)}, u32[]{:S(2)}) copy-start(bf16[128,640]{1,0:T(8,128)(2,1)} %copy-done.2) | copy-start | bytes 491524
  64.9 0.9 %copy-start.5 = (bf16[128,640]{1,0:T(8,128)(2,1)S(1)}, bf16[128,640]{1,0:T(8,128)(2,1)}, u32[]{:S(2)}) copy-start(bf16[128,640]{1,0:T(8,128)(2,1)} %copy-done.4) | copy-start | bytes 491524
  65.8 1.4 %copy-start.6 = (bf16[1,1,1536,512]{3,2,1,0:T(8,128)(2,1)S(1)}, bf16[1,1,1536,512]{3,2,1,0:T(8,128)(2,1)}, u32[]{:S(2)}) copy-start(bf16[1,1,1536,512]{3,2,1,0:T(8,128)(2,1)} %param.20) | copy-start | bytes 4718596
  67.2 1.1 %copy-start.7 = (bf16[1,1,1536,256]{3,2,1,0:T(8,128)(2,1)S(1)}, bf16[1,1,1536,256]{3,2,1,0:T(8,128)(2,1)}, u32[]{:S(2)}) copy-start(bf16[1,1,1536,256]{3,2,1,0:T(8,128)(2,1)} %param.17) | copy-start | bytes 2359300
  68.4 1.1 %copy-start.9 = (bf16[4,128,640]{2,1,0:T(8,128)(2,1)S(1)}, bf16[4,128,640]{2,1,0:T(8,128)(2,1)}, u32[]{:S(2)}) copy-start(bf16[4,128,640]{2,1,0:T(8,128)(2,1)} %copy-done.8) | copy-start | bytes 1966084
  69.5 0.8 %copy-start.10 = (bf16[1,1,256,128]{3,2,1,0:T(8,128)(2,1)S(1)}, bf16[1,1,256,128]{3,2,1,0:T(8,128)(2,1)}, u32[]{:S(2)}) copy-start(bf16[1,1,256,128]{3,2,1,0:T(8,128)(2,1)} %param.18) | copy-start | bytes 196612

commit v4 on v3

--- a/solution.py
+++ b/solution.py
@@ -42,6 +42,44 @@
 def even_to_odd(value):
     peers = lax.axis_size("sub")
     return lax.ppermute(value, "sub", [(i, i + 1) for i in range(0, peers, 2)])
+
+
+def in_groups(first, last):
+    group = lax.axis_index("grp")
+    return (group >= first) & (group < last)
+
+
+def step_kernel(first, last, base, value, left, out):
+    used = in_groups(first, last)
+    dims = (((1,), (1,)), ((), ()))
+
+    @pl.when(used)
+    def _():
+        whole = value[...]
+        count = whole.shape[0]
+        top = whole.astype(BF16)
+        both = jnp.concatenate([top, (whole - top.astype(F32)).astype(BF16)])
+        high = left[...].astype(BF16)
+        low = (left[...] - high.astype(F32)).astype(BF16)
+        far = lax.dot_general(both, high, dims, preferred_element_type=F32)
+        near = lax.dot_general(top, low, dims, preferred_element_type=F32)
+        out[...] = base[...] + far[:count] + far[count:] + near
+
+    @pl.when(jnp.logical_not(used))
+    def _():
+        out[...] = base[...]
+
+
+def add_step(base, value, left, first, last):
+    vmem = pl.BlockSpec(memory_space=pltpu.VMEM)
+    return pl.pallas_call(
+        functools.partial(step_kernel, first, last),
+        out_shape=jax.ShapeDtypeStruct(base.shape, F32),
+        in_specs=[vmem] * 3,
+        out_specs=vmem,
+        compiler_params=pltpu.CompilerParams(vmem_limit_bytes=8 << 20),
+        cost_estimate=pl.CostEstimate(flops=25_000_000, bytes_accessed=1_200_000, transcendentals=0),
+    )(base, value, left)
 
 
 def advance_kernel(first, last, left, right, product, *rounded):
@@ -137,18 +175,25 @@
     )(picks, mine, partner, before, after, returned, modes, basis, coeffs)
 
 
-def close_kernel(pieces, coupling, own, weight, fixed, top, block, interior):
+def close_kernel(pieces, coupling, own, weight, fixed, top_hbm, block_hbm, interior_hbm, top, block, interior, done):
     chips, _, columns, length = pieces.shape
     field = pieces[:, 1].reshape(chips * columns, length).astype(F32).T
     top[...] = field
+    stores = [pltpu.make_async_copy(top, top_hbm, done.at[0])]
+    stores[0].start()
     rounded = field.astype(BF16)
-    block[...] = (own[...] + jnp.dot(coupling[...], rounded, preferred_element_type=F32)).astype(BF16)
-
-    @pl.loop(0, weight.shape[0] // ROWS)
-    def _(step):
-        rows = pl.ds(pl.multiple_of(step * ROWS, ROWS), ROWS)
+    steps = weight.shape[0] // ROWS
+    for step in range(steps):
+        rows = pl.ds(step * ROWS, ROWS)
         part = jnp.dot(weight[rows, :], rounded, preferred_element_type=F32)
         interior[rows, :] = (fixed[rows, :] + part).astype(BF16)
+        stores.append(pltpu.make_async_copy(interior.at[rows, :], interior_hbm.at[rows, :], done.at[2 + step]))
+        stores[-1].start()
+    block[...] = (own[...] + jnp.dot(coupling[...], rounded, preferred_element_type=F32)).astype(BF16)
+    stores.append(pltpu.make_async_copy(block, block_hbm, done.at[1]))
+    stores[-1].start()
+    for store in stores:
+        store.wait()
 
 
 def close(pieces, coupling, own_block, weight, fixed):
@@ -162,7 +207,13 @@
             jax.ShapeDtypeStruct(fixed.shape, BF16),
         ),
         in_specs=[vmem] * 5,
-        out_specs=(vmem, vmem, vmem),
+        out_specs=[pl.BlockSpec(memory_space=pl.ANY)] * 3,
+        scratch_shapes=[
+            pltpu.VMEM((length, members // 2 * columns), F32),
+            pltpu.VMEM(own_block.shape, BF16),
+            pltpu.VMEM(fixed.shape, BF16),
+            pltpu.SemaphoreType.DMA((2 + fixed.shape[0] // ROWS,)),
+        ],
         compiler_params=pltpu.CompilerParams(vmem_limit_bytes=24 << 20),
         cost_estimate=pl.CostEstimate(flops=230_000_000, bytes_accessed=4_000_000, transcendentals=0),
     )(pieces.reshape(members // 2, 2, columns, length), coupling, own_block, weight, fixed)
@@ -204,16 +255,17 @@
     late_2b = along_chain(field, 2, range(LAST, chain))
     for first in range(2, LATE - 2, 2):
         earlier = along_chain(field, 2, range(first, first + 2))
-        field = field + rows_times(earlier, two)
+        field = add_step(field, earlier, two, first, first + 2)
     earlier_4 = along_chain(field, 4, range(LATE, LAST))
     earlier = along_chain(field, 2, range(LATE - 2, LATE))
-    late_a = lax.optimization_barrier(rows_times(late_2a, two))
+    field = add_step(field, late_2a, two, LATE, LAST)
     (four_a,) = advance(two, back_2a, 0, LATE, LAST)
-    field = field + late_a + rows_times(earlier, two) + rows_times(earlier_4, four_a)
+    field = add_step(field, earlier, two, LATE - 2, LATE)
+    field = add_step(field, earlier_4, four_a, LATE, LAST)
     earlier = along_chain(field, 4, range(LAST, chain))
-    late_b = lax.optimization_barrier(rows_times(late_2b, two))
+    field = add_step(field, late_2b, two, LAST, chain)
     (four_b,) = advance(two, back_2b, 0, LAST, chain)
-    field = field + late_b + rows_times(earlier, four_b)
+    field = add_step(field, earlier, four_b, LAST, chain)
 
     pieces = spread(field.astype(BF16), PARTS)
 

time: 76.6 us -> 78.9 us (1.030)
  the two profiles are of different devices: /device:TPU:483 before, /device:TPU:455 now
where the time goes in v4:
time: 78.9 us; the launch traced here: 78.2 us
  starting transfers between devices  32.5 us (41%)
  waiting for transfers between devices  24 us (30%)
  Pallas kernels  8.99 us (11%)
  local copies, waits for them, and re-layouts  4.83 us (6%)
  other arithmetic  4.27 us (5%)
  matrix products  1.84 us (2%)
  between operations  1.77 us (2%)
    ppermute x12, waiting for transfers between devices, along_chain(): return lax.ppermute(value, ('grp', 'sub'), pairs)  23.6 us
    ppermute x12, starting transfers between devices, along_chain(): return lax.ppermute(value, ('grp', 'sub'), pairs)  13.2 us
    all_to_all x2, starting transfers between devices, spread(): lax.all_to_all(copies, 'sub', 0, 0, axis_index_groups=groups if parts > 1...  13.2 us
    pallas_call x1, Pallas kernels, prepare(): pl.pallas_call(prepare_kernel, out_shape=(jax.ShapeDtypeStruct((points, l...  4 us
    unnamed x30, local copies, waits for them, and re-layouts  3.38 us
    ppermute x2, starting transfers between devices, even_along_loop(): lax.ppermute(value, 'sub', [(i, (i + by) % peers) for i in range(0, peers...  2.78 us
    pallas_call x3, Pallas kernels, advance(): pl.pallas_call(functools.partial(advance_kernel, first, last), out_shape=...  2.71 us
    concatenate x1, other arithmetic, body(): both = jnp.concatenate([before, after])  2.01 us
  transfers between devices with their start and end apart: 18, of which 3 were waited for; matrix products, arithmetic and copies ran while one was open for 8% of the time, Pallas kernels for 10%

profile of v4, /device:TPU:455, one launch (start us, length us, event | category | flops | bytes accessed | tf_op | source)
XLA Modules:
  0.0 78.2 jit_solution(11037190565668578129)
XLA Ops:
  0.6 0.0 copy-start
  0.7 1.3 %bitcast_convert_fusion = bf16[512,512]{1,0:T(8,128)(2,1)S(1)} fusion(f32[1,512,512]{2,1,0:T(8,128)} %param.13), kind=kLoop, calls=%fused_computation.14 | loop fusion | flops 262144 | bytes 1572864 | tf_op jit(solution)/shard_map/convert_element_type | solution.py:238
  2.0 0.0 copy-start.1
  2.0 2.8 %collective-permute-start.2 = (bf16[512,512]{1,0:T(8,128)(2,1)S(1)}, bf16[512,512]{1,0:T(8,128)(2,1)S(1)}, u32[]{:S(2)}, u32[]{:S(2)}) collective-permute-start(bf16[512,512]{1,0:T(8,128)(2,1)S(1)} %bitcast_convert_fusion), channel_id=1, source_target_pairs={{33,65},{35,67},{37,69},{39,71},{41,73},{43,75},{45,77},{47,79},{4... | collective-permute-start | bytes 1572872 | tf_op jit(solution)/shard_map/ppermute | solution.py:29
  4.9 0.1 fusion.9
  5.1 1.9 %collective-permute-start.12 = (bf16[128,640]{1,0:T(8,128)(2,1)S(1)}, bf16[128,640]{1,0:T(8,128)(2,1)S(1)}, u32[]{:S(2)}, u32[]{:S(2)}) collective-permute-start(bf16[128,640]{1,0:T(8,128)(2,1)S(1)} %get-tuple-element.20.mine), channel_id=1, source_target_pairs={{0,1},{1,0},{2,3},{3,2},{4,5},{5,4},{6,7},{7,6},{8,9},{9,8},{10,11... | collective-permute-start | bytes 491528 | tf_op jit(solution)/shard_map/ppermute | solution.py:34
  7.0 0.7 broadcast_in_dim.26
  7.7 7.8 %all-to-all-start = ((bf16[32,16,256]{2,1,0:T(8,128)(2,1)}), bf16[32,16,256]{2,1,0:T(8,128)(2,1)}, u32[]{:S(2)}, u32[]{:S(2)}) async-start(bf16[32,16,256]{2,1,0:T(8,128)(2,1)} %broadcast_in_dim.26), calls=%async_computation | async-start | bytes 524288 | tf_op jit(solution)/shard_map/all_to_all | solution.py:23
  15.5 0.8 pad_maximum_fusion.1
  16.3 1.4 %collective-permute-start.13 = (bf16[2,128,640]{2,1,0:T(8,128)(2,1)}, bf16[2,128,640]{2,1,0:T(8,128)(2,1)}, u32[]{:S(2)}, u32[]{:S(2)}) collective-permute-start(bf16[2,128,640]{2,1,0:T(8,128)(2,1)} %pad_maximum_fusion.1), channel_id=1, source_target_pairs={{0,2},{2,4},{4,6},{6,8},{8,10},{10,12},{12,14},{14,16},{16,18},{18... | collective-permute-start | bytes 983048 | tf_op jit(solution)/shard_map/ppermute | solution.py:39
  17.7 1.4 %collective-permute-start.14 = (bf16[2,128,640]{2,1,0:T(8,128)(2,1)}, bf16[2,128,640]{2,1,0:T(8,128)(2,1)}, u32[]{:S(2)}, u32[]{:S(2)}) collective-permute-start(bf16[2,128,640]{2,1,0:T(8,128)(2,1)} %pad_maximum_fusion.1), channel_id=1, source_target_pairs={{0,30},{2,0},{4,2},{6,4},{8,6},{10,8},{12,10},{14,12},{16,14},{18,... | collective-permute-start | bytes 983048 | tf_op jit(solution)/shard_map/ppermute | solution.py:39
  19.1 0.0 collective-permute-done.2.right
  19.1 1.7 %shard_map.130 = (f32[512,512]{1,0:T(8,128)S(1)}, bf16[512,512]{1,0:T(8,128)(2,1)}, bf16[512,512]{1,0:T(8,128)(2,1)S(1)}) custom-call(f32[512,512]{1,0:T(8,128)S(1)} %bitcast.38, bf16[512,512]{1,0:T(8,128)(2,1)S(1)} %collective-permute-done.2.right), custom_call_target="tpu_custom_call" | custom-call | flops 540000000 | bytes 3000000 | tf_op jit(solution)/shard_map/pallas_call | solution.py:112
  20.8 0.8 copy-done.8
  21.6 0.7 collective-permute-start.8
  22.3 0.4 all-to-all-done
  22.7 1.2 %fusion = f32[16,512]{1,0:T(8,128)S(1)} fusion(bf16[512,256]{1,0:T(8,128)(2,1)} %bitcast.2, bf16[1,256,128]{2,1,0:T(8,128)(2,1)S(1)} %copy-done, s32[]{:T(128)S(6)} %select_n.20), kind=kOutput, calls=%fused_computation.5 | convolution fusion | flops 4194304 | bytes 360452 | tf_op jit(solution)/shard_map/dot_general | solution.py:246
  23.9 1.9 %collective-permute-start = (f32[16,512]{1,0:T(8,128)S(1)}, f32[16,512]{1,0:T(8,128)S(1)}, u32[]{:S(2)}, u32[]{:S(2)}) collective-permute-start(f32[16,512]{1,0:T(8,128)S(1)} %fusion), channel_id=1, source_target_pairs={{1,33},{3,35},{5,37},{7,39},{9,41},{11,43},{13,45},{15,47},{17,49}... | collective-permute-start | bytes 98312 | tf_op jit(solution)/shard_map/ppermute | solution.py:29
  25.8 1.3 %collective-permute-start.11 = (bf16[512,512]{1,0:T(8,128)(2,1)}, bf16[512,512]{1,0:T(8,128)(2,1)S(1)}, u32[]{:S(2)}, u32[]{:S(2)}) collective-permute-start(bf16[512,512]{1,0:T(8,128)(2,1)} %copy-done.8), channel_id=1, source_target_pairs={{321,385},{323,387},{325,389},{327,391},{329,393},{331,395},{333,3... | collective-permute-start | bytes 1572872 | tf_op jit(solution)/shard_map/ppermute | solution.py:29
  27.1 0.0 collective-permute-done.14.after
  27.1 2.0 %pad_maximum_fusion = bf16[4,128,640]{2,1,0:T(8,128)(2,1)} fusion(bf16[2,128,640]{2,1,0:T(8,128)(2,1)} %collective-permute-done.14.after, bf16[2,128,640]{2,1,0:T(8,128)(2,1)} %collective-permute-done.13.before), kind=kLoop, calls=%fused_computation.1 | loop fusion | flops 327680 | bytes 1310720 | tf_op jit(solution)/shard_map/concatenate | solution.py:279
  29.1 1.3 %collective-permute-start.15 = (bf16[4,128,640]{2,1,0:T(8,128)(2,1)}, bf16[4,128,640]{2,1,0:T(8,128)(2,1)}, u32[]{:S(2)}, u32[]{:S(2)}) collective-permute-start(bf16[4,128,640]{2,1,0:T(8,128)(2,1)} %pad_maximum_fusion), channel_id=1, source_target_pairs={{0,1},{2,3},{4,5},{6,7},{8,9},{10,11},{12,13},{14,15},{16,17},{18,... | collective-permute-start | bytes 1966088 | tf_op jit(solution)/shard_map/ppermute | solution.py:44
  30.4 0.0 collective-permute-done
  30.4 0.5 convolution_add_fusion.base
  31.0 0.7 collective-permute-start.1
  31.7 0.7 collective-permute-start.3
  32.4 0.7 collective-permute-start.4
  33.1 0.7 collective-permute-start.5
  33.8 0.7 collective-permute-start.6
  34.5 1.3 %collective-permute-start.9 = (f32[16,512]{1,0:T(8,128)S(1)}, f32[16,512]{1,0:T(8,128)S(1)}, u32[]{:S(2)}, u32[]{:S(2)}) collective-permute-start(f32[16,512]{1,0:T(8,128)S(1)} %convolution_add_fusion.base), channel_id=1, source_target_pairs={{321,385},{323,387},{325,389},{327,391},{329,393},{331,395},{333,3... | collective-permute-start | bytes 98312 | tf_op jit(solution)/shard_map/ppermute | solution.py:29
  35.8 0.7 collective-permute-start.7
  36.5 0.1 shard_map.136.left
  36.6 1.3 %collective-permute-start.10 = (f32[16,512]{1,0:T(8,128)S(1)}, f32[16,512]{1,0:T(8,128)S(1)}, u32[]{:S(2)}, u32[]{:S(2)}) collective-permute-start(f32[16,512]{1,0:T(8,128)S(1)} %shard_map.137.base), channel_id=1, source_target_pairs={{257,385},{259,387},{261,389},{263,391},{265,393},{267,395},{269,3... | collective-permute-start | bytes 98312 | tf_op jit(solution)/shard_map/ppermute | solution.py:29
  37.9 5.0 %collective-permute-done.9.value = f32[16,512]{1,0:T(8,128)S(1)} collective-permute-done((f32[16,512]{1,0:T(8,128)S(1)}, f32[16,512]{1,0:T(8,128)S(1)}, u32[]{:S(2)}, u32[]{:S(2)}) %collective-permute-start.9) | collective-permute-done | bytes 32800 | tf_op jit(solution)/shard_map/ppermute | solution.py:29
  42.9 0.4 shard_map.138.base
  43.3 0.9 %shard_map.139.left = f32[512,512]{1,0:T(8,128)S(1)} custom-call(f32[512,512]{1,0:T(8,128)S(1)} %get-tuple-element.11.left, bf16[512,512]{1,0:T(8,128)(2,1)S(1)} %collective-permute-done.11.right), custom_call_target="tpu_custom_call" | custom-call | flops 540000000 | bytes 3000000 | tf_op jit(solution)/shard_map/pallas_call | solution.py:112
  44.2 0.0 copy-start.14
  44.2 0.0 copy-start.9
  44.3 18.6 %collective-permute-done.10.value = f32[16,512]{1,0:T(8,128)S(1)} collective-permute-done((f32[16,512]{1,0:T(8,128)S(1)}, f32[16,512]{1,0:T(8,128)S(1)}, u32[]{:S(2)}, u32[]{:S(2)}) %collective-permute-start.10) | collective-permute-done | bytes 32800 | tf_op jit(solution)/shard_map/ppermute | solution.py:29
  62.9 0.4 shard_map.140
  63.3 0.7 broadcast_in_dim.27
  64.0 5.5 %all-to-all-start.1 = ((bf16[16,16,512]{2,1,0:T(8,128)(2,1)}), bf16[16,16,512]{2,1,0:T(8,128)(2,1)S(1)}, u32[]{:S(2)}, u32[]{:S(2)}) async-start(bf16[16,16,512]{2,1,0:T(8,128)(2,1)} %broadcast_in_dim.27), calls=%async_computation.1 | async-start | bytes 524288 | tf_op jit(solution)/shard_map/all_to_all | solution.py:23
  70.2 0.1 pad_add_fusion.picks
  70.3 0.0 copy-start.6
  70.3 1.4 %copy-done.6 = bf16[1,1,1536,512]{3,2,1,0:T(8,128)(2,1)S(1)} copy-done((bf16[1,1,1536,512]{3,2,1,0:T(8,128)(2,1)S(1)}, bf16[1,1,1536,512]{3,2,1,0:T(8,128)(2,1)}, u32[]{:S(2)}) %copy-start.6) | copy-done | bytes 1572888
  71.7 1.1 %copy-done.7 = bf16[1,1,1536,256]{3,2,1,0:T(8,128)(2,1)S(1)} copy-done((bf16[1,1,1536,256]{3,2,1,0:T(8,128)(2,1)S(1)}, bf16[1,1,1536,256]{3,2,1,0:T(8,128)(2,1)}, u32[]{:S(2)}) %copy-start.7) | copy-done | bytes 786456
  72.8 4.0 %shard_map.141 = (bf16[1536,512]{1,0:T(8,128)(2,1)S(1)}, f32[1536,128]{1,0:T(8,128)S(1)}) custom-call(s32[6]{0:T(128)S(1)} %pad_add_fusion.picks, bf16[128,640]{1,0:T(8,128)(2,1)S(1)} %copy-done.5, bf16[128,640]{1,0:T(8,128)(2,1)S(1)} %copy-done.3, bf16[2,128,640]{2,1,0:T(8,128)(2,1)} %collective-permute-done.13.before, ...), custom_call_target="tpu_custom_call" | custom-call | flops 1200000000 | bytes 7000000 | tf_op jit(solution)/shard_map/pallas_call | solution.py:167
  76.8 1.4 %shard_map.142 = (f32[512,128]{1,0:T(8,128)}, bf16[128,128]{1,0:T(8,128)(2,1)}, bf16[1536,128]{1,0:T(8,128)(2,1)}) custom-call(bf16[8,2,16,512]{3,2,1,0:T(8,128)(2,1)S(1)} %bitcast.39, bf16[128,512]{1,0:T(8,128)(2,1)S(1)} %convert_bitcast_fusion.coupling, f32[128,128]{1,0:T(8,128)S(1)} %get-tuple-element.22.own, ...), custom_call_target="tpu_custom_call" | custom-call | flops 230000000 | bytes 4000000 | tf_op jit(solution)/shard_map/pallas_call | solution.py:202
  (44 shorter events, 0.3 us)
Async XLA Ops:
  0.6 22.1 %copy-start = (bf16[1,256,128]{2,1,0:T(8,128)(2,1)S(1)}, bf16[1,256,128]{2,1,0:T(8,128)(2,1)}, u32[]{:S(2)}) copy-start(bf16[1,256,128]{2,1,0:T(8,128)(2,1)} %param.12) | copy-start | bytes 196612
  0.6 4.2 %copy-start.10 = (f32[1,1,128,512]{3,2,1,0:T(8,128)S(1)}, f32[1,1,128,512]{3,2,1,0:T(8,128)}, u32[]{:S(2)}) copy-start(f32[1,1,128,512]{3,2,1,0:T(8,128)} %param.14) | copy-start | bytes 786436
  0.7 4.2 %copy-start.11 = (bf16[1,1,128,128]{3,2,1,0:T(8,128)(2,1)S(1)}, bf16[1,1,128,128]{3,2,1,0:T(8,128)(2,1)}, u32[]{:S(2)}) copy-start(bf16[1,1,128,128]{3,2,1,0:T(8,128)(2,1)} %param.16) | copy-start | bytes 98308
  0.7 4.2 %copy-start.12 = (bf16[1,1,128,128]{3,2,1,0:T(8,128)(2,1)S(1)}, bf16[1,1,128,128]{3,2,1,0:T(8,128)(2,1)}, u32[]{:S(2)}) copy-start(bf16[1,1,128,128]{3,2,1,0:T(8,128)(2,1)} %param.15) | copy-start | bytes 98308
  0.7 6.3 %copy-start.13 = (bf16[1,16,256]{2,1,0:T(8,128)(2,1)S(1)}, bf16[1,16,256]{2,1,0:T(8,128)(2,1)}, u32[]{:S(2)}) copy-start(bf16[1,16,256]{2,1,0:T(8,128)(2,1)} %param.11) | copy-start | bytes 24580
  2.0 17.1 %copy-start.1 = (f32[1,512,512]{2,1,0:T(8,128)S(1)}, f32[1,512,512]{2,1,0:T(8,128)}, u32[]{:S(2)}) copy-start(f32[1,512,512]{2,1,0:T(8,128)} %param.13) | copy-start | bytes 3145732
  2.0 17.0 %collective-permute-start.2 = (bf16[512,512]{1,0:T(8,128)(2,1)S(1)}, bf16[512,512]{1,0:T(8,128)(2,1)S(1)}, u32[]{:S(2)}, u32[]{:S(2)}) collective-permute-start(bf16[512,512]{1,0:T(8,128)(2,1)S(1)} %bitcast_convert_fusion), channel_id=1, source_target_pairs={{33,65},{35,67},{37,69},{39,71},{41,73},{43,75},{45,77},{47,79},{4... | collective-permute-start | bytes 1572872 | tf_op jit(solution)/shard_map/ppermute | solution.py:29
  5.1 14.0 %copy-start.4 = (bf16[128,640]{1,0:T(8,128)(2,1)}, bf16[128,640]{1,0:T(8,128)(2,1)S(1)}, u32[]{:S(2)}) copy-start(bf16[128,640]{1,0:T(8,128)(2,1)S(1)} %get-tuple-element.20.mine) | copy-start | bytes 491524
  5.1 10.4 %collective-permute-start.12 = (bf16[128,640]{1,0:T(8,128)(2,1)S(1)}, bf16[128,640]{1,0:T(8,128)(2,1)S(1)}, u32[]{:S(2)}, u32[]{:S(2)}) collective-permute-start(bf16[128,640]{1,0:T(8,128)(2,1)S(1)} %get-tuple-element.20.mine), channel_id=1, source_target_pairs={{0,1},{1,0},{2,3},{3,2},{4,5},{5,4},{6,7},{7,6},{8,9},{9,8},{10,11... | collective-permute-start | bytes 491528 | tf_op jit(solution)/shard_map/ppermute | solution.py:34
  7.7 15.0 %all-to-all-start = ((bf16[32,16,256]{2,1,0:T(8,128)(2,1)}), bf16[32,16,256]{2,1,0:T(8,128)(2,1)}, u32[]{:S(2)}, u32[]{:S(2)}) async-start(bf16[32,16,256]{2,1,0:T(8,128)(2,1)} %broadcast_in_dim.26), calls=%async_computation | async-start | bytes 524288 | tf_op jit(solution)/shard_map/all_to_all | solution.py:23
  15.5 3.6 %copy-start.2 = (bf16[128,640]{1,0:T(8,128)(2,1)}, bf16[128,640]{1,0:T(8,128)(2,1)S(1)}, u32[]{:S(2)}) copy-start(bf16[128,640]{1,0:T(8,128)(2,1)S(1)} %collective-permute-done.12.partner) | copy-start | bytes 491524
  16.3 10.8 %collective-permute-start.13 = (bf16[2,128,640]{2,1,0:T(8,128)(2,1)}, bf16[2,128,640]{2,1,0:T(8,128)(2,1)}, u32[]{:S(2)}, u32[]{:S(2)}) collective-permute-start(bf16[2,128,640]{2,1,0:T(8,128)(2,1)} %pad_maximum_fusion.1), channel_id=1, source_target_pairs={{0,2},{2,4},{4,6},{6,8},{8,10},{10,12},{12,14},{14,16},{16,18},{18... | collective-permute-start | bytes 983048 | tf_op jit(solution)/shard_map/ppermute | solution.py:39
  17.7 9.4 %collective-permute-start.14 = (bf16[2,128,640]{2,1,0:T(8,128)(2,1)}, bf16[2,128,640]{2,1,0:T(8,128)(2,1)}, u32[]{:S(2)}, u32[]{:S(2)}) collective-permute-start(bf16[2,128,640]{2,1,0:T(8,128)(2,1)} %pad_maximum_fusion.1), channel_id=1, source_target_pairs={{0,30},{2,0},{4,2},{6,4},{8,6},{10,8},{12,10},{14,12},{16,14},{18,... | collective-permute-start | bytes 983048 | tf_op jit(solution)/shard_map/ppermute | solution.py:39
  20.8 0.8 %copy-start.8 = (bf16[512,512]{1,0:T(8,128)(2,1)}, bf16[512,512]{1,0:T(8,128)(2,1)S(1)}, u32[]{:S(2)}) copy-start(bf16[512,512]{1,0:T(8,128)(2,1)S(1)} %get-tuple-element.13) | copy-start | bytes 1572868
  21.6 14.9 %collective-permute-start.8 = (bf16[512,512]{1,0:T(8,128)(2,1)}, bf16[512,512]{1,0:T(8,128)(2,1)S(1)}, u32[]{:S(2)}, u32[]{:S(2)}) collective-permute-start(bf16[512,512]{1,0:T(8,128)(2,1)} %get-tuple-element.12), channel_id=1, source_target_pairs={{257,321},{259,323},{261,325},{263,327},{265,329},{267,331},{269,3... | collective-permute-start | bytes 1572872 | tf_op jit(solution)/shard_map/ppermute | solution.py:29
  23.9 6.6 %collective-permute-start = (f32[16,512]{1,0:T(8,128)S(1)}, f32[16,512]{1,0:T(8,128)S(1)}, u32[]{:S(2)}, u32[]{:S(2)}) collective-permute-start(f32[16,512]{1,0:T(8,128)S(1)} %fusion), channel_id=1, source_target_pairs={{1,33},{3,35},{5,37},{7,39},{9,41},{11,43},{13,45},{15,47},{17,49}... | collective-permute-start | bytes 98312 | tf_op jit(solution)/shard_map/ppermute | solution.py:29
  25.8 17.5 %collective-permute-start.11 = (bf16[512,512]{1,0:T(8,128)(2,1)}, bf16[512,512]{1,0:T(8,128)(2,1)S(1)}, u32[]{:S(2)}, u32[]{:S(2)}) collective-permute-start(bf16[512,512]{1,0:T(8,128)(2,1)} %copy-done.8), channel_id=1, source_target_pairs={{321,385},{323,387},{325,389},{327,391},{329,393},{331,395},{333,3... | collective-permute-start | bytes 1572872 | tf_op jit(solution)/shard_map/ppermute | solution.py:29
  29.1 41.1 %collective-permute-start.15 = (bf16[4,128,640]{2,1,0:T(8,128)(2,1)}, bf16[4,128,640]{2,1,0:T(8,128)(2,1)}, u32[]{:S(2)}, u32[]{:S(2)}) collective-permute-start(bf16[4,128,640]{2,1,0:T(8,128)(2,1)} %pad_maximum_fusion), channel_id=1, source_target_pairs={{0,1},{2,3},{4,5},{6,7},{8,9},{10,11},{12,13},{14,15},{16,17},{18,... | collective-permute-start | bytes 1966088 | tf_op jit(solution)/shard_map/ppermute | solution.py:44
  31.0 0.7 collective-permute-start.1
  31.7 0.7 collective-permute-start.3
  32.4 1.3 %collective-permute-start.4 = (f32[16,512]{1,0:T(8,128)S(1)}, f32[16,512]{1,0:T(8,128)S(1)}, u32[]{:S(2)}, u32[]{:S(2)}) collective-permute-start(f32[16,512]{1,0:T(8,128)S(1)} %shard_map.132.base), channel_id=1, source_target_pairs={{129,193},{131,195},{133,197},{135,199},{137,201},{139,203},{141,2... | collective-permute-start | bytes 98312 | tf_op jit(solution)/shard_map/ppermute | solution.py:29
  33.1 1.4 %collective-permute-start.5 = (f32[16,512]{1,0:T(8,128)S(1)}, f32[16,512]{1,0:T(8,128)S(1)}, u32[]{:S(2)}, u32[]{:S(2)}) collective-permute-start(f32[16,512]{1,0:T(8,128)S(1)} %convolution_add_fusion.base), channel_id=1, source_target_pairs={{257,321},{259,323},{261,325},{263,327},{265,329},{267,331},{269,3... | collective-permute-start | bytes 98312 | tf_op jit(solution)/shard_map/ppermute | solution.py:29
  33.8 2.0 %collective-permute-start.6 = (f32[16,512]{1,0:T(8,128)S(1)}, f32[16,512]{1,0:T(8,128)S(1)}, u32[]{:S(2)}, u32[]{:S(2)}) collective-permute-start(f32[16,512]{1,0:T(8,128)S(1)} %shard_map.133.base), channel_id=1, source_target_pairs={{193,257},{195,259},{197,261},{199,263},{201,265},{203,267},{205,2... | collective-permute-start | bytes 98312 | tf_op jit(solution)/shard_map/ppermute | solution.py:29
  34.5 8.4 %collective-permute-start.9 = (f32[16,512]{1,0:T(8,128)S(1)}, f32[16,512]{1,0:T(8,128)S(1)}, u32[]{:S(2)}, u32[]{:S(2)}) collective-permute-start(f32[16,512]{1,0:T(8,128)S(1)} %convolution_add_fusion.base), channel_id=1, source_target_pairs={{321,385},{323,387},{325,389},{327,391},{329,393},{331,395},{333,3... | collective-permute-start | bytes 98312 | tf_op jit(solution)/shard_map/ppermute | solution.py:29
  35.8 0.8 %collective-permute-start.7 = (f32[16,512]{1,0:T(8,128)S(1)}, f32[16,512]{1,0:T(8,128)S(1)}, u32[]{:S(2)}, u32[]{:S(2)}) collective-permute-start(f32[16,512]{1,0:T(8,128)S(1)} %shard_map.133.base), channel_id=1, source_target_pairs={{193,321},{195,323},{197,325},{199,327},{201,329},{203,331},{205,3... | collective-permute-start | bytes 98312 | tf_op jit(solution)/shard_map/ppermute | solution.py:29
  36.6 26.2 %collective-permute-start.10 = (f32[16,512]{1,0:T(8,128)S(1)}, f32[16,512]{1,0:T(8,128)S(1)}, u32[]{:S(2)}, u32[]{:S(2)}) collective-permute-start(f32[16,512]{1,0:T(8,128)S(1)} %shard_map.137.base), channel_id=1, source_target_pairs={{257,385},{259,387},{261,389},{263,391},{265,393},{267,395},{269,3... | collective-permute-start | bytes 98312 | tf_op jit(solution)/shard_map/ppermute | solution.py:29
  44.2 25.3 %copy-start.14 = (s32[1,1,4]{2,1,0:T(1,128)S(1)}, s32[1,1,4]{2,1,0:T(1,128)}, u32[]{:S(2)}) copy-start(s32[1,1,4]{2,1,0:T(1,128)} %param.21) | copy-start | bytes 52
  44.2 26.0 %copy-start.3 = (bf16[128,640]{1,0:T(8,128)(2,1)S(1)}, bf16[128,640]{1,0:T(8,128)(2,1)}, u32[]{:S(2)}) copy-start(bf16[128,640]{1,0:T(8,128)(2,1)} %copy-done.2) | copy-start | bytes 491524
  44.2 26.0 %copy-start.5 = (bf16[128,640]{1,0:T(8,128)(2,1)S(1)}, bf16[128,640]{1,0:T(8,128)(2,1)}, u32[]{:S(2)}) copy-start(bf16[128,640]{1,0:T(8,128)(2,1)} %copy-done.4) | copy-start | bytes 491524
  44.2 26.0 %copy-start.9 = (bf16[1,1,256,128]{3,2,1,0:T(8,128)(2,1)S(1)}, bf16[1,1,256,128]{3,2,1,0:T(8,128)(2,1)}, u32[]{:S(2)}) copy-start(bf16[1,1,256,128]{3,2,1,0:T(8,128)(2,1)} %param.18) | copy-start | bytes 196612
  64.0 12.8 %all-to-all-start.1 = ((bf16[16,16,512]{2,1,0:T(8,128)(2,1)}), bf16[16,16,512]{2,1,0:T(8,128)(2,1)S(1)}, u32[]{:S(2)}, u32[]{:S(2)}) async-start(bf16[16,16,512]{2,1,0:T(8,128)(2,1)} %broadcast_in_dim.27), calls=%async_computation.1 | async-start | bytes 524288 | tf_op jit(solution)/shard_map/all_to_all | solution.py:23
  70.3 1.4 %copy-start.6 = (bf16[1,1,1536,512]{3,2,1,0:T(8,128)(2,1)S(1)}, bf16[1,1,1536,512]{3,2,1,0:T(8,128)(2,1)}, u32[]{:S(2)}) copy-start(bf16[1,1,1536,512]{3,2,1,0:T(8,128)(2,1)} %param.20) | copy-start | bytes 4718596
  71.7 1.1 %copy-start.7 = (bf16[1,1,1536,256]{3,2,1,0:T(8,128)(2,1)S(1)}, bf16[1,1,1536,256]{3,2,1,0:T(8,128)(2,1)}, u32[]{:S(2)}) copy-start(bf16[1,1,1536,256]{3,2,1,0:T(8,128)(2,1)} %param.17) | copy-start | bytes 2359300

commit v5 on v4

--- a/solution.py
+++ b/solution.py
@@ -258,10 +258,10 @@
         field = add_step(field, earlier, two, first, first + 2)
     earlier_4 = along_chain(field, 4, range(LATE, LAST))
     earlier = along_chain(field, 2, range(LATE - 2, LATE))
-    field = add_step(field, late_2a, two, LATE, LAST)
+    field = field + rows_times(late_2a, two)
     (four_a,) = advance(two, back_2a, 0, LATE, LAST)
-    field = add_step(field, earlier, two, LATE - 2, LATE)
-    field = add_step(field, earlier_4, four_a, LATE, LAST)
+    field = field + rows_times(earlier, two)
+    field = field + rows_times(earlier_4, four_a)
     earlier = along_chain(field, 4, range(LAST, chain))
     field = add_step(field, late_2b, two, LAST, chain)
     (four_b,) = advance(two, back_2b, 0, LAST, chain)

time: 78.9 us -> 76.4 us (0.968)
  the two profiles are of different devices: /device:TPU:455 before, /device:TPU:481 now
where the time goes in v5:
time: 76.4 us; the launch traced here: 75.7 us
  starting transfers between devices  27.6 us (36%)
  waiting for transfers between devices  25.8 us (34%)
  Pallas kernels  8.82 us (12%)
  local copies, waits for them, and re-layouts  5.05 us (7%)
  other arithmetic  4.17 us (5%)
  matrix products  2.48 us (3%)
  between operations  1.82 us (2%)
    ppermute x12, waiting for transfers between devices, along_chain(): return lax.ppermute(value, ('grp', 'sub'), pairs)  19.7 us
    ppermute x12, starting transfers between devices, along_chain(): return lax.ppermute(value, ('grp', 'sub'), pairs)  11.3 us
    all_to_all x2, starting transfers between devices, spread(): lax.all_to_all(copies, 'sub', 0, 0, axis_index_groups=groups if parts > 1...  10.9 us
    all_to_all x2, waiting for transfers between devices, spread(): lax.all_to_all(copies, 'sub', 0, 0, axis_index_groups=groups if parts > 1...  6.16 us
    pallas_call x1, Pallas kernels, prepare(): pl.pallas_call(prepare_kernel, out_shape=(jax.ShapeDtypeStruct((points, l...  3.89 us
    unnamed x30, local copies, waits for them, and re-layouts  3.6 us
    pallas_call x3, Pallas kernels, advance(): pl.pallas_call(functools.partial(advance_kernel, first, last), out_shape=...  2.7 us
    dot_general x4, matrix products, rows_times(): lax.dot_general(value, left, dims, precision=lax.Precision.HIGH, preferre...  2.1 us
  transfers between devices with their start and end apart: 18, of which 4 were waited for; matrix products, arithmetic and copies ran while one was open for 9% of the time, Pallas kernels for 10%

profile of v5, /device:TPU:481, one launch (start us, length us, event | category | flops | bytes accessed | tf_op | source)
XLA Modules:
  0.0 75.7 jit_solution(8965350047946673759)
XLA Ops:
  0.6 0.0 copy-start
  0.7 1.3 %bitcast_convert_fusion = bf16[512,512]{1,0:T(8,128)(2,1)S(1)} fusion(f32[1,512,512]{2,1,0:T(8,128)} %param.13), kind=kLoop, calls=%fused_computation.17 | loop fusion | flops 262144 | bytes 1572864 | tf_op jit(solution)/shard_map/convert_element_type | solution.py:238
  2.0 1.4 %collective-permute-start.2 = (bf16[512,512]{1,0:T(8,128)(2,1)S(1)}, bf16[512,512]{1,0:T(8,128)(2,1)S(1)}, u32[]{:S(2)}, u32[]{:S(2)}) collective-permute-start(bf16[512,512]{1,0:T(8,128)(2,1)S(1)} %bitcast_convert_fusion), channel_id=1, source_target_pairs={{33,65},{35,67},{37,69},{39,71},{41,73},{43,75},{45,77},{47,79},{4... | collective-permute-start | bytes 1572872 | tf_op jit(solution)/shard_map/ppermute | solution.py:29
  3.5 0.1 fusion.11
  3.7 2.0 %collective-permute-start.12 = (bf16[128,640]{1,0:T(8,128)(2,1)S(1)}, bf16[128,640]{1,0:T(8,128)(2,1)S(1)}, u32[]{:S(2)}, u32[]{:S(2)}) collective-permute-start(bf16[128,640]{1,0:T(8,128)(2,1)S(1)} %get-tuple-element.20.mine), channel_id=1, source_target_pairs={{0,1},{1,0},{2,3},{3,2},{4,5},{5,4},{6,7},{7,6},{8,9},{9,8},{10,11... | collective-permute-start | bytes 491528 | tf_op jit(solution)/shard_map/ppermute | solution.py:34
  5.7 0.7 broadcast_in_dim.26
  6.4 7.5 %all-to-all-start = ((bf16[32,16,256]{2,1,0:T(8,128)(2,1)}), bf16[32,16,256]{2,1,0:T(8,128)(2,1)S(1)}, u32[]{:S(2)}, u32[]{:S(2)}) async-start(bf16[32,16,256]{2,1,0:T(8,128)(2,1)} %broadcast_in_dim.26), calls=%async_computation | async-start | bytes 524288 | tf_op jit(solution)/shard_map/all_to_all | solution.py:23
  14.0 0.8 %pad_maximum_fusion.1 = bf16[2,128,640]{2,1,0:T(8,128)(2,1)} fusion(bf16[1,128,640]{2,1,0:T(8,128)(2,1)S(1)} %bitcast.46, bf16[1,128,640]{2,1,0:T(8,128)(2,1)S(1)} %get-tuple-element.19), kind=kLoop, calls=%fused_computation.5 | loop fusion | flops 163840 | bytes 655360 | tf_op jit(solution)/shard_map/stack | solution.py:276
  14.8 0.7 collective-permute-start.13
  15.5 1.4 %collective-permute-start.14 = (bf16[2,128,640]{2,1,0:T(8,128)(2,1)}, bf16[2,128,640]{2,1,0:T(8,128)(2,1)}, u32[]{:S(2)}, u32[]{:S(2)}) collective-permute-start(bf16[2,128,640]{2,1,0:T(8,128)(2,1)} %pad_maximum_fusion.1), channel_id=1, source_target_pairs={{0,30},{2,0},{4,2},{6,4},{8,6},{10,8},{12,10},{14,12},{16,14},{18,... | collective-permute-start | bytes 983048 | tf_op jit(solution)/shard_map/ppermute | solution.py:39
  16.9 6.2 %all-to-all-done = bf16[32,16,256]{2,1,0:T(8,128)(2,1)S(1)} async-done(((bf16[32,16,256]{2,1,0:T(8,128)(2,1)}), bf16[32,16,256]{2,1,0:T(8,128)(2,1)S(1)}, u32[]{:S(2)}, u32[]{:S(2)}) %all-to-all-start) | async-done | bytes 262176 | tf_op jit(solution)/shard_map/all_to_all | solution.py:23
  23.0 0.2 fusion.2
  23.3 1.3 %collective-permute-start = (f32[16,512]{1,0:T(8,128)S(1)}, f32[16,512]{1,0:T(8,128)S(1)}, u32[]{:S(2)}, u32[]{:S(2)}) collective-permute-start(f32[16,512]{1,0:T(8,128)S(1)} %fusion.2), channel_id=1, source_target_pairs={{1,33},{3,35},{5,37},{7,39},{9,41},{11,43},{13,45},{15,47},{17,49}... | collective-permute-start | bytes 98312 | tf_op jit(solution)/shard_map/ppermute | solution.py:29
  24.6 1.7 %shard_map.130 = (f32[512,512]{1,0:T(8,128)S(1)}, bf16[512,512]{1,0:T(8,128)(2,1)}, bf16[512,512]{1,0:T(8,128)(2,1)S(1)}) custom-call(f32[512,512]{1,0:T(8,128)S(1)} %bitcast.44, bf16[512,512]{1,0:T(8,128)(2,1)S(1)} %collective-permute-done.2.right), custom_call_target="tpu_custom_call" | custom-call | flops 540000000 | bytes 3000000 | tf_op jit(solution)/shard_map/pallas_call | solution.py:112
  26.3 0.7 collective-permute-start.8
  27.0 0.1 copy-done.8
  27.1 1.4 %collective-permute-done = f32[16,512]{1,0:T(8,128)S(1)} collective-permute-done((f32[16,512]{1,0:T(8,128)S(1)}, f32[16,512]{1,0:T(8,128)S(1)}, u32[]{:S(2)}, u32[]{:S(2)}) %collective-permute-start) | collective-permute-done | bytes 32800 | tf_op jit(solution)/shard_map/ppermute | solution.py:29
  28.6 0.5 convolution_add_fusion.1.base
  29.1 0.7 collective-permute-start.1
  29.8 0.7 collective-permute-start.3
  30.5 0.7 collective-permute-start.4
  31.2 0.7 collective-permute-start.5
  31.9 1.3 %collective-permute-start.9 = (f32[16,512]{1,0:T(8,128)S(1)}, f32[16,512]{1,0:T(8,128)S(1)}, u32[]{:S(2)}, u32[]{:S(2)}) collective-permute-start(f32[16,512]{1,0:T(8,128)S(1)} %convolution_add_fusion.1.base), channel_id=1, source_target_pairs={{321,385},{323,387},{325,389},{327,391},{329,393},{331,395},{333,3... | collective-permute-start | bytes 98312 | tf_op jit(solution)/shard_map/ppermute | solution.py:29
  33.2 0.7 collective-permute-start.6
  33.9 1.9 %pad_maximum_fusion = bf16[4,128,640]{2,1,0:T(8,128)(2,1)} fusion(bf16[2,128,640]{2,1,0:T(8,128)(2,1)} %collective-permute-done.14.after, bf16[2,128,640]{2,1,0:T(8,128)(2,1)S(1)} %collective-permute-done.13.before), kind=kLoop, calls=%fused_computation.4 | loop fusion | flops 327680 | bytes 1310720 | tf_op jit(solution)/shard_map/concatenate | solution.py:279
  35.8 1.3 %collective-permute-start.15 = (bf16[4,128,640]{2,1,0:T(8,128)(2,1)}, bf16[4,128,640]{2,1,0:T(8,128)(2,1)}, u32[]{:S(2)}, u32[]{:S(2)}) collective-permute-start(bf16[4,128,640]{2,1,0:T(8,128)(2,1)} %pad_maximum_fusion), channel_id=1, source_target_pairs={{0,1},{2,3},{4,5},{6,7},{8,9},{10,11},{12,13},{14,15},{16,17},{18,... | collective-permute-start | bytes 1966088 | tf_op jit(solution)/shard_map/ppermute | solution.py:44
  37.1 1.3 %collective-permute-start.11 = (bf16[512,512]{1,0:T(8,128)(2,1)}, bf16[512,512]{1,0:T(8,128)(2,1)S(1)}, u32[]{:S(2)}, u32[]{:S(2)}) collective-permute-start(bf16[512,512]{1,0:T(8,128)(2,1)} %copy-done.8), channel_id=1, source_target_pairs={{321,385},{323,387},{325,389},{327,391},{329,393},{331,395},{333,3... | collective-permute-start | bytes 1572872 | tf_op jit(solution)/shard_map/ppermute | solution.py:29
  38.4 0.5 fusion.12
  38.9 0.0 collective-permute-done.8.right
  38.9 0.7 collective-permute-start.7
  39.6 0.1 shard_map.134
  39.7 0.5 fusion.13
  40.2 0.0 collective-permute-done.5
  40.3 0.5 fusion.1.base
  40.8 1.3 %collective-permute-start.10 = (f32[16,512]{1,0:T(8,128)S(1)}, f32[16,512]{1,0:T(8,128)S(1)}, u32[]{:S(2)}, u32[]{:S(2)}) collective-permute-start(f32[16,512]{1,0:T(8,128)S(1)} %fusion.1.base), channel_id=1, source_target_pairs={{257,385},{259,387},{261,389},{263,391},{265,393},{267,395},{269,3... | collective-permute-start | bytes 98312 | tf_op jit(solution)/shard_map/ppermute | solution.py:29
  42.1 0.4 shard_map.135.base
  42.5 11.9 %collective-permute-done.11.right = bf16[512,512]{1,0:T(8,128)(2,1)S(1)} collective-permute-done((bf16[512,512]{1,0:T(8,128)(2,1)}, bf16[512,512]{1,0:T(8,128)(2,1)S(1)}, u32[]{:S(2)}, u32[]{:S(2)}) %collective-permute-start.11) | collective-permute-done | bytes 524320 | tf_op jit(solution)/shard_map/ppermute | solution.py:29
  54.5 0.9 %shard_map.136.left = f32[512,512]{1,0:T(8,128)S(1)} custom-call(f32[512,512]{1,0:T(8,128)S(1)} %get-tuple-element.11.left, bf16[512,512]{1,0:T(8,128)(2,1)S(1)} %collective-permute-done.11.right), custom_call_target="tpu_custom_call" | custom-call | flops 540000000 | bytes 3000000 | tf_op jit(solution)/shard_map/pallas_call | solution.py:112
  55.4 6.2 %collective-permute-done.10.value = f32[16,512]{1,0:T(8,128)S(1)} collective-permute-done((f32[16,512]{1,0:T(8,128)S(1)}, f32[16,512]{1,0:T(8,128)S(1)}, u32[]{:S(2)}, u32[]{:S(2)}) %collective-permute-start.10) | collective-permute-done | bytes 32800 | tf_op jit(solution)/shard_map/ppermute | solution.py:29
  61.6 0.4 shard_map.137
  62.1 0.7 broadcast_in_dim.27
  62.8 3.4 %all-to-all-start.1 = ((bf16[16,16,512]{2,1,0:T(8,128)(2,1)}), bf16[16,16,512]{2,1,0:T(8,128)(2,1)S(1)}, u32[]{:S(2)}, u32[]{:S(2)}) async-start(bf16[16,16,512]{2,1,0:T(8,128)(2,1)} %broadcast_in_dim.27), calls=%async_computation.1 | async-start | bytes 524288 | tf_op jit(solution)/shard_map/all_to_all | solution.py:23
  66.9 0.1 pad_add_fusion.picks
  67.0 0.9 %copy-done.5 = bf16[128,640]{1,0:T(8,128)(2,1)S(1)} copy-done((bf16[128,640]{1,0:T(8,128)(2,1)S(1)}, bf16[128,640]{1,0:T(8,128)(2,1)}, u32[]{:S(2)}) %copy-start.5) | copy-done | bytes 163864
  67.9 1.4 %copy-done.6 = bf16[1,1,1536,512]{3,2,1,0:T(8,128)(2,1)S(1)} copy-done((bf16[1,1,1536,512]{3,2,1,0:T(8,128)(2,1)S(1)}, bf16[1,1,1536,512]{3,2,1,0:T(8,128)(2,1)}, u32[]{:S(2)}) %copy-start.6) | copy-done | bytes 1572888
  69.3 1.1 %copy-done.7 = bf16[1,1,1536,256]{3,2,1,0:T(8,128)(2,1)S(1)} copy-done((bf16[1,1,1536,256]{3,2,1,0:T(8,128)(2,1)S(1)}, bf16[1,1,1536,256]{3,2,1,0:T(8,128)(2,1)}, u32[]{:S(2)}) %copy-start.7) | copy-done | bytes 786456
  70.4 3.9 %shard_map.138 = (bf16[1536,512]{1,0:T(8,128)(2,1)S(1)}, f32[1536,128]{1,0:T(8,128)S(1)}) custom-call(s32[6]{0:T(128)S(1)} %pad_add_fusion.picks, bf16[128,640]{1,0:T(8,128)(2,1)S(1)} %copy-done.5, bf16[128,640]{1,0:T(8,128)(2,1)S(1)} %copy-done.3, bf16[2,128,640]{2,1,0:T(8,128)(2,1)S(1)} %collective-permute-done.13.before, ...), custom_call_target="tpu_custom_call" | custom-call | flops 1200000000 | bytes 7000000 | tf_op jit(solution)/shard_map/pallas_call | solution.py:167
  74.4 1.4 %shard_map.139 = (f32[512,128]{1,0:T(8,128)}, bf16[128,128]{1,0:T(8,128)(2,1)}, bf16[1536,128]{1,0:T(8,128)(2,1)}) custom-call(bf16[8,2,16,512]{3,2,1,0:T(8,128)(2,1)S(1)} %bitcast.45, bf16[128,512]{1,0:T(8,128)(2,1)S(1)} %convert_bitcast_fusion.coupling, f32[128,128]{1,0:T(8,128)S(1)} %get-tuple-element.22.own, ...), custom_call_target="tpu_custom_call" | custom-call | flops 230000000 | bytes 4000000 | tf_op jit(solution)/shard_map/pallas_call | solution.py:202
  (44 shorter events, 0.2 us)
Async XLA Ops:
  0.6 22.4 %copy-start = (bf16[1,256,128]{2,1,0:T(8,128)(2,1)S(1)}, bf16[1,256,128]{2,1,0:T(8,128)(2,1)}, u32[]{:S(2)}) copy-start(bf16[1,256,128]{2,1,0:T(8,128)(2,1)} %param.12) | copy-start | bytes 196612
  0.6 2.8 %copy-start.10 = (f32[1,1,128,512]{3,2,1,0:T(8,128)S(1)}, f32[1,1,128,512]{3,2,1,0:T(8,128)}, u32[]{:S(2)}) copy-start(f32[1,1,128,512]{3,2,1,0:T(8,128)} %param.14) | copy-start | bytes 786436
  0.7 2.9 %copy-start.11 = (bf16[1,1,128,128]{3,2,1,0:T(8,128)(2,1)S(1)}, bf16[1,1,128,128]{3,2,1,0:T(8,128)(2,1)}, u32[]{:S(2)}) copy-start(bf16[1,1,128,128]{3,2,1,0:T(8,128)(2,1)} %param.16) | copy-start | bytes 98308
  0.7 2.9 %copy-start.12 = (bf16[1,1,128,128]{3,2,1,0:T(8,128)(2,1)S(1)}, bf16[1,1,128,128]{3,2,1,0:T(8,128)(2,1)}, u32[]{:S(2)}) copy-start(bf16[1,1,128,128]{3,2,1,0:T(8,128)(2,1)} %param.15) | copy-start | bytes 98308
  0.7 5.0 %copy-start.13 = (bf16[1,16,256]{2,1,0:T(8,128)(2,1)S(1)}, bf16[1,16,256]{2,1,0:T(8,128)(2,1)}, u32[]{:S(2)}) copy-start(bf16[1,16,256]{2,1,0:T(8,128)(2,1)} %param.11) | copy-start | bytes 24580
  2.0 22.6 %copy-start.1 = (f32[1,512,512]{2,1,0:T(8,128)S(1)}, f32[1,512,512]{2,1,0:T(8,128)}, u32[]{:S(2)}) copy-start(f32[1,512,512]{2,1,0:T(8,128)} %param.13) | copy-start | bytes 3145732
  2.0 22.5 %collective-permute-start.2 = (bf16[512,512]{1,0:T(8,128)(2,1)S(1)}, bf16[512,512]{1,0:T(8,128)(2,1)S(1)}, u32[]{:S(2)}, u32[]{:S(2)}) collective-permute-start(bf16[512,512]{1,0:T(8,128)(2,1)S(1)} %bitcast_convert_fusion), channel_id=1, source_target_pairs={{33,65},{35,67},{37,69},{39,71},{41,73},{43,75},{45,77},{47,79},{4... | collective-permute-start | bytes 1572872 | tf_op jit(solution)/shard_map/ppermute | solution.py:29
  3.7 20.9 %copy-start.4 = (bf16[128,640]{1,0:T(8,128)(2,1)}, bf16[128,640]{1,0:T(8,128)(2,1)S(1)}, u32[]{:S(2)}) copy-start(bf16[128,640]{1,0:T(8,128)(2,1)S(1)} %get-tuple-element.20.mine) | copy-start | bytes 491524
  3.7 10.3 %collective-permute-start.12 = (bf16[128,640]{1,0:T(8,128)(2,1)S(1)}, bf16[128,640]{1,0:T(8,128)(2,1)S(1)}, u32[]{:S(2)}, u32[]{:S(2)}) collective-permute-start(bf16[128,640]{1,0:T(8,128)(2,1)S(1)} %get-tuple-element.20.mine), channel_id=1, source_target_pairs={{0,1},{1,0},{2,3},{3,2},{4,5},{5,4},{6,7},{7,6},{8,9},{9,8},{10,11... | collective-permute-start | bytes 491528 | tf_op jit(solution)/shard_map/ppermute | solution.py:34
  6.4 16.6 %all-to-all-start = ((bf16[32,16,256]{2,1,0:T(8,128)(2,1)}), bf16[32,16,256]{2,1,0:T(8,128)(2,1)S(1)}, u32[]{:S(2)}, u32[]{:S(2)}) async-start(bf16[32,16,256]{2,1,0:T(8,128)(2,1)} %broadcast_in_dim.26), calls=%async_computation | async-start | bytes 524288 | tf_op jit(solution)/shard_map/all_to_all | solution.py:23
  14.0 10.6 %copy-start.2 = (bf16[128,640]{1,0:T(8,128)(2,1)}, bf16[128,640]{1,0:T(8,128)(2,1)S(1)}, u32[]{:S(2)}) copy-start(bf16[128,640]{1,0:T(8,128)(2,1)S(1)} %collective-permute-done.12.partner) | copy-start | bytes 491524
  14.8 18.4 %collective-permute-start.13 = (bf16[2,128,640]{2,1,0:T(8,128)(2,1)}, bf16[2,128,640]{2,1,0:T(8,128)(2,1)S(1)}, u32[]{:S(2)}, u32[]{:S(2)}) collective-permute-start(bf16[2,128,640]{2,1,0:T(8,128)(2,1)} %pad_maximum_fusion.1), channel_id=1, source_target_pairs={{0,2},{2,4},{4,6},{6,8},{8,10},{10,12},{12,14},{14,16},{16,18},{18... | collective-permute-start | bytes 983048 | tf_op jit(solution)/shard_map/ppermute | solution.py:39
  15.5 18.4 %collective-permute-start.14 = (bf16[2,128,640]{2,1,0:T(8,128)(2,1)}, bf16[2,128,640]{2,1,0:T(8,128)(2,1)}, u32[]{:S(2)}, u32[]{:S(2)}) collective-permute-start(bf16[2,128,640]{2,1,0:T(8,128)(2,1)} %pad_maximum_fusion.1), channel_id=1, source_target_pairs={{0,30},{2,0},{4,2},{6,4},{8,6},{10,8},{12,10},{14,12},{16,14},{18,... | collective-permute-start | bytes 983048 | tf_op jit(solution)/shard_map/ppermute | solution.py:39
  23.3 5.3 %collective-permute-start = (f32[16,512]{1,0:T(8,128)S(1)}, f32[16,512]{1,0:T(8,128)S(1)}, u32[]{:S(2)}, u32[]{:S(2)}) collective-permute-start(f32[16,512]{1,0:T(8,128)S(1)} %fusion.2), channel_id=1, source_target_pairs={{1,33},{3,35},{5,37},{7,39},{9,41},{11,43},{13,45},{15,47},{17,49}... | collective-permute-start | bytes 98312 | tf_op jit(solution)/shard_map/ppermute | solution.py:29
  26.3 0.8 %copy-start.8 = (bf16[512,512]{1,0:T(8,128)(2,1)}, bf16[512,512]{1,0:T(8,128)(2,1)S(1)}, u32[]{:S(2)}) copy-start(bf16[512,512]{1,0:T(8,128)(2,1)S(1)} %get-tuple-element.13) | copy-start | bytes 1572868
  26.3 12.6 %collective-permute-start.8 = (bf16[512,512]{1,0:T(8,128)(2,1)}, bf16[512,512]{1,0:T(8,128)(2,1)S(1)}, u32[]{:S(2)}, u32[]{:S(2)}) collective-permute-start(bf16[512,512]{1,0:T(8,128)(2,1)} %get-tuple-element.12), channel_id=1, source_target_pairs={{257,321},{259,323},{261,325},{263,327},{265,329},{267,331},{269,3... | collective-permute-start | bytes 1572872 | tf_op jit(solution)/shard_map/ppermute | solution.py:29
  29.1 0.7 collective-permute-start.1
  29.8 0.7 collective-permute-start.3
  30.5 1.4 %collective-permute-start.4 = (f32[16,512]{1,0:T(8,128)S(1)}, f32[16,512]{1,0:T(8,128)S(1)}, u32[]{:S(2)}, u32[]{:S(2)}) collective-permute-start(f32[16,512]{1,0:T(8,128)S(1)} %shard_map.132.base), channel_id=1, source_target_pairs={{129,193},{131,195},{133,197},{135,199},{137,201},{139,203},{141,2... | collective-permute-start | bytes 98312 | tf_op jit(solution)/shard_map/ppermute | solution.py:29
  31.2 9.1 %collective-permute-start.5 = (f32[16,512]{1,0:T(8,128)S(1)}, f32[16,512]{1,0:T(8,128)S(1)}, u32[]{:S(2)}, u32[]{:S(2)}) collective-permute-start(f32[16,512]{1,0:T(8,128)S(1)} %convolution_add_fusion.1.base), channel_id=1, source_target_pairs={{257,321},{259,323},{261,325},{263,327},{265,329},{267,331},{269,3... | collective-permute-start | bytes 98312 | tf_op jit(solution)/shard_map/ppermute | solution.py:29
  31.9 10.2 %collective-permute-start.9 = (f32[16,512]{1,0:T(8,128)S(1)}, f32[16,512]{1,0:T(8,128)S(1)}, u32[]{:S(2)}, u32[]{:S(2)}) collective-permute-start(f32[16,512]{1,0:T(8,128)S(1)} %convolution_add_fusion.1.base), channel_id=1, source_target_pairs={{321,385},{323,387},{325,389},{327,391},{329,393},{331,395},{333,3... | collective-permute-start | bytes 98312 | tf_op jit(solution)/shard_map/ppermute | solution.py:29
  33.2 3.9 %collective-permute-start.6 = (f32[16,512]{1,0:T(8,128)S(1)}, f32[16,512]{1,0:T(8,128)S(1)}, u32[]{:S(2)}, u32[]{:S(2)}) collective-permute-start(f32[16,512]{1,0:T(8,128)S(1)} %shard_map.133), channel_id=1, source_target_pairs={{193,257},{195,259},{197,261},{199,263},{201,265},{203,267},{205,2... | collective-permute-start | bytes 98312 | tf_op jit(solution)/shard_map/ppermute | solution.py:29
  35.8 31.2 %collective-permute-start.15 = (bf16[4,128,640]{2,1,0:T(8,128)(2,1)}, bf16[4,128,640]{2,1,0:T(8,128)(2,1)}, u32[]{:S(2)}, u32[]{:S(2)}) collective-permute-start(bf16[4,128,640]{2,1,0:T(8,128)(2,1)} %pad_maximum_fusion), channel_id=1, source_target_pairs={{0,1},{2,3},{4,5},{6,7},{8,9},{10,11},{12,13},{14,15},{16,17},{18,... | collective-permute-start | bytes 1966088 | tf_op jit(solution)/shard_map/ppermute | solution.py:44
  37.1 17.4 %collective-permute-start.11 = (bf16[512,512]{1,0:T(8,128)(2,1)}, bf16[512,512]{1,0:T(8,128)(2,1)S(1)}, u32[]{:S(2)}, u32[]{:S(2)}) collective-permute-start(bf16[512,512]{1,0:T(8,128)(2,1)} %copy-done.8), channel_id=1, source_target_pairs={{321,385},{323,387},{325,389},{327,391},{329,393},{331,395},{333,3... | collective-permute-start | bytes 1572872 | tf_op jit(solution)/shard_map/ppermute | solution.py:29
  38.9 0.8 %collective-permute-start.7 = (f32[16,512]{1,0:T(8,128)S(1)}, f32[16,512]{1,0:T(8,128)S(1)}, u32[]{:S(2)}, u32[]{:S(2)}) collective-permute-start(f32[16,512]{1,0:T(8,128)S(1)} %shard_map.133), channel_id=1, source_target_pairs={{193,321},{195,323},{197,325},{199,327},{201,329},{203,331},{205,3... | collective-permute-start | bytes 98312 | tf_op jit(solution)/shard_map/ppermute | solution.py:29
  40.8 20.8 %collective-permute-start.10 = (f32[16,512]{1,0:T(8,128)S(1)}, f32[16,512]{1,0:T(8,128)S(1)}, u32[]{:S(2)}, u32[]{:S(2)}) collective-permute-start(f32[16,512]{1,0:T(8,128)S(1)} %fusion.1.base), channel_id=1, source_target_pairs={{257,385},{259,387},{261,389},{263,391},{265,393},{267,395},{269,3... | collective-permute-start | bytes 98312 | tf_op jit(solution)/shard_map/ppermute | solution.py:29
  55.4 10.9 %copy-start.14 = (s32[1,1,4]{2,1,0:T(1,128)S(1)}, s32[1,1,4]{2,1,0:T(1,128)}, u32[]{:S(2)}) copy-start(s32[1,1,4]{2,1,0:T(1,128)} %param.21) | copy-start | bytes 52
  55.4 11.6 %copy-start.3 = (bf16[128,640]{1,0:T(8,128)(2,1)S(1)}, bf16[128,640]{1,0:T(8,128)(2,1)}, u32[]{:S(2)}) copy-start(bf16[128,640]{1,0:T(8,128)(2,1)} %copy-done.2) | copy-start | bytes 491524
  55.4 11.6 %copy-start.9 = (bf16[1,1,256,128]{3,2,1,0:T(8,128)(2,1)S(1)}, bf16[1,1,256,128]{3,2,1,0:T(8,128)(2,1)}, u32[]{:S(2)}) copy-start(bf16[1,1,256,128]{3,2,1,0:T(8,128)(2,1)} %param.18) | copy-start | bytes 196612
  62.8 11.6 %all-to-all-start.1 = ((bf16[16,16,512]{2,1,0:T(8,128)(2,1)}), bf16[16,16,512]{2,1,0:T(8,128)(2,1)S(1)}, u32[]{:S(2)}, u32[]{:S(2)}) async-start(bf16[16,16,512]{2,1,0:T(8,128)(2,1)} %broadcast_in_dim.27), calls=%async_computation.1 | async-start | bytes 524288 | tf_op jit(solution)/shard_map/all_to_all | solution.py:23
  67.0 0.9 %copy-start.5 = (bf16[128,640]{1,0:T(8,128)(2,1)S(1)}, bf16[128,640]{1,0:T(8,128)(2,1)}, u32[]{:S(2)}) copy-start(bf16[128,640]{1,0:T(8,128)(2,1)} %copy-done.4) | copy-start | bytes 491524
  67.9 1.4 %copy-start.6 = (bf16[1,1,1536,512]{3,2,1,0:T(8,128)(2,1)S(1)}, bf16[1,1,1536,512]{3,2,1,0:T(8,128)(2,1)}, u32[]{:S(2)}) copy-start(bf16[1,1,1536,512]{3,2,1,0:T(8,128)(2,1)} %param.20) | copy-start | bytes 4718596
  69.3 1.1 %copy-start.7 = (bf16[1,1,1536,256]{3,2,1,0:T(8,128)(2,1)S(1)}, bf16[1,1,1536,256]{3,2,1,0:T(8,128)(2,1)}, u32[]{:S(2)}) copy-start(bf16[1,1,1536,256]{3,2,1,0:T(8,128)(2,1)} %param.17) | copy-start | bytes 2359300
